TPU v7x, 32 devices: a whole 2x2x4 slice. The times are simulated.
32 devices in a mesh: depth: 4 (over y, core), tile: 8 (over z, x).
Axes of the slice: x: 2, y: 2, z: 4, core: 2. Of those that a mesh axis runs over, the one named last changes fastest.
Arguments:
- density: int32 [128, 512, 1024], P('depth', 'tile'), may hold values from 0 to 255
- view_flip: int32 [8], P('tile'), may hold values from 0 to 1
- tf_coeff: float32 [4, 4], replicated, may hold values from -4 to 4
Outputs:
- shaded: float32 [3, 512, 1024], P(None, 'tile', 'depth')
All inputs are finite; a program needn't handle non-finite values.
Results may differ from a plain program's by a relative error of at most 0.0003.
Values may be sent and summed in bfloat16 or wider, within the bound.
No kernel may reach another device: no remote copies, remote signals or barrier semaphores. Data moves between devices by JAX's collectives and lax.ppermute only.
A program may use at most 192 MiB of HBM per device.

v0:
```python
import jax
import jax.numpy as jnp
from jax import lax
from jax.sharding import PartitionSpec as P

RADIUS = 8


opacity_scale = 0.008
grad_half = 1.0
light_x = 0.48
light_y = 0.6
light_z = 0.64
spatial_scale = 1.0 / 72.0
depth_weight = 20.0
normal_weight = 2.0


def with_halo(shard, sides, width):
    for axis, dim in sides:
        count, length = (lax.axis_size(axis), shard.shape[dim])
        up = [(i, (i + 1) % count) for i in range(count - 1)]
        down = [(j, i) for i, j in up]
        last = lax.slice_in_dim(shard, length - width, length, axis=dim)
        first = lax.slice_in_dim(shard, 0, width, axis=dim)
        before = lax.ppermute(last, axis, up)
        after = lax.ppermute(first, axis, down)
        shard = jnp.concatenate([before, shard, after], axis=dim)
    return shard


def swapped(block, axis, stride):
    count = lax.axis_size(axis)
    route = []
    for low in range(count):
        high = low | 1 << stride
        if high != low and high < count:
            route += [(low, high), (high, low)]
    return lax.ppermute(block, axis, route)


def polynomial(coeff, scaled):
    return coeff[0] + scaled * (coeff[1] + scaled * (coeff[2] + scaled * coeff[3]))


def integrate(field, flipped, tf_coeff, depth_start, depth_total):
    centre = field[1:-1, 1:-1, :]
    sideways = jnp.pad(centre, ((0, 0), (0, 0), (1, 1)))
    grad_x = (sideways[:, :, 2:] - sideways[:, :, :-2]) * grad_half
    grad_y = (field[1:-1, 2:, :] - field[1:-1, :-2, :]) * grad_half
    grad_z = (field[2:, 1:-1, :] - field[:-2, 1:-1, :]) * grad_half
    scaling = lax.rsqrt(1.0 + grad_x * grad_x + grad_y * grad_y + grad_z * grad_z)
    normal_x = grad_x * scaling
    normal_y = grad_y * scaling
    normal_z = grad_z * scaling
    shading = 0.35 + 0.65 * jnp.abs(light_x * normal_x + light_y * normal_y + light_z * normal_z)
    scaled = 2.0 * centre - 1.0
    sigma = opacity_scale * jax.nn.softplus(polynomial(tf_coeff[0], scaled))
    running = jnp.cumsum(sigma, axis=0)
    total = running[-1]
    optical = jnp.where(flipped == 1, total - running, running - sigma)
    weight = jnp.exp(-optical) * (1.0 - jnp.exp(-sigma))
    cells = sigma.shape[0]
    height = (
        (depth_start + jnp.arange(cells, dtype=jnp.int32)).astype(jnp.float32) + 0.5
    ) / depth_total
    height = jnp.where(flipped == 1, 1.0 - height, height)[:, None, None]
    planes = []
    for channel in range(1, 4):
        colour = jax.nn.sigmoid(polynomial(tf_coeff[channel], scaled)) * shading
        planes.append(jnp.sum(weight * colour, axis=0))
    planes.append(1.0 - jnp.exp(-total))
    planes.append(jnp.sum(weight * height, axis=0))
    planes.append(jnp.sum(weight * normal_x, axis=0))
    planes.append(jnp.sum(weight * normal_y, axis=0))
    planes.append(jnp.sum(weight * normal_z, axis=0))
    return jnp.stack(planes, axis=0)


def shade_image(extended, rows, cols):
    colour = extended[0:3]
    normal = extended[5:8]
    facing = jnp.maximum(light_x * normal[0] + light_y * normal[1] + light_z * normal[2], 0.0)
    lit = colour * (0.4 + 0.6 * facing)
    stacked = jnp.concatenate([extended, lit], axis=0)
    centre = extended[:, RADIUS : RADIUS + rows, RADIUS : RADIUS + cols]
    span = 2 * RADIUS + 1

    def row_step(offset_y, sums):
        numer, denom = sums
        offset_y = offset_y.astype(jnp.int32)
        rise = (offset_y - RADIUS).astype(jnp.float32)
        for offset_x in range(span):
            near = lax.dynamic_slice(
                stacked, (jnp.int32(0), offset_y, jnp.int32(offset_x)), (11, rows, cols)
            )
            run = float(offset_x - RADIUS)
            exponent = -(rise * rise + run * run) * spatial_scale
            exponent = exponent - depth_weight * (centre[4] - near[4]) ** 2
            exponent = exponent - normal_weight * jnp.sum((centre[5:8] - near[5:8]) ** 2, axis=0)
            weight = near[3] * jnp.exp(exponent)
            numer = numer + weight * near[8:11]
            denom = denom + weight
        return (numer, denom)

    start = (jnp.zeros((3, rows, cols), jnp.float32), jnp.zeros((rows, cols), jnp.float32))
    numer, denom = lax.fori_loop(0, span, row_step, start)
    return numer / (1.0 + denom)


def over_layer(front, back):
    return front + (1.0 - front[3:4]) * back


def reverse_bits(value, rounds):
    result = 0
    for level in range(rounds):
        result = result * 2 + (value >> level) % 2
    return result


def per_device(density, view_flip, tf_coeff):
    depth_cells, rows, width = density.shape
    count = lax.axis_size("depth")
    position = lax.axis_index("depth")
    flipped = view_flip[0]
    levels = density.astype(jnp.bfloat16)
    extended = with_halo(levels, (("depth", 0), ("tile", 1)), 1)
    field = extended.astype(jnp.float32) / 255.0
    planes = integrate(field, flipped, tf_coeff, position * depth_cells, depth_cells * count)
    columns = width // count
    blocks = planes.reshape(8, rows, count, columns)
    rounds = count.bit_length() - 1
    current = jnp.concatenate(
        [
            blocks[:, :, reverse_bits(place, rounds) : reverse_bits(place, rounds) + 1]
            for place in range(count)
        ],
        axis=2,
    )
    for level in range(rounds):
        half = current.shape[2] // 2
        upper = position // 2**level % 2
        kept = lax.dynamic_slice_in_dim(current, upper * half, half, 2)
        given = lax.dynamic_slice_in_dim(current, (1 - upper) * half, half, 2)
        partner = swapped(given, "depth", level)
        leading = upper == flipped
        front = jnp.where(leading, kept, partner)
        back = jnp.where(leading, partner, kept)
        current = over_layer(front, back)
    composite = current[:, :, 0]
    bordered = with_halo(composite, (("depth", 2), ("tile", 1)), RADIUS)
    return shade_image(bordered, rows, columns)


def solution(mesh):
    in_specs = (P("depth", "tile", None), P("tile"), P())
    out_specs = P(None, "tile", "depth")
    return jax.shard_map(
        per_device, mesh=mesh, in_specs=in_specs, out_specs=out_specs, check_vma=False
    )
```

profile of v0, /device:TPU:9, one launch (start us, length us, event | category | flops | bytes accessed | tf_op | source)
XLA Modules:
  0.0 294.8 jit_solution(12159834379690453884)
XLA Ops:
  0.0 4.6 %convert_element_type.25 = bf16[32,64,1024]{2,1,0:T(8,128)(2,1)S(1)} convert(s32[32,64,1024]{2,1,0:T(8,128)} %param.5) | non-fusion elementwise | flops 2097152 | bytes 12582912 | tf_op jit(solution)/shard_map/convert_element_type | solution.py:127
  6.6 3.7 %collective-permute-start = (bf16[1,64,1024]{2,1,0:T(8,128)(2,1)S(1)}, bf16[1,64,1024]{2,1,0:T(8,128)(2,1)S(1)}, u32[]{:S(2)}, u32[]{:S(2)}) collective-permute-start(bf16[1,64,1024]{2,1,0:T(8,128)(2,1)S(1)} %get-tuple-element.217), channel_id=1, source_target_pairs={{0,8},{8,16},{16,24},{1,9},{9,17},{17,25},{2,10},{10,18},{18,26},{... | collective-permute-start | bytes 393224 | tf_op jit(solution)/shard_map/ppermute | solution.py:26
  13.6 2.9 collective-permute-done.1
  18.0 3.1 %collective-permute-start.2 = (bf16[34,1,1024]{2,1,0:T(2,128)(2,1)S(1)}, bf16[34,1,1024]{2,1,0:T(2,128)(2,1)S(1)}, u32[]{:S(2)}, u32[]{:S(2)}) collective-permute-start(bf16[34,1,1024]{2,1,0:T(2,128)(2,1)S(1)} %get-tuple-element.215), channel_id=1, source_target_pairs={{0,1},{1,2},{2,3},{3,4},{4,5},{5,6},{6,7},{8,9},{9,10},{10,11},{11... | collective-permute-start | bytes 208904 | tf_op jit(solution)/shard_map/ppermute | solution.py:26
  21.1 3.1 %collective-permute-start.3 = (bf16[34,1,1024]{2,1,0:T(2,128)(2,1)S(1)}, bf16[34,1,1024]{2,1,0:T(2,128)(2,1)S(1)}, u32[]{:S(2)}, u32[]{:S(2)}) collective-permute-start(bf16[34,1,1024]{2,1,0:T(2,128)(2,1)S(1)} %get-tuple-element.216), channel_id=1, source_target_pairs={{1,0},{2,1},{3,2},{4,3},{5,4},{6,5},{7,6},{9,8},{10,9},{11,10},{12... | collective-permute-start | bytes 208904 | tf_op jit(solution)/shard_map/ppermute | solution.py:27
  24.8 2.8 collective-permute-done.3
  27.6 4.7 %convert_multiply_fusion = f32[34,66,1024]{2,1,0:T(8,128)S(1)} fusion(bf16[34,1,1024]{2,1,0:T(2,128)(2,1)S(1)} %collective-permute-done.3, bf16[1,64,1024]{2,1,0:T(8,128)(2,1)S(1)} %collective-permute-done.1, bf16[32,64,1024]{2,1,0:T(8,128)(2,1)} %copy-done.1, bf16[1,64,1024]{2,1,0:T(8,128)(2,1)S(1)} %collective-permute-done, ...), kind=kLoop, calls=%fused_computation.290 | loop fusion | flops 25276416 | bytes 13787136 | tf_op jit(solution)/shard_map/div | solution.py:129
  32.4 4.9 %slice.1012 = f32[32,64,1024]{2,1,0:T(8,128)} slice(f32[34,66,1024]{2,1,0:T(8,128)S(1)} %convert_multiply_fusion), slice={[1:33], [1:65], [0:1024]} | slice | bytes 16777216 | tf_op jit(solution)/shard_map/slice | solution.py:47
  38.6 10.4 %fusion.215 = f32[32,64,1024]{2,1,0:T(8,128)S(1)} fusion(f32[]{:T(128)} %bitcast.4, f32[]{:T(128)} %bitcast.3, f32[]{:T(128)} %bitcast.2, f32[]{:T(128)} %bitcast.1, f32[34,66,1024]{2,1,0:T(8,128)S(1)} %convert_multiply_fusion), kind=kOutput, calls=%fused_computation.353 | output fusion | flops 96468992 | bytes 16777232 | tf_op jit(solution)/shard_map/jit(cumsum)/reduce_window_sum | solution.py:59
  49.0 3.3 %copy-done.2 = f32[32,64,1024]{2,1,0:T(8,128)} copy-done((f32[32,64,1024]{2,1,0:T(8,128)}, f32[32,64,1024]{2,1,0:T(8,128)S(1)}, u32[]{:S(2)}) %copy-start.2) | copy-done | bytes 8388632
  53.1 41.3 %multiply_reduce_fusion = (f32[64,1024]{1,0:T(8,128)S(1)}, f32[64,1024]{1,0:T(8,128)S(1)}, f32[64,1024]{1,0:T(8,128)S(1)}, f32[64,1024]{1,0:T(8,128)S(1)}, f32[3...) fusion(f32[32]{0:T(128)S(1)} %broadcast_select_fusion.3, ...), kind=kLoop, calls=%fused_computation.297 | loop fusion | flops 87818240 | bytes 93585552 | tf_op jit(solution)/shard_map/reduce_sum | solution.py:76
  94.4 29.6 %multiply_reduce_fusion.4 = (f32[64,1024]{1,0:T(8,128)S(1)}, f32[64,1024]{1,0:T(8,128)}, f32[64,1024]{1,0:T(8,128)S(1)}) fusion(f32[32,64,1024]{2,1,0:T(8,128)} %get-tuple-element.194, f32[]{:T(128)} %bitcast.17, f32[]{:T(128)} %bitcast.16, f32[]{:T(128)} %bitcast.15, f32[]{:T(128)} %bitcast.14, f32[34,66,1024]{2,1,0:T(8,128)} %copy-done, f32[]{:T(128)} %bitcast.13, ...), kind=kLoop, calls=%fused_computation.301 | loop fusion | flops 115146752 | bytes 42729520 | tf_op jit(solution)/shard_map/reduce_sum | solution.py:71
  139.3 2.9 collective-permute-done.4
  146.2 13.0 %collective-permute-done.5 = f32[8,64,1,256]{3,2,1,0:T(1,128)S(1)} collective-permute-done((f32[8,64,1,256]{3,2,1,0:T(1,128)S(1)}, f32[8,64,1,256]{3,2,1,0:T(1,128)S(1)}, u32[]{:S(2)}, u32[]{:S(2)}) %collective-permute-start.5) | collective-permute-done | bytes 524320 | tf_op jit(solution)/shard_map/ppermute | solution.py:39
  161.0 3.1 %collective-permute-start.6 = (f32[8,64,8]{2,1,0:T(8,128)S(1)}, f32[8,64,8]{2,1,0:T(8,128)S(1)}, u32[]{:S(2)}, u32[]{:S(2)}) collective-permute-start(f32[8,64,8]{2,1,0:T(8,128)S(1)} %get-tuple-element.225), channel_id=1, source_target_pairs={{0,8},{8,16},{16,24},{1,9},{9,17},{17,25},{2,10},{10,18},{18,26},{... | collective-permute-start | bytes 49160 | tf_op jit(solution)/shard_map/ppermute | solution.py:26
  167.4 4.4 %collective-permute-done.7 = f32[8,64,8]{2,1,0:T(8,128)S(1)} collective-permute-done((f32[8,64,8]{2,1,0:T(8,128)S(1)}, f32[8,64,8]{2,1,0:T(8,128)S(1)}, u32[]{:S(2)}, u32[]{:S(2)}) %collective-permute-start.7) | collective-permute-done | bytes 16416 | tf_op jit(solution)/shard_map/ppermute | solution.py:27
  172.0 4.1 %collective-permute-start.8 = (f32[8,8,272]{2,1,0:T(8,128)S(1)}, f32[8,8,272]{2,1,0:T(8,128)S(1)}, u32[]{:S(2)}, u32[]{:S(2)}) collective-permute-start(f32[8,8,272]{2,1,0:T(8,128)S(1)} %get-tuple-element.223), channel_id=1, source_target_pairs={{0,1},{1,2},{2,3},{3,4},{4,5},{5,6},{6,7},{8,9},{9,10},{10,11},{11... | collective-permute-start | bytes 208904 | tf_op jit(solution)/shard_map/ppermute | solution.py:26
  178.3 3.1 %collective-permute-done.9 = f32[8,8,272]{2,1,0:T(8,128)S(1)} collective-permute-done((f32[8,8,272]{2,1,0:T(8,128)S(1)}, f32[8,8,272]{2,1,0:T(8,128)S(1)}, u32[]{:S(2)}, u32[]{:S(2)}) %collective-permute-start.9) | collective-permute-done | bytes 69664 | tf_op jit(solution)/shard_map/ppermute | solution.py:27
  182.3 110.9 %while.18 = (s32[]{:T(128)}, f32[3,64,256]{2,1,0:T(8,128)S(1)}, f32[64,256]{1,0:T(8,128)}, f32[11,80,272]{2,1,0:T(8,128)S(1)}, f32[8,64,256]{2,1,0:T(8,128)S(1)}...) while((s32[]{:T(128)}, f32[3,64,256]{2,1,0:T(8,128)S(1)}, ...), condition=%wide.region_26.27_spmd.clone, body=%wide.region_8.26_spmd.clone.sunk | while | flops 8142884 | bytes 17760984 | solution.py:107
  189.2 2.1 fusion.236
  195.8 2.1 fusion.236
  202.4 2.1 fusion.236
  215.5 2.1 fusion.236
  222.0 2.1 fusion.236
  235.1 2.1 fusion.236
  241.7 2.1 fusion.236
  248.3 2.1 fusion.236
  254.8 2.1 fusion.236
  261.4 2.1 fusion.236
  268.0 2.1 fusion.236
  274.5 2.1 fusion.236
  281.1 2.1 fusion.236
  (167 shorter events, 119.1 us)
Async XLA Ops:
  0.0 12.9 %copy-start.4 = (f32[4,4]{1,0:T(4,128)S(1)}, f32[4,4]{1,0:T(4,128)}, u32[]{:S(2)}) copy-start(f32[4,4]{1,0:T(4,128)} %param.7) | copy-start | bytes 196
  4.6 1.9 copy-start.1
  6.6 7.1 %collective-permute-start = (bf16[1,64,1024]{2,1,0:T(8,128)(2,1)S(1)}, bf16[1,64,1024]{2,1,0:T(8,128)(2,1)S(1)}, u32[]{:S(2)}, u32[]{:S(2)}) collective-permute-start(bf16[1,64,1024]{2,1,0:T(8,128)(2,1)S(1)} %get-tuple-element.217), channel_id=1, source_target_pairs={{0,8},{8,16},{16,24},{1,9},{9,17},{17,25},{2,10},{10,18},{18,26},{... | collective-permute-start | bytes 393224 | tf_op jit(solution)/shard_map/ppermute | solution.py:26
  10.3 6.3 %collective-permute-start.1 = (bf16[1,64,1024]{2,1,0:T(8,128)(2,1)S(1)}, bf16[1,64,1024]{2,1,0:T(8,128)(2,1)S(1)}, u32[]{:S(2)}, u32[]{:S(2)}) collective-permute-start(bf16[1,64,1024]{2,1,0:T(8,128)(2,1)S(1)} %get-tuple-element.218), channel_id=1, source_target_pairs={{8,0},{16,8},{24,16},{9,1},{17,9},{25,17},{10,2},{18,10},{26,18},{... | collective-permute-start | bytes 393224 | tf_op jit(solution)/shard_map/ppermute | solution.py:27
  18.0 6.8 %collective-permute-start.2 = (bf16[34,1,1024]{2,1,0:T(2,128)(2,1)S(1)}, bf16[34,1,1024]{2,1,0:T(2,128)(2,1)S(1)}, u32[]{:S(2)}, u32[]{:S(2)}) collective-permute-start(bf16[34,1,1024]{2,1,0:T(2,128)(2,1)S(1)} %get-tuple-element.215), channel_id=1, source_target_pairs={{0,1},{1,2},{2,3},{3,4},{4,5},{5,6},{6,7},{8,9},{9,10},{10,11},{11... | collective-permute-start | bytes 208904 | tf_op jit(solution)/shard_map/ppermute | solution.py:26
  21.1 6.5 %collective-permute-start.3 = (bf16[34,1,1024]{2,1,0:T(2,128)(2,1)S(1)}, bf16[34,1,1024]{2,1,0:T(2,128)(2,1)S(1)}, u32[]{:S(2)}, u32[]{:S(2)}) collective-permute-start(bf16[34,1,1024]{2,1,0:T(2,128)(2,1)S(1)} %get-tuple-element.216), channel_id=1, source_target_pairs={{1,0},{2,1},{3,2},{4,3},{5,4},{6,5},{7,6},{9,8},{10,9},{11,10},{12... | collective-permute-start | bytes 208904 | tf_op jit(solution)/shard_map/ppermute | solution.py:27
  32.4 6.3 %copy-start = (f32[34,66,1024]{2,1,0:T(8,128)}, f32[34,66,1024]{2,1,0:T(8,128)S(1)}, u32[]{:S(2)}) copy-start(f32[34,66,1024]{2,1,0:T(8,128)S(1)} %convert_multiply_fusion) | copy-start | bytes 27574276
  49.0 3.3 %copy-start.2 = (f32[32,64,1024]{2,1,0:T(8,128)}, f32[32,64,1024]{2,1,0:T(8,128)S(1)}, u32[]{:S(2)}) copy-start(f32[32,64,1024]{2,1,0:T(8,128)S(1)} %fusion.215) | copy-start | bytes 25165828
  139.3 2.9 collective-permute-start.4
  142.2 1.0 copy-start.3
  145.8 13.4 %collective-permute-start.5 = (f32[8,64,1,256]{3,2,1,0:T(1,128)S(1)}, f32[8,64,1,256]{3,2,1,0:T(1,128)S(1)}, u32[]{:S(2)}, u32[]{:S(2)}) collective-permute-start(f32[8,64,1,256]{3,2,1,0:T(1,128)S(1)} %constant_dynamic-slice_fusion), channel_id=1, source_target_pairs={{0,16},{16,0},{8,24},{24,8},{1,17},{17,1},{9,25},{25,9},{2,18},{18... | collective-permute-start | bytes 1572872 | tf_op jit(solution)/shard_map/ppermute | solution.py:39
  161.0 6.4 %collective-permute-start.6 = (f32[8,64,8]{2,1,0:T(8,128)S(1)}, f32[8,64,8]{2,1,0:T(8,128)S(1)}, u32[]{:S(2)}, u32[]{:S(2)}) collective-permute-start(f32[8,64,8]{2,1,0:T(8,128)S(1)} %get-tuple-element.225), channel_id=1, source_target_pairs={{0,8},{8,16},{16,24},{1,9},{9,17},{17,25},{2,10},{10,18},{18,26},{... | collective-permute-start | bytes 49160 | tf_op jit(solution)/shard_map/ppermute | solution.py:26
  164.1 7.7 %collective-permute-start.7 = (f32[8,64,8]{2,1,0:T(8,128)S(1)}, f32[8,64,8]{2,1,0:T(8,128)S(1)}, u32[]{:S(2)}, u32[]{:S(2)}) collective-permute-start(f32[8,64,8]{2,1,0:T(8,128)S(1)} %get-tuple-element.226), channel_id=1, source_target_pairs={{8,0},{16,8},{24,16},{9,1},{17,9},{25,17},{10,2},{18,10},{26,18},{... | collective-permute-start | bytes 49160 | tf_op jit(solution)/shard_map/ppermute | solution.py:27
  172.0 6.4 %collective-permute-start.8 = (f32[8,8,272]{2,1,0:T(8,128)S(1)}, f32[8,8,272]{2,1,0:T(8,128)S(1)}, u32[]{:S(2)}, u32[]{:S(2)}) collective-permute-start(f32[8,8,272]{2,1,0:T(8,128)S(1)} %get-tuple-element.223), channel_id=1, source_target_pairs={{0,1},{1,2},{2,3},{3,4},{4,5},{5,6},{6,7},{8,9},{9,10},{10,11},{11... | collective-permute-start | bytes 208904 | tf_op jit(solution)/shard_map/ppermute | solution.py:26
  176.1 5.4 %collective-permute-start.9 = (f32[8,8,272]{2,1,0:T(8,128)S(1)}, f32[8,8,272]{2,1,0:T(8,128)S(1)}, u32[]{:S(2)}, u32[]{:S(2)}) collective-permute-start(f32[8,8,272]{2,1,0:T(8,128)S(1)} %get-tuple-element.224), channel_id=1, source_target_pairs={{1,0},{2,1},{3,2},{4,3},{5,4},{6,5},{7,6},{9,8},{10,9},{11,10},{12... | collective-permute-start | bytes 208904 | tf_op jit(solution)/shard_map/ppermute | solution.py:27
where the time goes:
time: 298 us; the launch traced here: 295 us
  other arithmetic  211 us (71%)
  waiting for transfers between devices  31.2 us (10%)
  local copies, waits for them, and re-layouts  26.4 us (9%)
  starting transfers between devices  23.4 us (8%)
    reduce_sum x1, other arithmetic, integrate(): planes.append(jnp.sum(weight * normal_z, axis=0))  41.3 us
    add x17, other arithmetic, row_step(): denom = denom + weight  35.7 us
    add x17, other arithmetic, row_step(): numer = numer + weight * near[8:11]  31.6 us
    reduce_sum x1, other arithmetic, integrate(): planes.append(jnp.sum(weight * colour, axis=0))  29.6 us
    mul x68, other arithmetic, row_step(): numer = numer + weight * near[8:11]  26.6 us
    ppermute x2, waiting for transfers between devices, swapped(): return lax.ppermute(block, axis, route)  15.9 us
    reduce_sum x17, other arithmetic, row_step(): jnp.sum((centre[5:8] - near[5:8]) ** 2, axis=0)  15.3 us
    ppermute x4, starting transfers between devices, with_halo(): before = lax.ppermute(last, axis, up)  14 us
  transfers between devices with their start and end apart: 10, of which 9 were waited for; matrix products, arithmetic and copies ran while one was open for 0% of the time, Pallas kernels for 0%

commit v1 on v0

v1 whole, which is shorter than its diff:
```python
import functools
import math

import jax
import jax.numpy as jnp
from jax import lax
from jax.experimental import pallas as pl
from jax.experimental.pallas import tpu as pltpu
from jax.sharding import PartitionSpec as P

RADIUS = 8
LANES = 128
SUB = 8
LOG2E = math.log2(math.e)
OPACITY = 0.008
LIGHT = (0.48, 0.6, 0.64)
SPATIAL = 1.0 / 72.0
DEPTH_W = 20.0
NORMAL_W = 2.0
CENTRE = 127.5


def shifts(axis):
    count = lax.axis_size(axis)
    up = [(i, i + 1) for i in range(count - 1)]
    return up, [(j, i) for i, j in up]


def swapped(block, axis, stride):
    count = lax.axis_size(axis)
    route = []
    for low in range(count):
        high = low | 1 << stride
        if high != low and high < count:
            route += [(low, high), (high, low)]
    return lax.ppermute(block, axis, route)


def integrate_kernel(
    depth_total, flip_ref, base_ref, coeff_ref, density_ref, zlo_ref, zhi_ref, ylo_ref, yhi_ref,
    out_ref, stage, field, ylo_f, yhi_f, sems,
):
    cells, rows, width = density_ref.shape
    tiles = width // LANES
    copies = []
    for z in range(cells):
        copies.append(pltpu.make_async_copy(density_ref.at[z], stage.at[z], sems.at[z]))
        copies[-1].start()
    flip = flip_ref[0]
    outside = jnp.full((SUB, LANES), -CENTRE, jnp.float32)
    for j in range(tiles):
        cols = pl.ds(j * LANES, LANES)
        ylo_f[j] = ylo_ref[:, cols].astype(jnp.float32) - CENTRE
        yhi_f[j] = yhi_ref[:, cols].astype(jnp.float32) - CENTRE
        field[0, j + 1, SUB : SUB + rows, :] = zlo_ref[:, cols].astype(jnp.float32) - CENTRE
        field[cells + 1, j + 1, SUB : SUB + rows, :] = zhi_ref[:, cols].astype(jnp.float32) - CENTRE

    def fill(z, carry):
        pltpu.make_async_copy(density_ref.at[z], stage.at[z], sems.at[z]).wait()
        for i in range(rows // SUB):
            field[z + 1, 0, pl.ds(SUB + SUB * i, SUB), :] = outside
            field[z + 1, tiles + 1, pl.ds(SUB + SUB * i, SUB), :] = outside
        for j in range(tiles):
            cols = pl.ds(j * LANES, LANES)
            field[z + 1, j + 1, SUB : SUB + rows, :] = stage[z, :, cols].astype(jnp.float32) - CENTRE
            field[z + 1, j + 1, SUB - 1 : SUB, :] = ylo_f[j, pl.ds(z, 1), :]
            field[z + 1, j + 1, SUB + rows : SUB + rows + 1, :] = yhi_f[j, pl.ds(z, 1), :]
        return carry

    lax.fori_loop(0, cells, fill, 0)

    coeffs = []
    for row in range(4):
        scale = LOG2E if row == 0 else -LOG2E
        coeffs.append([coeff_ref[row, k] * (scale / CENTRE**k) for k in range(4)])
    sign = jnp.where(flip == 1, 1.0, -1.0)
    rate = sign * OPACITY
    lx, ly, lz = (0.65 * v for v in LIGHT)
    lane = lax.broadcasted_iota(jnp.int32, (SUB, LANES), 1)
    first_lane = lane == 0
    last_lane = lane == LANES - 1
    base = base_ref[0]
    step = 1.0 / depth_total
    start = (base.astype(jnp.float32) + 0.5) * step
    finish = (base.astype(jnp.float32) + (cells - 0.5)) * step
    h_first = jnp.where(flip == 1, 1.0 - start, start)
    h_last = jnp.where(flip == 1, 1.0 - finish, finish)
    delta = jnp.where(flip == 1, -step, step)

    def poly(c, t):
        return c[0] + t * (c[1] + t * (c[2] + t * c[3]))

    def block(index, carry):
        j = index // (rows // SUB) + 1
        r = pl.multiple_of((index % (rows // SUB)) * SUB, SUB)
        at = pl.ds(r + SUB, SUB)
        zero = jnp.zeros((SUB, LANES), jnp.float32)
        tau = zero
        factor = jnp.ones((SUB, LANES), jnp.float32)
        between = zero
        sums = [zero] * 6
        below = field[0, j, at, :]
        here = field[1, j, at, :]
        for z in range(1, cells + 1):
            above = field[z + 1, j, at, :]
            left = pltpu.roll(jnp.where(last_lane, field[z, j - 1, at, :], here), 1, 1)
            right = pltpu.roll(jnp.where(first_lane, field[z, j + 1, at, :], here), LANES - 1, 1)
            gx = right - left
            gy = field[z, j, pl.ds(r + SUB + 1, SUB), :] - field[z, j, pl.ds(r + SUB - 1, SUB), :]
            gz = above - below
            norm = lax.rsqrt(gx * gx + gy * gy + (gz * gz + 255.0 * 255.0))
            shade = 0.35 + jnp.abs((lx * gx + ly * gy + lz * gz) * norm)
            tau = tau + jnp.log2(1.0 + jnp.exp2(poly(coeffs[0], here)))
            following = jnp.exp2(rate * tau)
            weight = following - factor
            factor = following
            if z < cells:
                between = between + following
            tilt = weight * norm
            lit = weight * shade
            terms = [lit * (1.0 / (1.0 + jnp.exp2(poly(coeffs[k], here)))) for k in (1, 2, 3)]
            terms += [tilt * gx, tilt * gy, tilt * gz]
            sums = [s + t for s, t in zip(sums, terms)]
            below, here = here, above
        inverse = 1.0 / factor
        flipped = flip == 1
        scale = jnp.where(flipped, inverse, -1.0)
        for k in range(3):
            out_ref[k, j - 1, pl.ds(r, SUB), :] = sums[k] * scale
            out_ref[k + 5, j - 1, pl.ds(r, SUB), :] = sums[k + 3] * scale
        out_ref[3, j - 1, pl.ds(r, SUB), :] = 1.0 - jnp.where(flipped, inverse, factor)
        out_ref[4, j - 1, pl.ds(r, SUB), :] = (h_last * factor - h_first - delta * between) * scale
        return carry

    lax.fori_loop(0, tiles * (rows // SUB), block, 0)


def integrate(density, view_flip, tf_coeff, base, depth_total, zlo, zhi, ylo, yhi):
    cells, rows, width = density.shape
    tiles = width // LANES
    smem = pl.BlockSpec(memory_space=pltpu.SMEM)
    vmem = pl.BlockSpec(memory_space=pltpu.VMEM)
    return pl.pallas_call(
        functools.partial(integrate_kernel, depth_total),
        out_shape=jax.ShapeDtypeStruct((8, tiles, rows, LANES), jnp.float32),
        in_specs=[smem, smem, smem, pl.BlockSpec(memory_space=pl.ANY), vmem, vmem, vmem, vmem],
        out_specs=vmem,
        scratch_shapes=[
            pltpu.VMEM((cells, rows, width), jnp.int32),
            pltpu.VMEM((cells + 2, tiles + 2, rows + 2 * SUB, LANES), jnp.float32),
            pltpu.VMEM((tiles, cells, LANES), jnp.float32),
            pltpu.VMEM((tiles, cells, LANES), jnp.float32),
            pltpu.SemaphoreType.DMA((cells,)),
        ],
        compiler_params=pltpu.CompilerParams(vmem_limit_bytes=48 << 20),
        name="integrate",
    )(view_flip, base, tf_coeff, density, zlo, zhi, ylo, yhi)


def shade_kernel(
    core_ref, left_ref, right_ref, top_ref, bottom_ref, out_ref, planes, feats, buf_a, buf_b, acc
):
    _, tiles, rows, _ = core_ref.shape
    blocks = rows // SUB
    halves = blocks // 4
    cols = tiles * LANES
    for k in range(8):
        for t in (0, tiles + 1):
            planes[k, t] = jnp.zeros((rows + 2 * SUB, LANES), jnp.float32)
        planes[k, 0, SUB : SUB + rows, LANES - RADIUS : LANES] = left_ref[k]
        planes[k, tiles + 1, SUB : SUB + rows, 0:RADIUS] = right_ref[k]
        for j in range(tiles):
            planes[k, j + 1, SUB : SUB + rows, :] = core_ref[k, j]
        for ref, start in ((top_ref, 0), (bottom_ref, SUB + rows)):
            planes[k, 0, start : start + SUB, LANES - RADIUS : LANES] = ref[k, :, 0:RADIUS]
            planes[k, tiles + 1, start : start + SUB, 0:RADIUS] = ref[
                k, :, cols + RADIUS : cols + 2 * RADIUS
            ]
            for j in range(tiles):
                planes[k, j + 1, start : start + SUB, :] = ref[
                    k, :, RADIUS + j * LANES : RADIUS + (j + 1) * LANES
                ]

    row_blocks = blocks + 2

    def features(index, carry):
        t = index // row_blocks
        at = pl.ds(pl.multiple_of((index % row_blocks) * SUB, SUB), SUB)
        red, green, blue, alpha, depth, nx, ny, nz = [planes[k, t, at, :] for k in range(8)]
        facing = jnp.maximum(LIGHT[0] * nx + LIGHT[1] * ny + LIGHT[2] * nz, 0.0)
        lit = 0.4 + 0.6 * facing
        own = (DEPTH_W * LOG2E) * depth * depth + (NORMAL_W * LOG2E) * (nx * nx + ny * ny + nz * nz)
        feats[0, t, at, :] = jnp.log2(jnp.maximum(alpha, 1e-37)) - own
        feats[1, t, at, :] = depth
        feats[2, t, at, :] = nx
        feats[3, t, at, :] = ny
        feats[4, t, at, :] = nz
        feats[5, t, at, :] = red * lit
        feats[6, t, at, :] = green * lit
        feats[7, t, at, :] = blue * lit
        return carry

    lax.fori_loop(0, (tiles + 2) * row_blocks, features, 0)
    lane = lax.broadcasted_iota(jnp.int32, (SUB, LANES), 1)

    def shift(index, buf, j, blk):
        offset = index - RADIUS
        run = offset.astype(jnp.float32)
        spread = -(SPATIAL * LOG2E) * run * run
        other = jnp.where(offset < 0, j, j + 2)
        border = jnp.where(offset < 0, LANES + offset, offset)
        amount = jnp.where(offset > 0, LANES - offset, -offset)
        below = lane < border
        take_other = (below & (offset >= 0)) | (jnp.logical_not(below) & (offset < 0))
        at = pl.ds(pl.multiple_of(blk * SUB, SUB), SUB)
        for k in range(8):
            mixed = jnp.where(take_other, feats[k, other, at, :], feats[k, j + 1, at, :])
            moved = pltpu.roll(mixed, amount, 1)
            if k == 0:
                moved = moved + spread
            buf[k, j, at, :] = moved

    for j in range(tiles):
        for k in range(4):
            acc[k, j] = jnp.zeros((rows, LANES), jnp.float32)

    def shift_all(index, buf):
        def one(t, carry):
            shift(index, buf, t // row_blocks, t % row_blocks)
            return carry

        lax.fori_loop(0, tiles * row_blocks, one, 0)

    share = -(-row_blocks // halves)

    def taps(buf, next_index, next_buf):
        def one(t, carry):
            j = t // halves
            half = t % halves
            first = half * 4
            if next_buf is not None:
                for b in range(share):
                    shift(next_index, next_buf, j, jnp.minimum(half * share + b, row_blocks - 1))
            own = []
            for i in range(4):
                rows_at = pl.ds(SUB + first + i, SUB, stride=blocks)
                depth = feats[1, j + 1, rows_at, :] * (2.0 * DEPTH_W * LOG2E)
                normal = [
                    feats[k, j + 1, rows_at, :] * (2.0 * NORMAL_W * LOG2E) for k in (2, 3, 4)
                ]
                own.append([depth] + normal)
            sums = [
                [acc[k, j, pl.ds(first + i, SUB, stride=blocks), :] for k in range(4)]
                for i in range(4)
            ]
            for near in range(-RADIUS, 4 + RADIUS):
                q = [
                    buf[k, j, pl.ds(SUB + first + near, SUB, stride=blocks), :] for k in range(8)
                ]
                for i in range(4):
                    dy = near - i
                    if abs(dy) > RADIUS:
                        continue
                    p = own[i]
                    power = (q[0] + p[0] * q[1]) + (p[1] * q[2] + p[2] * q[3])
                    power = power + (p[3] * q[4] - SPATIAL * LOG2E * dy * dy)
                    weight = jnp.exp2(power)
                    s = sums[i]
                    sums[i] = [
                        s[0] + weight * q[5],
                        s[1] + weight * q[6],
                        s[2] + weight * q[7],
                        s[3] + weight,
                    ]
            for i in range(4):
                for k in range(4):
                    acc[k, j, pl.ds(first + i, SUB, stride=blocks), :] = sums[i][k]
            return carry

        lax.fori_loop(0, tiles * halves, one, 0)

    shift_all(jnp.int32(0), buf_a)

    def pair(step, carry):
        taps(buf_a, 2 * step + 1, buf_b)
        taps(buf_b, 2 * step + 2, buf_a)
        return carry

    lax.fori_loop(0, RADIUS, pair, 0)
    taps(buf_a, None, None)

    for j in range(tiles):
        for b in range(blocks):
            at = pl.ds(b * SUB, SUB)
            inner = pl.ds(SUB + b * SUB, SUB)
            depth, nx, ny, nz = [feats[k, j + 1, inner, :] for k in (1, 2, 3, 4)]
            own = (DEPTH_W * LOG2E) * depth * depth + (NORMAL_W * LOG2E) * (
                nx * nx + ny * ny + nz * nz
            )
            level = jnp.exp2(-own)
            scale = level / (1.0 + level * acc[3, j, at, :])
            for k in range(3):
                out_ref[k, at, pl.ds(j * LANES, LANES)] = acc[k, j, at, :] * scale


def shade(core, left, right, top, bottom):
    _, tiles, rows, _ = core.shape
    vmem = pl.BlockSpec(memory_space=pltpu.VMEM)
    wide = (8, tiles + 2, rows + 2 * SUB, LANES)
    moved = (8, tiles, rows + 2 * SUB, LANES)
    return pl.pallas_call(
        shade_kernel,
        out_shape=jax.ShapeDtypeStruct((3, rows, tiles * LANES), jnp.float32),
        in_specs=[vmem] * 5,
        out_specs=vmem,
        scratch_shapes=[
            pltpu.VMEM(wide, jnp.float32),
            pltpu.VMEM(wide, jnp.float32),
            pltpu.VMEM(moved, jnp.float32),
            pltpu.VMEM(moved, jnp.float32),
            pltpu.VMEM((4, tiles, rows, LANES), jnp.float32),
        ],
        compiler_params=pltpu.CompilerParams(vmem_limit_bytes=32 << 20),
        name="shade",
    )(core, left, right, top, bottom)


def over_layer(front, back):
    return front + (1.0 - front[3:4]) * back


def reverse_bits(value, rounds):
    result = 0
    for level in range(rounds):
        result = result * 2 + (value >> level) % 2
    return result


def per_device(density, view_flip, tf_coeff):
    cells, rows, width = density.shape
    count = lax.axis_size("depth")
    position = lax.axis_index("depth")
    flipped = view_flip[0]
    up, down = shifts("depth")
    zlo = lax.ppermute(density[-1].astype(jnp.bfloat16), "depth", up)
    zhi = lax.ppermute(density[0].astype(jnp.bfloat16), "depth", down)
    up, down = shifts("tile")
    ylo = lax.ppermute(density[:, -1].astype(jnp.bfloat16), "tile", up)
    yhi = lax.ppermute(density[:, 0].astype(jnp.bfloat16), "tile", down)
    base = (position * cells).astype(jnp.int32).reshape(1)
    planes = integrate(density, view_flip, tf_coeff, base, cells * count, zlo, zhi, ylo, yhi)
    tiles = width // LANES
    own = tiles // count
    rounds = count.bit_length() - 1
    blocks = planes.reshape(8, count, own, rows, LANES)
    current = jnp.concatenate(
        [
            blocks[:, reverse_bits(place, rounds) : reverse_bits(place, rounds) + 1]
            for place in range(count)
        ],
        axis=1,
    )
    for level in range(rounds):
        half = current.shape[1] // 2
        upper = position // 2**level % 2
        kept = lax.dynamic_slice_in_dim(current, upper * half, half, 1)
        given = lax.dynamic_slice_in_dim(current, (1 - upper) * half, half, 1)
        partner = swapped(given, "depth", level)
        leading = upper == flipped
        front = jnp.where(leading, kept, partner)
        back = jnp.where(leading, partner, kept)
        current = over_layer(front, back)
    core = current[:, 0]
    up, down = shifts("depth")
    left = lax.ppermute(core[:, -1, :, LANES - RADIUS :], "depth", up)
    right = lax.ppermute(core[:, 0, :, :RADIUS], "depth", down)
    up, down = shifts("tile")

    def edge(start):
        pieces = [left[:, start : start + RADIUS]]
        pieces += [core[:, j, start : start + RADIUS] for j in range(own)]
        pieces += [right[:, start : start + RADIUS]]
        return jnp.concatenate(pieces, axis=2)

    top = lax.ppermute(edge(rows - RADIUS), "tile", up)
    bottom = lax.ppermute(edge(0), "tile", down)
    return shade(core, left, right, top, bottom)


def solution(mesh):
    in_specs = (P("depth", "tile", None), P("tile"), P())
    out_specs = P(None, "tile", "depth")
    return jax.shard_map(
        per_device, mesh=mesh, in_specs=in_specs, out_specs=out_specs, check_vma=False
    )
```

time: 298 us -> 120 us (0.40)
  the two profiles are of different devices: /device:TPU:9 before, /device:TPU:4 now
where the time goes in v1:
time: 120 us
  Pallas kernels  53.9 us (45%)
  waiting for transfers between devices  31.4 us (26%)
  starting transfers between devices  20.3 us (17%)
  other arithmetic  10.1 us (8%)
  local copies, waits for them, and re-layouts  3.03 us (3%)
    pallas_call x1, Pallas kernels, integrate(): pl.pallas_call(functools.partial(integrate_kernel, depth_total), out_shap...  27.1 us
    pallas_call x1, Pallas kernels, shade(): pl.pallas_call(shade_kernel, out_shape=jax.ShapeDtypeStruct((3, rows, til...  26.8 us
    ppermute x2, waiting for transfers between devices, swapped(): return lax.ppermute(block, axis, route)  16.8 us
    another operation x1, other arithmetic  7.84 us
    ppermute x1, waiting for transfers between devices, per_device(): bottom = lax.ppermute(edge(0), 'tile', down)  4.43 us
    ppermute x1, starting transfers between devices, per_device(): top = lax.ppermute(edge(rows - RADIUS), 'tile', up)  4.36 us
    ppermute x1, waiting for transfers between devices, per_device(): yhi = lax.ppermute(density[:, 0].astype(jnp.bfloat16), 'tile', down)  4.18 us
    ppermute x1, waiting for transfers between devices, per_device(): left = lax.ppermute(core[:, -1, :, LANES - RADIUS:], 'depth', up)  3.84 us
  transfers between devices with their start and end apart: 10, of which 7 were waited for; matrix products, arithmetic and copies ran while one was open for 0% of the time, Pallas kernels for 0%

profile of v1, /device:TPU:4, one launch (start us, length us, event | category | flops | bytes accessed | tf_op | source)
XLA Modules:
  0.0 119.7 jit_solution(3701470537540020412)
XLA Ops:
  0.0 7.8 %copy_convert_fusion = bf16[32,64,1024]{2,0,1:T(8,128)(2,1)S(1)} fusion(s32[32,64,1024]{2,1,0:T(8,128)} %density_ref.1), kind=kLoop, calls=%fused_computation | loop fusion | flops 2097152 | bytes 12582912 | tf_op jit(solution)/shard_map/convert.3
  7.9 0.5 fusion.2
  8.4 1.9 %collective-permute-start = (bf16[64,1024]{1,0:T(8,128)(2,1)S(1)}, bf16[64,1024]{1,0:T(8,128)(2,1)S(1)}, u32[]{:S(2)}, u32[]{:S(2)}) collective-permute-start(bf16[64,1024]{1,0:T(8,128)(2,1)S(1)} %bitcast.34), channel_id=1, source_target_pairs={{0,8},{8,16},{16,24},{1,9},{9,17},{17,25},{2,10},{10,18},{18,26},{... | collective-permute-start | bytes 393224 | tf_op jit(solution)/shard_map/ppermute | solution.py:345
  10.3 3.6 %collective-permute-start.1 = (bf16[64,1024]{1,0:T(8,128)(2,1)S(1)}, bf16[64,1024]{1,0:T(8,128)(2,1)S(1)}, u32[]{:S(2)}, u32[]{:S(2)}) collective-permute-start(bf16[64,1024]{1,0:T(8,128)(2,1)S(1)} %bitcast.35), channel_id=1, source_target_pairs={{8,0},{16,8},{24,16},{9,1},{17,9},{25,17},{10,2},{18,10},{26,18},{... | collective-permute-start | bytes 393224 | tf_op jit(solution)/shard_map/ppermute | solution.py:346
  14.0 3.4 %collective-permute-start.2 = (bf16[32,1024]{1,0:T(8,128)(2,1)S(1)}, bf16[32,1024]{1,0:T(8,128)(2,1)S(1)}, u32[]{:S(2)}, u32[]{:S(2)}) collective-permute-start(bf16[32,1024]{1,0:T(8,128)(2,1)S(1)} %get-tuple-element.6), channel_id=1, source_target_pairs={{0,1},{1,2},{2,3},{3,4},{4,5},{5,6},{6,7},{8,9},{9,10},{10,11},{11... | collective-permute-start | bytes 196616 | tf_op jit(solution)/shard_map/ppermute | solution.py:348
  17.4 1.3 %collective-permute-start.3 = (bf16[32,1024]{1,0:T(8,128)(2,1)S(1)}, bf16[32,1024]{1,0:T(8,128)(2,1)S(1)}, u32[]{:S(2)}, u32[]{:S(2)}) collective-permute-start(bf16[32,1024]{1,0:T(8,128)(2,1)S(1)} %get-tuple-element.5), channel_id=1, source_target_pairs={{1,0},{2,1},{3,2},{4,3},{5,4},{6,5},{7,6},{9,8},{10,9},{11,10},{12... | collective-permute-start | bytes 196616 | tf_op jit(solution)/shard_map/ppermute | solution.py:349
  19.4 4.2 %collective-permute-done.3.yhi_ref = bf16[32,1024]{1,0:T(8,128)(2,1)S(1)} collective-permute-done((bf16[32,1024]{1,0:T(8,128)(2,1)S(1)}, bf16[32,1024]{1,0:T(8,128)(2,1)S(1)}, u32[]{:S(2)}, u32[]{:S(2)}) %collective-permute-start.3) | collective-permute-done | bytes 65568 | tf_op jit(solution)/shard_map/ppermute | solution.py:349
  23.6 27.1 %integrate.1 = f32[8,8,64,128]{3,2,1,0:T(8,128)S(1)} custom-call(s32[1]{0:T(128)} %copy.17.flip_ref, s32[1]{0:T(128)} %bitcast.1.base_ref, f32[4,4]{1,0:T(4,128)S(1)} %copy-done, s32[32,64,1024]{2,1,0:T(8,128)} %density_ref.1, bf16[64,1024]{1,0:T(8,128)(2,1)S(1)} %collective-permute-done.zlo_ref, bf16[64,1024]{1,0:T(8,128)(2,1)S(1)} %collective-permute-done.1.zhi_ref, ...), custom_call_target="tpu_custom_call" | custom-call | tf_op jit(solution)/shard_map/integrate/pallas_call | solution.py:143
  50.7 0.1 copy.8
  50.8 0.2 fusion.3
  51.1 0.2 pad_maximum_fusion
  51.3 1.1 constant_dynamic-slice_fusion.1
  52.4 2.9 %collective-permute-done.4 = f32[8,2,2,64,128]{4,3,0,2,1:T(8,128)S(1)} collective-permute-done((f32[8,2,2,64,128]{4,3,0,2,1:T(8,128)}, f32[8,2,2,64,128]{4,3,0,2,1:T(8,128)S(1)}, u32[]{:S(2)}, u32[]{:S(2)}) %collective-permute-start.4) | collective-permute-done | bytes 1048608 | tf_op jit(solution)/shard_map/ppermute | solution.py:36
  55.3 0.2 dynamic-slice_select_fusion
  55.5 0.8 copy-done.1
  56.3 1.5 %multiply_add_fusion = f32[8,2,2,64,128]{4,3,0,2,1:T(8,128)S(1)} fusion(f32[8,2,2,64,128]{4,3,0,2,1:T(8,128)} %copy-done.1, f32[8,4,2,64,128]{4,3,0,2,1:T(8,128)S(1)} %pad_maximum_fusion, s32[]{:T(128)S(6)} %select_n.57, f32[2,2,64,128]{3,2,1,0:T(8,128)S(1)} %fusion, pred[]{:T(512)S(6)} %eq.10), kind=kLoop, calls=%fused_computation.2 | loop fusion | flops 1048576 | bytes 3276805 | tf_op jit(solution)/shard_map/add | solution.py:329
  57.8 0.1 collective-permute-start.5
  57.9 13.9 %collective-permute-done.5 = f32[8,1,2,64,128]{4,3,0,2,1:T(8,128)S(1)} collective-permute-done((f32[8,1,2,64,128]{4,3,0,2,1:T(8,128)S(1)}, f32[8,1,2,64,128]{4,3,0,2,1:T(8,128)S(1)}, u32[]{:S(2)}, u32[]{:S(2)}) %collective-permute-start.5) | collective-permute-done | bytes 524320 | tf_op jit(solution)/shard_map/ppermute | solution.py:36
  71.8 0.1 dynamic-slice_select_fusion.1
  71.9 0.1 add_bitcast_fusion
  72.0 0.1 slice_bitcast_fusion
  72.1 1.9 %collective-permute-start.7 = (f32[8,64,8]{2,1,0:T(8,128)S(1)}, f32[8,64,8]{2,1,0:T(8,128)S(1)}, u32[]{:S(2)}, u32[]{:S(2)}) collective-permute-start(f32[8,64,8]{2,1,0:T(8,128)S(1)} %get-tuple-element.17), channel_id=1, source_target_pairs={{8,0},{16,8},{24,16},{9,1},{17,9},{25,17},{10,2},{18,10},{26,18},{... | collective-permute-start | bytes 49160 | tf_op jit(solution)/shard_map/ppermute | solution.py:376
  74.1 2.4 %collective-permute-start.6 = (f32[8,64,8]{2,1,0:T(8,128)S(1)}, f32[8,64,8]{2,1,0:T(8,128)S(1)}, u32[]{:S(2)}, u32[]{:S(2)}) collective-permute-start(f32[8,64,8]{2,1,0:T(8,128)S(1)} %get-tuple-element.18), channel_id=1, source_target_pairs={{0,8},{8,16},{16,24},{1,9},{9,17},{17,25},{2,10},{10,18},{18,26},{... | collective-permute-start | bytes 49160 | tf_op jit(solution)/shard_map/ppermute | solution.py:375
  76.5 1.4 %collective-permute-done.7.right_ref = f32[8,64,8]{2,1,0:T(8,128)S(1)} collective-permute-done((f32[8,64,8]{2,1,0:T(8,128)S(1)}, f32[8,64,8]{2,1,0:T(8,128)S(1)}, u32[]{:S(2)}, u32[]{:S(2)}) %collective-permute-start.7) | collective-permute-done | bytes 16416 | tf_op jit(solution)/shard_map/ppermute | solution.py:376
  77.9 3.8 %collective-permute-done.6.left_ref = f32[8,64,8]{2,1,0:T(8,128)S(1)} collective-permute-done((f32[8,64,8]{2,1,0:T(8,128)S(1)}, f32[8,64,8]{2,1,0:T(8,128)S(1)}, u32[]{:S(2)}, u32[]{:S(2)}) %collective-permute-start.6) | collective-permute-done | bytes 16416 | tf_op jit(solution)/shard_map/ppermute | solution.py:375
  81.8 0.1 pad_maximum_fusion.1
  81.9 4.4 %collective-permute-start.8 = (f32[8,8,272]{2,1,0:T(8,128)S(1)}, f32[8,8,272]{2,1,0:T(8,128)S(1)}, u32[]{:S(2)}, u32[]{:S(2)}) collective-permute-start(f32[8,8,272]{2,1,0:T(8,128)S(1)} %pad_maximum_fusion.1), channel_id=1, source_target_pairs={{0,1},{1,2},{2,3},{3,4},{4,5},{5,6},{6,7},{8,9},{9,10},{10,11},{11... | collective-permute-start | bytes 208904 | tf_op jit(solution)/shard_map/ppermute | solution.py:385
  86.2 0.1 pad_maximum_fusion.2
  86.4 1.3 %collective-permute-start.9 = (f32[8,8,272]{2,1,0:T(8,128)S(1)}, f32[8,8,272]{2,1,0:T(8,128)S(1)}, u32[]{:S(2)}, u32[]{:S(2)}) collective-permute-start(f32[8,8,272]{2,1,0:T(8,128)S(1)} %pad_maximum_fusion.2), channel_id=1, source_target_pairs={{1,0},{2,1},{3,2},{4,3},{5,4},{6,5},{7,6},{9,8},{10,9},{11,10},{12... | collective-permute-start | bytes 208904 | tf_op jit(solution)/shard_map/ppermute | solution.py:386
  87.7 0.7 collective-permute-done.8.top_ref
  88.4 4.4 %collective-permute-done.9.bottom_ref = f32[8,8,272]{2,1,0:T(8,128)S(1)} collective-permute-done((f32[8,8,272]{2,1,0:T(8,128)S(1)}, f32[8,8,272]{2,1,0:T(8,128)S(1)}, u32[]{:S(2)}, u32[]{:S(2)}) %collective-permute-start.9) | collective-permute-done | bytes 69664 | tf_op jit(solution)/shard_map/ppermute | solution.py:386
  92.9 26.8 %shade.1 = f32[3,64,256]{2,1,0:T(8,128)} custom-call(f32[8,2,64,128]{3,2,1,0:T(8,128)S(1)} %copy.9.core_ref, f32[8,64,8]{2,1,0:T(8,128)S(1)} %collective-permute-done.6.left_ref, f32[8,64,8]{2,1,0:T(8,128)S(1)} %collective-permute-done.7.right_ref, f32[8,8,272]{2,1,0:T(8,128)S(1)} %collective-permute-done.8.top_ref, ...), custom_call_target="tpu_custom_call" | custom-call | tf_op jit(solution)/shard_map/shade/pallas_call | solution.py:311
  (17 shorter events, 0.3 us)
Async XLA Ops:
  7.8 15.7 %copy-start = (f32[4,4]{1,0:T(4,128)S(1)}, f32[4,4]{1,0:T(4,128)}, u32[]{:S(2)}) copy-start(f32[4,4]{1,0:T(4,128)} %coeff_ref.1) | copy-start | bytes 196
  8.4 15.2 %collective-permute-start = (bf16[64,1024]{1,0:T(8,128)(2,1)S(1)}, bf16[64,1024]{1,0:T(8,128)(2,1)S(1)}, u32[]{:S(2)}, u32[]{:S(2)}) collective-permute-start(bf16[64,1024]{1,0:T(8,128)(2,1)S(1)} %bitcast.34), channel_id=1, source_target_pairs={{0,8},{8,16},{16,24},{1,9},{9,17},{17,25},{2,10},{10,18},{18,26},{... | collective-permute-start | bytes 393224 | tf_op jit(solution)/shard_map/ppermute | solution.py:345
  10.3 13.2 %collective-permute-start.1 = (bf16[64,1024]{1,0:T(8,128)(2,1)S(1)}, bf16[64,1024]{1,0:T(8,128)(2,1)S(1)}, u32[]{:S(2)}, u32[]{:S(2)}) collective-permute-start(bf16[64,1024]{1,0:T(8,128)(2,1)S(1)} %bitcast.35), channel_id=1, source_target_pairs={{8,0},{16,8},{24,16},{9,1},{17,9},{25,17},{10,2},{18,10},{26,18},{... | collective-permute-start | bytes 393224 | tf_op jit(solution)/shard_map/ppermute | solution.py:346
  14.0 5.4 %collective-permute-start.2 = (bf16[32,1024]{1,0:T(8,128)(2,1)S(1)}, bf16[32,1024]{1,0:T(8,128)(2,1)S(1)}, u32[]{:S(2)}, u32[]{:S(2)}) collective-permute-start(bf16[32,1024]{1,0:T(8,128)(2,1)S(1)} %get-tuple-element.6), channel_id=1, source_target_pairs={{0,1},{1,2},{2,3},{3,4},{4,5},{5,6},{6,7},{8,9},{9,10},{10,11},{11... | collective-permute-start | bytes 196616 | tf_op jit(solution)/shard_map/ppermute | solution.py:348
  17.4 6.2 %collective-permute-start.3 = (bf16[32,1024]{1,0:T(8,128)(2,1)S(1)}, bf16[32,1024]{1,0:T(8,128)(2,1)S(1)}, u32[]{:S(2)}, u32[]{:S(2)}) collective-permute-start(bf16[32,1024]{1,0:T(8,128)(2,1)S(1)} %get-tuple-element.5), channel_id=1, source_target_pairs={{1,0},{2,1},{3,2},{4,3},{5,4},{6,5},{7,6},{9,8},{10,9},{11,10},{12... | collective-permute-start | bytes 196616 | tf_op jit(solution)/shard_map/ppermute | solution.py:349
  52.4 2.9 %collective-permute-start.4 = (f32[8,2,2,64,128]{4,3,0,2,1:T(8,128)}, f32[8,2,2,64,128]{4,3,0,2,1:T(8,128)S(1)}, u32[]{:S(2)}, u32[]{:S(2)}) collective-permute-start(f32[8,2,2,64,128]{4,3,0,2,1:T(8,128)} %constant_dynamic-slice_fusion.1), channel_id=1, source_target_pairs={{0,8},{8,0},{16,24},{24,16},{1,9},{9,1},{17,25},{25,17},{2,10},{10... | collective-permute-start | bytes 3145736 | tf_op jit(solution)/shard_map/ppermute | solution.py:36
  55.3 1.0 copy-start.1
  57.8 14.0 %collective-permute-start.5 = (f32[8,1,2,64,128]{4,3,0,2,1:T(8,128)S(1)}, f32[8,1,2,64,128]{4,3,0,2,1:T(8,128)S(1)}, u32[]{:S(2)}, u32[]{:S(2)}) collective-permute-start(f32[8,1,2,64,128]{4,3,0,2,1:T(8,128)S(1)} %constant_dynamic-slice_fusion), channel_id=1, source_target_pairs={{0,16},{16,0},{8,24},{24,8},{1,17},{17,1},{9,25},{25,9},{2,18},{18... | collective-permute-start | bytes 1572872 | tf_op jit(solution)/shard_map/ppermute | solution.py:36
  72.1 5.8 %collective-permute-start.7 = (f32[8,64,8]{2,1,0:T(8,128)S(1)}, f32[8,64,8]{2,1,0:T(8,128)S(1)}, u32[]{:S(2)}, u32[]{:S(2)}) collective-permute-start(f32[8,64,8]{2,1,0:T(8,128)S(1)} %get-tuple-element.17), channel_id=1, source_target_pairs={{8,0},{16,8},{24,16},{9,1},{17,9},{25,17},{10,2},{18,10},{26,18},{... | collective-permute-start | bytes 49160 | tf_op jit(solution)/shard_map/ppermute | solution.py:376
  74.1 7.7 %collective-permute-start.6 = (f32[8,64,8]{2,1,0:T(8,128)S(1)}, f32[8,64,8]{2,1,0:T(8,128)S(1)}, u32[]{:S(2)}, u32[]{:S(2)}) collective-permute-start(f32[8,64,8]{2,1,0:T(8,128)S(1)} %get-tuple-element.18), channel_id=1, source_target_pairs={{0,8},{8,16},{16,24},{1,9},{9,17},{17,25},{2,10},{10,18},{18,26},{... | collective-permute-start | bytes 49160 | tf_op jit(solution)/shard_map/ppermute | solution.py:375
  81.9 6.6 %collective-permute-start.8 = (f32[8,8,272]{2,1,0:T(8,128)S(1)}, f32[8,8,272]{2,1,0:T(8,128)S(1)}, u32[]{:S(2)}, u32[]{:S(2)}) collective-permute-start(f32[8,8,272]{2,1,0:T(8,128)S(1)} %pad_maximum_fusion.1), channel_id=1, source_target_pairs={{0,1},{1,2},{2,3},{3,4},{4,5},{5,6},{6,7},{8,9},{9,10},{10,11},{11... | collective-permute-start | bytes 208904 | tf_op jit(solution)/shard_map/ppermute | solution.py:385
  86.4 6.5 %collective-permute-start.9 = (f32[8,8,272]{2,1,0:T(8,128)S(1)}, f32[8,8,272]{2,1,0:T(8,128)S(1)}, u32[]{:S(2)}, u32[]{:S(2)}) collective-permute-start(f32[8,8,272]{2,1,0:T(8,128)S(1)} %pad_maximum_fusion.2), channel_id=1, source_target_pairs={{1,0},{2,1},{3,2},{4,3},{5,4},{6,5},{7,6},{9,8},{10,9},{11,10},{12... | collective-permute-start | bytes 208904 | tf_op jit(solution)/shard_map/ppermute | solution.py:386

commit v2 on v1

--- a/solution.py
+++ b/solution.py
@@ -36,38 +36,93 @@
     return lax.ppermute(block, axis, route)
 
 
+def edges_kernel(density_ref, zlo_ref, zhi_ref, ylo_ref, yhi_ref, planes, bands, lines, sems):
+    cells, rows, width = density_ref.shape
+    tiles = width // LANES
+    copies = []
+    for side in range(2):
+        copies.append(
+            pltpu.make_async_copy(
+                density_ref.at[side * (cells - 1)], planes.at[side], sems.at[2 * side]
+            )
+        )
+        copies.append(
+            pltpu.make_async_copy(
+                density_ref.at[:, side * (rows - SUB) : side * (rows - SUB) + SUB, :],
+                bands.at[side],
+                sems.at[2 * side + 1],
+            )
+        )
+    for copy in copies:
+        copy.start()
+    for copy in copies:
+        copy.wait()
+    zlo_ref[...] = planes[0].astype(jnp.float32).astype(jnp.bfloat16)
+    zhi_ref[...] = planes[1].astype(jnp.float32).astype(jnp.bfloat16)
+    for side, ref in ((0, ylo_ref), (1, yhi_ref)):
+        row = side * (SUB - 1)
+        for z in range(cells):
+            lines[z : z + 1, :] = bands[side, z, row : row + 1, :].astype(jnp.float32)
+        ref[...] = lines[...].astype(jnp.bfloat16)
+
+
+def edges(density):
+    cells, rows, width = density.shape
+    vmem = pl.BlockSpec(memory_space=pltpu.VMEM)
+    plane = jax.ShapeDtypeStruct((rows, width), jnp.bfloat16)
+    line = jax.ShapeDtypeStruct((cells, width), jnp.bfloat16)
+    return pl.pallas_call(
+        edges_kernel,
+        out_shape=(plane, plane, line, line),
+        in_specs=[pl.BlockSpec(memory_space=pl.ANY)],
+        out_specs=[vmem] * 4,
+        scratch_shapes=[
+            pltpu.VMEM((2, rows, width), jnp.int32),
+            pltpu.VMEM((2, cells, SUB, width), jnp.int32),
+            pltpu.VMEM((cells, width), jnp.float32),
+            pltpu.SemaphoreType.DMA((4,)),
+        ],
+        compiler_params=pltpu.CompilerParams(vmem_limit_bytes=24 << 20),
+        name="edges",
+    )(density)
+
+
 def integrate_kernel(
-    depth_total, flip_ref, base_ref, coeff_ref, density_ref, zlo_ref, zhi_ref, ylo_ref, yhi_ref,
-    out_ref, stage, field, ylo_f, yhi_f, sems,
+    place, own, flip_ref, coeff_ref, density_ref, zlo_ref, zhi_ref, ylo_ref, yhi_ref,
+    out_ref, field, zlo_f, zhi_f, sems,
 ):
     cells, rows, width = density_ref.shape
     tiles = width // LANES
-    copies = []
-    for z in range(cells):
-        copies.append(pltpu.make_async_copy(density_ref.at[z], stage.at[z], sems.at[z]))
-        copies[-1].start()
+    blocks = rows // SUB
+    count = tiles // own
+    position = lax.axis_index("depth")
+    c, y = position % 2, position // 2 % 2
+    first = (lax.rem(c + place[0], 2) + 2 * lax.rem(y + place[1], 2) + 4 * place[2]) * own
+    sources = [jnp.maximum(first - 1, 0)]
+    sources += [first + j for j in range(own)]
+    sources += [jnp.minimum(first + own, tiles - 1)]
+
+    def copy(b, j):
+        start = pl.multiple_of(sources[j] * LANES, LANES)
+        return pltpu.make_async_copy(
+            density_ref.at[:, pl.ds(b * SUB, SUB), pl.ds(start, LANES)],
+            field.at[:, j, pl.ds(SUB + b * SUB, SUB), :],
+            sems.at[b, j],
+        )
+
+    for b in range(blocks):
+        for j in range(own + 2):
+            copy(b, j).start()
     flip = flip_ref[0]
-    outside = jnp.full((SUB, LANES), -CENTRE, jnp.float32)
-    for j in range(tiles):
-        cols = pl.ds(j * LANES, LANES)
-        ylo_f[j] = ylo_ref[:, cols].astype(jnp.float32) - CENTRE
-        yhi_f[j] = yhi_ref[:, cols].astype(jnp.float32) - CENTRE
-        field[0, j + 1, SUB : SUB + rows, :] = zlo_ref[:, cols].astype(jnp.float32) - CENTRE
-        field[cells + 1, j + 1, SUB : SUB + rows, :] = zhi_ref[:, cols].astype(jnp.float32) - CENTRE
-
-    def fill(z, carry):
-        pltpu.make_async_copy(density_ref.at[z], stage.at[z], sems.at[z]).wait()
-        for i in range(rows // SUB):
-            field[z + 1, 0, pl.ds(SUB + SUB * i, SUB), :] = outside
-            field[z + 1, tiles + 1, pl.ds(SUB + SUB * i, SUB), :] = outside
-        for j in range(tiles):
-            cols = pl.ds(j * LANES, LANES)
-            field[z + 1, j + 1, SUB : SUB + rows, :] = stage[z, :, cols].astype(jnp.float32) - CENTRE
-            field[z + 1, j + 1, SUB - 1 : SUB, :] = ylo_f[j, pl.ds(z, 1), :]
-            field[z + 1, j + 1, SUB + rows : SUB + rows + 1, :] = yhi_f[j, pl.ds(z, 1), :]
-        return carry
-
-    lax.fori_loop(0, cells, fill, 0)
+    for j in range(own):
+        cols = pl.ds(pl.multiple_of((first + j) * LANES, LANES), LANES)
+        zlo_f[j] = zlo_ref[:, cols].astype(jnp.float32) - CENTRE
+        zhi_f[j] = zhi_ref[:, cols].astype(jnp.float32) - CENTRE
+        top = ylo_ref[:, cols].astype(jnp.float32).astype(jnp.int32)
+        bottom = yhi_ref[:, cols].astype(jnp.float32).astype(jnp.int32)
+        for z in range(cells):
+            field[z, j + 1, SUB - 1 : SUB, :] = top[z : z + 1]
+            field[z, j + 1, SUB + rows : SUB + rows + 1, :] = bottom[z : z + 1]
 
     coeffs = []
     for row in range(4):
@@ -79,10 +134,10 @@
     lane = lax.broadcasted_iota(jnp.int32, (SUB, LANES), 1)
     first_lane = lane == 0
     last_lane = lane == LANES - 1
-    base = base_ref[0]
-    step = 1.0 / depth_total
-    start = (base.astype(jnp.float32) + 0.5) * step
-    finish = (base.astype(jnp.float32) + (cells - 0.5)) * step
+    base = (position * cells).astype(jnp.float32)
+    step = 1.0 / (cells * count)
+    start = (base + 0.5) * step
+    finish = (base + (cells - 0.5)) * step
     h_first = jnp.where(flip == 1, 1.0 - start, start)
     h_last = jnp.where(flip == 1, 1.0 - finish, finish)
     delta = jnp.where(flip == 1, -step, step)
@@ -90,23 +145,55 @@
     def poly(c, t):
         return c[0] + t * (c[1] + t * (c[2] + t * c[3]))
 
-    def block(index, carry):
-        j = index // (rows // SUB) + 1
-        r = pl.multiple_of((index % (rows // SUB)) * SUB, SUB)
+    def arrive(b):
+        for j in range(own + 2):
+            copy(b, j).wait()
+        at = pl.ds(SUB + b * SUB, SUB)
+
+        @pl.when(first == 0)
+        def _():
+            for z in range(cells):
+                field[z, 0, at, :] = jnp.zeros((SUB, LANES), jnp.int32)
+
+        @pl.when(first + own == tiles)
+        def _():
+            for z in range(cells):
+                field[z, own + 1, at, :] = jnp.zeros((SUB, LANES), jnp.int32)
+
+    arrive(0)
+
+    def block(b, carry):
+        @pl.when(b + 1 < blocks)
+        def _():
+            arrive(b + 1)
+
+        r = pl.multiple_of(b * SUB, SUB)
+        for j in range(1, own + 1):
+            column(r, j)
+        return carry
+
+    def column(r, j):
         at = pl.ds(r + SUB, SUB)
         zero = jnp.zeros((SUB, LANES), jnp.float32)
         tau = zero
         factor = jnp.ones((SUB, LANES), jnp.float32)
         between = zero
         sums = [zero] * 6
-        below = field[0, j, at, :]
-        here = field[1, j, at, :]
-        for z in range(1, cells + 1):
-            above = field[z + 1, j, at, :]
-            left = pltpu.roll(jnp.where(last_lane, field[z, j - 1, at, :], here), 1, 1)
-            right = pltpu.roll(jnp.where(first_lane, field[z, j + 1, at, :], here), LANES - 1, 1)
-            gx = right - left
-            gy = field[z, j, pl.ds(r + SUB + 1, SUB), :] - field[z, j, pl.ds(r + SUB - 1, SUB), :]
+        below = zlo_f[j - 1, pl.ds(r, SUB), :]
+        raw = field[0, j, at, :]
+        here = raw.astype(jnp.float32) - CENTRE
+        for z in range(cells):
+            if z + 1 < cells:
+                raw_above = field[z + 1, j, at, :]
+                above = raw_above.astype(jnp.float32) - CENTRE
+            else:
+                raw_above = raw
+                above = zhi_f[j - 1, pl.ds(r, SUB), :]
+            left = pltpu.roll(jnp.where(last_lane, field[z, j - 1, at, :], raw), 1, 1)
+            right = pltpu.roll(jnp.where(first_lane, field[z, j + 1, at, :], raw), LANES - 1, 1)
+            gx = (right - left).astype(jnp.float32)
+            up = field[z, j, pl.ds(r + SUB + 1, SUB), :]
+            gy = (up - field[z, j, pl.ds(r + SUB - 1, SUB), :]).astype(jnp.float32)
             gz = above - below
             norm = lax.rsqrt(gx * gx + gy * gy + (gz * gz + 255.0 * 255.0))
             shade = 0.35 + jnp.abs((lx * gx + ly * gy + lz * gz) * norm)
@@ -114,47 +201,50 @@
             following = jnp.exp2(rate * tau)
             weight = following - factor
             factor = following
-            if z < cells:
+            if z < cells - 1:
                 between = between + following
             tilt = weight * norm
             lit = weight * shade
             terms = [lit * (1.0 / (1.0 + jnp.exp2(poly(coeffs[k], here)))) for k in (1, 2, 3)]
             terms += [tilt * gx, tilt * gy, tilt * gz]
             sums = [s + t for s, t in zip(sums, terms)]
-            below, here = here, above
+            below, here, raw = here, above, raw_above
         inverse = 1.0 / factor
         flipped = flip == 1
         scale = jnp.where(flipped, inverse, -1.0)
+        out = pl.ds(r, SUB)
         for k in range(3):
-            out_ref[k, j - 1, pl.ds(r, SUB), :] = sums[k] * scale
-            out_ref[k + 5, j - 1, pl.ds(r, SUB), :] = sums[k + 3] * scale
-        out_ref[3, j - 1, pl.ds(r, SUB), :] = 1.0 - jnp.where(flipped, inverse, factor)
-        out_ref[4, j - 1, pl.ds(r, SUB), :] = (h_last * factor - h_first - delta * between) * scale
-        return carry
-
-    lax.fori_loop(0, tiles * (rows // SUB), block, 0)
-
-
-def integrate(density, view_flip, tf_coeff, base, depth_total, zlo, zhi, ylo, yhi):
+            out_ref[k, j - 1, out, :] = sums[k] * scale
+            out_ref[k + 5, j - 1, out, :] = sums[k + 3] * scale
+        out_ref[3, j - 1, out, :] = 1.0 - jnp.where(flipped, inverse, factor)
+        out_ref[4, j - 1, out, :] = (h_last * factor - h_first - delta * between) * scale
+
+    lax.fori_loop(0, blocks, block, 0)
+
+
+def integrate(place, count, view_flip, tf_coeff, density, zlo, zhi, ylo, yhi):
     cells, rows, width = density.shape
-    tiles = width // LANES
+    own = width // LANES // count
     smem = pl.BlockSpec(memory_space=pltpu.SMEM)
     vmem = pl.BlockSpec(memory_space=pltpu.VMEM)
+    voxels = cells * rows * own * LANES
     return pl.pallas_call(
-        functools.partial(integrate_kernel, depth_total),
-        out_shape=jax.ShapeDtypeStruct((8, tiles, rows, LANES), jnp.float32),
-        in_specs=[smem, smem, smem, pl.BlockSpec(memory_space=pl.ANY), vmem, vmem, vmem, vmem],
+        functools.partial(integrate_kernel, place, own),
+        out_shape=jax.ShapeDtypeStruct((8, own, rows, LANES), jnp.float32),
+        in_specs=[smem, smem, pl.BlockSpec(memory_space=pl.ANY), vmem, vmem, vmem, vmem],
         out_specs=vmem,
         scratch_shapes=[
-            pltpu.VMEM((cells, rows, width), jnp.int32),
-            pltpu.VMEM((cells + 2, tiles + 2, rows + 2 * SUB, LANES), jnp.float32),
-            pltpu.VMEM((tiles, cells, LANES), jnp.float32),
-            pltpu.VMEM((tiles, cells, LANES), jnp.float32),
-            pltpu.SemaphoreType.DMA((cells,)),
+            pltpu.VMEM((cells, own + 2, rows + 2 * SUB, LANES), jnp.int32),
+            pltpu.VMEM((own, rows, LANES), jnp.float32),
+            pltpu.VMEM((own, rows, LANES), jnp.float32),
+            pltpu.SemaphoreType.DMA((rows // SUB, own + 2)),
         ],
-        compiler_params=pltpu.CompilerParams(vmem_limit_bytes=48 << 20),
+        compiler_params=pltpu.CompilerParams(vmem_limit_bytes=24 << 20),
+        cost_estimate=pl.CostEstimate(
+            flops=70 * voxels, transcendentals=10 * voxels, bytes_accessed=8 * voxels
+        ),
         name="integrate",
-    )(view_flip, base, tf_coeff, density, zlo, zhi, ylo, yhi)
+    )(view_flip, tf_coeff, density, zlo, zhi, ylo, yhi)
 
 
 def shade_kernel(
@@ -203,22 +293,29 @@
     lax.fori_loop(0, (tiles + 2) * row_blocks, features, 0)
     lane = lax.broadcasted_iota(jnp.int32, (SUB, LANES), 1)
 
-    def shift(index, buf, j, blk):
+
+    def shift_setup(index):
         offset = index - RADIUS
         run = offset.astype(jnp.float32)
         spread = -(SPATIAL * LOG2E) * run * run
-        other = jnp.where(offset < 0, j, j + 2)
         border = jnp.where(offset < 0, LANES + offset, offset)
         amount = jnp.where(offset > 0, LANES - offset, -offset)
         below = lane < border
         take_other = (below & (offset >= 0)) | (jnp.logical_not(below) & (offset < 0))
+        return jnp.where(offset < 0, 0, 2), amount, take_other, spread
+
+    def moved(setup, k, j, blk):
+        other, amount, take_other, spread = setup
+        at = pl.ds(blk * SUB, SUB)
+        mixed = jnp.where(take_other, feats[k, j + other, at, :], feats[k, j + 1, at, :])
+        m = pltpu.roll(mixed, amount, 1)
+        return m + spread if k == 0 else m
+
+    def shift(index, buf, j, blk):
+        s = shift_setup(index)
         at = pl.ds(pl.multiple_of(blk * SUB, SUB), SUB)
         for k in range(8):
-            mixed = jnp.where(take_other, feats[k, other, at, :], feats[k, j + 1, at, :])
-            moved = pltpu.roll(mixed, amount, 1)
-            if k == 0:
-                moved = moved + spread
-            buf[k, j, at, :] = moved
+            buf[k, j, at, :] = moved(s, k, j, blk)
 
     for j in range(tiles):
         for k in range(4):
@@ -234,13 +331,25 @@
     share = -(-row_blocks // halves)
 
     def taps(buf, next_index, next_buf):
+        pending = []
+        items = []
+        if next_buf is not None:
+            setup = shift_setup(next_index)
+            items = [(k, jj, b) for jj in range(tiles) for b in range(row_blocks) for k in range(8)]
+
+        def pump(force=False):
+            for _ in range(2):
+                if items:
+                    k, jj, b = items.pop(0)
+                    pending.append((moved(setup, k, jj, b), k, jj, b))
+            while len(pending) > (0 if force else 8):
+                v, k, jj, b = pending.pop(0)
+                next_buf[k, jj, pl.ds(b * SUB, SUB), :] = v
+
         def one(t, carry):
             j = t // halves
             half = t % halves
             first = half * 4
-            if next_buf is not None:
-                for b in range(share):
-                    shift(next_index, next_buf, j, jnp.minimum(half * share + b, row_blocks - 1))
             own = []
             for i in range(4):
                 rows_at = pl.ds(SUB + first + i, SUB, stride=blocks)
@@ -257,6 +366,7 @@
                 q = [
                     buf[k, j, pl.ds(SUB + first + near, SUB, stride=blocks), :] for k in range(8)
                 ]
+                pump()
                 for i in range(4):
                     dy = near - i
                     if abs(dy) > RADIUS:
@@ -277,7 +387,8 @@
                     acc[k, j, pl.ds(first + i, SUB, stride=blocks), :] = sums[i][k]
             return carry
 
-        lax.fori_loop(0, tiles * halves, one, 0)
+        for t in range(tiles*halves): one(t,0)
+        while items or pending: pump(not items)
 
     shift_all(jnp.int32(0), buf_a)
 
@@ -325,10 +436,6 @@
     )(core, left, right, top, bottom)
 
 
-def over_layer(front, back):
-    return front + (1.0 - front[3:4]) * back
-
-
 def reverse_bits(value, rounds):
     result = 0
     for level in range(rounds):
@@ -336,41 +443,60 @@
     return result
 
 
+def over(kept, partner, kept_leads):
+    front = jnp.where(kept_leads, kept, partner)
+    back = jnp.where(kept_leads, partner, kept)
+    return front + (1.0 - front[3:4]) * back
+
+
 def per_device(density, view_flip, tf_coeff):
     cells, rows, width = density.shape
     count = lax.axis_size("depth")
     position = lax.axis_index("depth")
     flipped = view_flip[0]
+    rounds = count.bit_length() - 1
+    high = count // 4
+    first_plane, last_plane, first_line, last_line = edges(density)
     up, down = shifts("depth")
-    zlo = lax.ppermute(density[-1].astype(jnp.bfloat16), "depth", up)
-    zhi = lax.ppermute(density[0].astype(jnp.bfloat16), "depth", down)
+    zlo = lax.ppermute(last_plane, "depth", up)
+    zhi = lax.ppermute(first_plane, "depth", down)
     up, down = shifts("tile")
-    ylo = lax.ppermute(density[:, -1].astype(jnp.bfloat16), "tile", up)
-    yhi = lax.ppermute(density[:, 0].astype(jnp.bfloat16), "tile", down)
-    base = (position * cells).astype(jnp.int32).reshape(1)
-    planes = integrate(density, view_flip, tf_coeff, base, cells * count, zlo, zhi, ylo, yhi)
-    tiles = width // LANES
-    own = tiles // count
-    rounds = count.bit_length() - 1
-    blocks = planes.reshape(8, count, own, rows, LANES)
-    current = jnp.concatenate(
-        [
-            blocks[:, reverse_bits(place, rounds) : reverse_bits(place, rounds) + 1]
-            for place in range(count)
-        ],
-        axis=1,
-    )
-    for level in range(rounds):
+    ylo = lax.ppermute(last_line, "tile", up)
+    yhi = lax.ppermute(first_line, "tile", down)
+
+    def quarter(core_bit, chip_bit, flip):
+        parts = [
+            integrate(
+                (core_bit, chip_bit, h), count, flip, tf_coeff, density, zlo, zhi, ylo, yhi
+            )
+            for h in range(high)
+        ]
+        return jnp.stack(parts, axis=1)
+
+    leads = [position // 2**level % 2 == flipped for level in range(rounds)]
+    far_given = quarter(1, 1, view_flip)
+    far_given, flip = lax.optimization_barrier((far_given, view_flip))
+    far_partner = swapped(far_given, "depth", 0)
+    far_kept = quarter(0, 1, flip)
+    far = over(far_kept, far_partner, leads[0])
+    far, flip = lax.optimization_barrier((far, flip))
+    chip_partner = swapped(far, "depth", 1)
+    near_given = quarter(1, 0, flip)
+    near_given, flip = lax.optimization_barrier((near_given, flip))
+    near_partner = swapped(near_given, "depth", 0)
+    near_kept = quarter(0, 0, flip)
+    current = over(over(near_kept, near_partner, leads[0]), chip_partner, leads[1])
+    for level in range(2, rounds):
         half = current.shape[1] // 2
+        order = [reverse_bits(place, rounds - 2) for place in range(high)]
+        if level == 2:
+            current = jnp.concatenate([current[:, p : p + 1] for p in order], axis=1)
         upper = position // 2**level % 2
         kept = lax.dynamic_slice_in_dim(current, upper * half, half, 1)
         given = lax.dynamic_slice_in_dim(current, (1 - upper) * half, half, 1)
-        partner = swapped(given, "depth", level)
-        leading = upper == flipped
-        front = jnp.where(leading, kept, partner)
-        back = jnp.where(leading, partner, kept)
-        current = over_layer(front, back)
+        current = over(kept, swapped(given, "depth", level), leads[level])
     core = current[:, 0]
+    own = core.shape[1]
     up, down = shifts("depth")
     left = lax.ppermute(core[:, -1, :, LANES - RADIUS :], "depth", up)
     right = lax.ppermute(core[:, 0, :, :RADIUS], "depth", down)

time: 120 us -> 104 us (0.87)
  the two profiles are of different devices: /device:TPU:4 before, /device:TPU:9 now
where the time goes in v2:
time: 104 us; the launch traced here: 103 us
  Pallas kernels  51.7 us (50%)
  starting transfers between devices  27.4 us (26%)
  waiting for transfers between devices  12.3 us (12%)
  local copies, waits for them, and re-layouts  10.4 us (10%)
    pallas_call x4, Pallas kernels, integrate(): pl.pallas_call(functools.partial(integrate_kernel, place, own), out_shape...  29.7 us
    pallas_call x1, Pallas kernels, shade(): pl.pallas_call(shade_kernel, out_shape=jax.ShapeDtypeStruct((3, rows, til...  21.6 us
    unnamed x8, local copies, waits for them, and re-layouts  10.1 us
    ppermute x1, waiting for transfers between devices, per_device(): right = lax.ppermute(core[:, 0, :, :RADIUS], 'depth', down)  4.41 us
    ppermute x1, starting transfers between devices, per_device(): left = lax.ppermute(core[:, -1, :, LANES - RADIUS:], 'depth', up)  4.05 us
    ppermute x1, starting transfers between devices, per_device(): bottom = lax.ppermute(edge(0), 'tile', down)  3.96 us
    ppermute x1, starting transfers between devices, per_device(): zlo = lax.ppermute(last_plane, 'depth', up)  3.71 us
    ppermute x3, starting transfers between devices, swapped(): return lax.ppermute(block, axis, route)  3.41 us
  transfers between devices with their start and end apart: 11, of which 6 were waited for; matrix products, arithmetic and copies ran while one was open for 0% of the time, Pallas kernels for 22%

profile of v2, /device:TPU:9, one launch (start us, length us, event | category | flops | bytes accessed | tf_op | source)
XLA Modules:
  0.0 103.4 jit_solution(5142233101213038862)
XLA Ops:
  0.0 3.4 %copy-done = s32[32,64,1024]{2,1,0:T(8,128)S(1)} copy-done((s32[32,64,1024]{2,1,0:T(8,128)S(1)}, s32[32,64,1024]{2,1,0:T(8,128)}, u32[]{:S(2)}) %copy-start) | copy-done | bytes 8388632
  3.4 0.4 edges.1
  3.8 3.7 %collective-permute-start = (bf16[64,1024]{1,0:T(8,128)(2,1)S(1)}, bf16[64,1024]{1,0:T(8,128)(2,1)S(1)}, u32[]{:S(2)}, u32[]{:S(2)}) collective-permute-start(bf16[64,1024]{1,0:T(8,128)(2,1)S(1)} %get-tuple-element.15), channel_id=1, source_target_pairs={{0,8},{8,16},{16,24},{1,9},{9,17},{17,25},{2,10},{10,18},{18,26},{... | collective-permute-start | bytes 393224 | tf_op jit(solution)/shard_map/ppermute | solution.py:461
  7.5 1.9 %collective-permute-start.1 = (bf16[64,1024]{1,0:T(8,128)(2,1)S(1)}, bf16[64,1024]{1,0:T(8,128)(2,1)S(1)}, u32[]{:S(2)}, u32[]{:S(2)}) collective-permute-start(bf16[64,1024]{1,0:T(8,128)(2,1)S(1)} %get-tuple-element.16), channel_id=1, source_target_pairs={{8,0},{16,8},{24,16},{9,1},{17,9},{25,17},{10,2},{18,10},{26,18},{... | collective-permute-start | bytes 393224 | tf_op jit(solution)/shard_map/ppermute | solution.py:462
  9.5 3.1 %collective-permute-start.2 = (bf16[32,1024]{1,0:T(8,128)(2,1)S(1)}, bf16[32,1024]{1,0:T(8,128)(2,1)S(1)}, u32[]{:S(2)}, u32[]{:S(2)}) collective-permute-start(bf16[32,1024]{1,0:T(8,128)(2,1)S(1)} %get-tuple-element.17), channel_id=1, source_target_pairs={{0,1},{1,2},{2,3},{3,4},{4,5},{5,6},{6,7},{8,9},{9,10},{10,11},{11... | collective-permute-start | bytes 196616 | tf_op jit(solution)/shard_map/ppermute | solution.py:464
  12.6 3.1 %collective-permute-start.3 = (bf16[32,1024]{1,0:T(8,128)(2,1)S(1)}, bf16[32,1024]{1,0:T(8,128)(2,1)S(1)}, u32[]{:S(2)}, u32[]{:S(2)}) collective-permute-start(bf16[32,1024]{1,0:T(8,128)(2,1)S(1)} %get-tuple-element.18), channel_id=1, source_target_pairs={{1,0},{2,1},{3,2},{4,3},{5,4},{6,5},{7,6},{9,8},{10,9},{11,10},{12... | collective-permute-start | bytes 196616 | tf_op jit(solution)/shard_map/ppermute | solution.py:465
  16.3 1.3 %collective-permute-done.3.yhi_ref = bf16[32,1024]{1,0:T(8,128)(2,1)S(1)} collective-permute-done((bf16[32,1024]{1,0:T(8,128)(2,1)S(1)}, bf16[32,1024]{1,0:T(8,128)(2,1)S(1)}, u32[]{:S(2)}, u32[]{:S(2)}) %collective-permute-start.3) | collective-permute-done | bytes 65568 | tf_op jit(solution)/shard_map/ppermute | solution.py:465
  17.6 7.4 %integrate.4 = f32[8,2,64,128]{3,2,1,0:T(8,128)S(1)} custom-call(s32[1]{0:T(128)} %copy.25.flip_ref, f32[4,4]{1,0:T(4,128)S(1)} %copy-done.3, s32[32,64,1024]{2,1,0:T(8,128)S(1)} %copy-done, bf16[64,1024]{1,0:T(8,128)(2,1)S(1)} %collective-permute-done.zlo_ref, bf16[64,1024]{1,0:T(8,128)(2,1)S(1)} %collective-permute-done.1.zhi_ref, ...), custom_call_target="tpu_custom_call" | custom-call | flops 36700160 | bytes 4194304 | tf_op jit(solution)/shard_map/integrate/pallas_call | solution.py:231
  25.0 0.1 collective-permute-start.4
  25.1 3.4 %copy-done.1 = s32[32,64,1024]{2,1,0:T(8,128)S(1)} copy-done((s32[32,64,1024]{2,1,0:T(8,128)S(1)}, s32[32,64,1024]{2,1,0:T(8,128)}, u32[]{:S(2)}) %copy-start.1) | copy-done | bytes 8388632
  28.5 7.5 %integrate.6 = f32[8,2,64,128]{3,2,1,0:T(8,128)S(1)} custom-call(s32[1]{0:T(128)} %copy.25.flip_ref, f32[4,4]{1,0:T(4,128)S(1)} %copy-done.3, s32[32,64,1024]{2,1,0:T(8,128)S(1)} %copy-done.1, bf16[64,1024]{1,0:T(8,128)(2,1)S(1)} %collective-permute-done.zlo_ref, bf16[64,1024]{1,0:T(8,128)(2,1)S(1)} %collective-permute-done.1.zhi_ref, ...), custom_call_target="tpu_custom_call" | custom-call | flops 36700160 | bytes 4194304 | tf_op jit(solution)/shard_map/integrate/pallas_call | solution.py:231
  36.0 7.5 %integrate.5 = f32[8,2,64,128]{3,2,1,0:T(8,128)S(1)} custom-call(s32[1]{0:T(128)} %copy.25.flip_ref, f32[4,4]{1,0:T(4,128)S(1)} %copy-done.3, s32[32,64,1024]{2,1,0:T(8,128)S(1)} %copy-done.1, bf16[64,1024]{1,0:T(8,128)(2,1)S(1)} %collective-permute-done.zlo_ref, bf16[64,1024]{1,0:T(8,128)(2,1)S(1)} %collective-permute-done.1.zhi_ref, ...), custom_call_target="tpu_custom_call" | custom-call | flops 36700160 | bytes 4194304 | tf_op jit(solution)/shard_map/integrate/pallas_call | solution.py:231
  43.6 0.1 fusion.3
  43.7 0.4 collective-permute-start.5
  44.1 3.0 %collective-permute-start.6 = (f32[8,1,2,64,128]{4,3,0,2,1:T(8,128)S(1)}, f32[8,1,2,64,128]{4,3,0,2,1:T(8,128)S(1)}, u32[]{:S(2)}, u32[]{:S(2)}) collective-permute-start(f32[8,1,2,64,128]{4,3,0,2,1:T(8,128)S(1)} %fusion.3), channel_id=1, source_target_pairs={{0,16},{16,0},{8,24},{24,8},{1,17},{17,1},{9,25},{25,9},{2,18},{18... | collective-permute-start | bytes 1572872 | tf_op jit(solution)/shard_map/ppermute | solution.py:36
  47.0 3.4 %copy-done.2 = s32[32,64,1024]{2,1,0:T(8,128)S(1)} copy-done((s32[32,64,1024]{2,1,0:T(8,128)S(1)}, s32[32,64,1024]{2,1,0:T(8,128)}, u32[]{:S(2)}) %copy-start.2) | copy-done | bytes 8388632
  50.4 7.4 %integrate.7 = f32[8,2,64,128]{3,2,1,0:T(8,128)S(1)} custom-call(s32[1]{0:T(128)} %copy.25.flip_ref, f32[4,4]{1,0:T(4,128)S(1)} %copy-done.3, s32[32,64,1024]{2,1,0:T(8,128)S(1)} %copy-done.2, bf16[64,1024]{1,0:T(8,128)(2,1)S(1)} %collective-permute-done.zlo_ref, bf16[64,1024]{1,0:T(8,128)(2,1)S(1)} %collective-permute-done.1.zhi_ref, ...), custom_call_target="tpu_custom_call" | custom-call | flops 36700160 | bytes 4194304 | tf_op jit(solution)/shard_map/integrate/pallas_call | solution.py:231
  57.9 1.2 %collective-permute-done.6 = f32[8,1,2,64,128]{4,3,0,2,1:T(8,128)S(1)} collective-permute-done((f32[8,1,2,64,128]{4,3,0,2,1:T(8,128)S(1)}, f32[8,1,2,64,128]{4,3,0,2,1:T(8,128)S(1)}, u32[]{:S(2)}, u32[]{:S(2)}) %collective-permute-start.6) | collective-permute-done | bytes 524320 | tf_op jit(solution)/shard_map/ppermute | solution.py:36
  59.1 0.1 broadcast_select_fusion
  59.3 0.2 add_bitcast_fusion
  59.5 0.1 slice_bitcast_fusion
  59.6 4.0 %collective-permute-start.7 = (f32[8,64,8]{2,1,0:T(8,128)S(1)}, f32[8,64,8]{2,1,0:T(8,128)S(1)}, u32[]{:S(2)}, u32[]{:S(2)}) collective-permute-start(f32[8,64,8]{2,1,0:T(8,128)S(1)} %get-tuple-element.30), channel_id=1, source_target_pairs={{0,8},{8,16},{16,24},{1,9},{9,17},{17,25},{2,10},{10,18},{18,26},{... | collective-permute-start | bytes 49160 | tf_op jit(solution)/shard_map/ppermute | solution.py:501
  63.7 1.9 %collective-permute-start.8 = (f32[8,64,8]{2,1,0:T(8,128)S(1)}, f32[8,64,8]{2,1,0:T(8,128)S(1)}, u32[]{:S(2)}, u32[]{:S(2)}) collective-permute-start(f32[8,64,8]{2,1,0:T(8,128)S(1)} %get-tuple-element.29), channel_id=1, source_target_pairs={{8,0},{16,8},{24,16},{9,1},{17,9},{25,17},{10,2},{18,10},{26,18},{... | collective-permute-start | bytes 49160 | tf_op jit(solution)/shard_map/ppermute | solution.py:502
  65.6 1.3 %collective-permute-done.7.left_ref = f32[8,64,8]{2,1,0:T(8,128)S(1)} collective-permute-done((f32[8,64,8]{2,1,0:T(8,128)S(1)}, f32[8,64,8]{2,1,0:T(8,128)S(1)}, u32[]{:S(2)}, u32[]{:S(2)}) %collective-permute-start.7) | collective-permute-done | bytes 16416 | tf_op jit(solution)/shard_map/ppermute | solution.py:501
  66.9 4.4 %collective-permute-done.8.right_ref = f32[8,64,8]{2,1,0:T(8,128)S(1)} collective-permute-done((f32[8,64,8]{2,1,0:T(8,128)S(1)}, f32[8,64,8]{2,1,0:T(8,128)S(1)}, u32[]{:S(2)}, u32[]{:S(2)}) %collective-permute-start.8) | collective-permute-done | bytes 16416 | tf_op jit(solution)/shard_map/ppermute | solution.py:502
  71.4 0.1 pad_maximum_fusion.1
  71.5 4.0 %collective-permute-start.10 = (f32[8,8,272]{2,1,0:T(8,128)S(1)}, f32[8,8,272]{2,1,0:T(8,128)S(1)}, u32[]{:S(2)}, u32[]{:S(2)}) collective-permute-start(f32[8,8,272]{2,1,0:T(8,128)S(1)} %pad_maximum_fusion.1), channel_id=1, source_target_pairs={{1,0},{2,1},{3,2},{4,3},{5,4},{6,5},{7,6},{9,8},{10,9},{11,10},{12... | collective-permute-start | bytes 208904 | tf_op jit(solution)/shard_map/ppermute | solution.py:512
  75.4 0.1 pad_maximum_fusion
  75.6 2.2 %collective-permute-start.9 = (f32[8,8,272]{2,1,0:T(8,128)S(1)}, f32[8,8,272]{2,1,0:T(8,128)S(1)}, u32[]{:S(2)}, u32[]{:S(2)}) collective-permute-start(f32[8,8,272]{2,1,0:T(8,128)S(1)} %pad_maximum_fusion), channel_id=1, source_target_pairs={{0,1},{1,2},{2,3},{3,4},{4,5},{5,6},{6,7},{8,9},{9,10},{10,11},{11... | collective-permute-start | bytes 208904 | tf_op jit(solution)/shard_map/ppermute | solution.py:511
  77.8 0.8 collective-permute-done.10.bottom_ref
  78.6 3.2 %collective-permute-done.9.top_ref = f32[8,8,272]{2,1,0:T(8,128)S(1)} collective-permute-done((f32[8,8,272]{2,1,0:T(8,128)S(1)}, f32[8,8,272]{2,1,0:T(8,128)S(1)}, u32[]{:S(2)}, u32[]{:S(2)}) %collective-permute-start.9) | collective-permute-done | bytes 69664 | tf_op jit(solution)/shard_map/ppermute | solution.py:511
  81.8 21.6 %shade.1 = f32[3,64,256]{2,1,0:T(8,128)} custom-call(f32[8,2,64,128]{3,2,1,0:T(8,128)S(1)} %copy.8.core_ref, f32[8,64,8]{2,1,0:T(8,128)S(1)} %collective-permute-done.7.left_ref, f32[8,64,8]{2,1,0:T(8,128)S(1)} %collective-permute-done.8.right_ref, f32[8,8,272]{2,1,0:T(8,128)S(1)} %collective-permute-done.9.top_ref, ...), custom_call_target="tpu_custom_call" | custom-call | tf_op jit(solution)/shard_map/shade/pallas_call | solution.py:422
  (21 shorter events, 0.3 us)
Async XLA Ops:
  0.0 3.4 %copy-start = (s32[32,64,1024]{2,1,0:T(8,128)S(1)}, s32[32,64,1024]{2,1,0:T(8,128)}, u32[]{:S(2)}) copy-start(s32[32,64,1024]{2,1,0:T(8,128)} %density_ref.9) | copy-start | bytes 25165828
  3.4 14.2 %copy-start.3 = (f32[4,4]{1,0:T(4,128)S(1)}, f32[4,4]{1,0:T(4,128)}, u32[]{:S(2)}) copy-start(f32[4,4]{1,0:T(4,128)} %coeff_ref.7) | copy-start | bytes 196
  3.8 13.8 %collective-permute-start = (bf16[64,1024]{1,0:T(8,128)(2,1)S(1)}, bf16[64,1024]{1,0:T(8,128)(2,1)S(1)}, u32[]{:S(2)}, u32[]{:S(2)}) collective-permute-start(bf16[64,1024]{1,0:T(8,128)(2,1)S(1)} %get-tuple-element.15), channel_id=1, source_target_pairs={{0,8},{8,16},{16,24},{1,9},{9,17},{17,25},{2,10},{10,18},{18,26},{... | collective-permute-start | bytes 393224 | tf_op jit(solution)/shard_map/ppermute | solution.py:461
  7.5 10.1 %collective-permute-start.1 = (bf16[64,1024]{1,0:T(8,128)(2,1)S(1)}, bf16[64,1024]{1,0:T(8,128)(2,1)S(1)}, u32[]{:S(2)}, u32[]{:S(2)}) collective-permute-start(bf16[64,1024]{1,0:T(8,128)(2,1)S(1)} %get-tuple-element.16), channel_id=1, source_target_pairs={{8,0},{16,8},{24,16},{9,1},{17,9},{25,17},{10,2},{18,10},{26,18},{... | collective-permute-start | bytes 393224 | tf_op jit(solution)/shard_map/ppermute | solution.py:462
  9.5 6.8 %collective-permute-start.2 = (bf16[32,1024]{1,0:T(8,128)(2,1)S(1)}, bf16[32,1024]{1,0:T(8,128)(2,1)S(1)}, u32[]{:S(2)}, u32[]{:S(2)}) collective-permute-start(bf16[32,1024]{1,0:T(8,128)(2,1)S(1)} %get-tuple-element.17), channel_id=1, source_target_pairs={{0,1},{1,2},{2,3},{3,4},{4,5},{5,6},{6,7},{8,9},{9,10},{10,11},{11... | collective-permute-start | bytes 196616 | tf_op jit(solution)/shard_map/ppermute | solution.py:464
  12.6 5.0 %collective-permute-start.3 = (bf16[32,1024]{1,0:T(8,128)(2,1)S(1)}, bf16[32,1024]{1,0:T(8,128)(2,1)S(1)}, u32[]{:S(2)}, u32[]{:S(2)}) collective-permute-start(bf16[32,1024]{1,0:T(8,128)(2,1)S(1)} %get-tuple-element.18), channel_id=1, source_target_pairs={{1,0},{2,1},{3,2},{4,3},{5,4},{6,5},{7,6},{9,8},{10,9},{11,10},{12... | collective-permute-start | bytes 196616 | tf_op jit(solution)/shard_map/ppermute | solution.py:465
  25.0 18.5 %collective-permute-start.4 = (f32[8,1,2,64,128]{4,3,0,2,1:T(8,128)S(1)}, f32[8,1,2,64,128]{4,3,0,2,1:T(8,128)S(1)}, u32[]{:S(2)}, u32[]{:S(2)}) collective-permute-start(f32[8,1,2,64,128]{4,3,0,2,1:T(8,128)S(1)} %bitcast.52), channel_id=1, source_target_pairs={{0,8},{8,0},{16,24},{24,16},{1,9},{9,1},{17,25},{25,17},{2,10},{10... | collective-permute-start | bytes 1572872 | tf_op jit(solution)/shard_map/ppermute | solution.py:36
  25.1 3.4 %copy-start.1 = (s32[32,64,1024]{2,1,0:T(8,128)S(1)}, s32[32,64,1024]{2,1,0:T(8,128)}, u32[]{:S(2)}) copy-start(s32[32,64,1024]{2,1,0:T(8,128)} %density_ref.9) | copy-start | bytes 25165828
  43.7 14.1 %collective-permute-start.5 = (f32[8,1,2,64,128]{4,3,0,2,1:T(8,128)S(1)}, f32[8,1,2,64,128]{4,3,0,2,1:T(8,128)S(1)}, u32[]{:S(2)}, u32[]{:S(2)}) collective-permute-start(f32[8,1,2,64,128]{4,3,0,2,1:T(8,128)S(1)} %bitcast.51), channel_id=1, source_target_pairs={{0,8},{8,0},{16,24},{24,16},{1,9},{9,1},{17,25},{25,17},{2,10},{10... | collective-permute-start | bytes 1572872 | tf_op jit(solution)/shard_map/ppermute | solution.py:36
  44.1 15.1 %collective-permute-start.6 = (f32[8,1,2,64,128]{4,3,0,2,1:T(8,128)S(1)}, f32[8,1,2,64,128]{4,3,0,2,1:T(8,128)S(1)}, u32[]{:S(2)}, u32[]{:S(2)}) collective-permute-start(f32[8,1,2,64,128]{4,3,0,2,1:T(8,128)S(1)} %fusion.3), channel_id=1, source_target_pairs={{0,16},{16,0},{8,24},{24,8},{1,17},{17,1},{9,25},{25,9},{2,18},{18... | collective-permute-start | bytes 1572872 | tf_op jit(solution)/shard_map/ppermute | solution.py:36
  47.0 3.4 %copy-start.2 = (s32[32,64,1024]{2,1,0:T(8,128)S(1)}, s32[32,64,1024]{2,1,0:T(8,128)}, u32[]{:S(2)}) copy-start(s32[32,64,1024]{2,1,0:T(8,128)} %density_ref.9) | copy-start | bytes 25165828
  59.6 7.3 %collective-permute-start.7 = (f32[8,64,8]{2,1,0:T(8,128)S(1)}, f32[8,64,8]{2,1,0:T(8,128)S(1)}, u32[]{:S(2)}, u32[]{:S(2)}) collective-permute-start(f32[8,64,8]{2,1,0:T(8,128)S(1)} %get-tuple-element.30), channel_id=1, source_target_pairs={{0,8},{8,16},{16,24},{1,9},{9,17},{17,25},{2,10},{10,18},{18,26},{... | collective-permute-start | bytes 49160 | tf_op jit(solution)/shard_map/ppermute | solution.py:501
  63.7 7.7 %collective-permute-start.8 = (f32[8,64,8]{2,1,0:T(8,128)S(1)}, f32[8,64,8]{2,1,0:T(8,128)S(1)}, u32[]{:S(2)}, u32[]{:S(2)}) collective-permute-start(f32[8,64,8]{2,1,0:T(8,128)S(1)} %get-tuple-element.29), channel_id=1, source_target_pairs={{8,0},{16,8},{24,16},{9,1},{17,9},{25,17},{10,2},{18,10},{26,18},{... | collective-permute-start | bytes 49160 | tf_op jit(solution)/shard_map/ppermute | solution.py:502
  71.5 7.2 %collective-permute-start.10 = (f32[8,8,272]{2,1,0:T(8,128)S(1)}, f32[8,8,272]{2,1,0:T(8,128)S(1)}, u32[]{:S(2)}, u32[]{:S(2)}) collective-permute-start(f32[8,8,272]{2,1,0:T(8,128)S(1)} %pad_maximum_fusion.1), channel_id=1, source_target_pairs={{1,0},{2,1},{3,2},{4,3},{5,4},{6,5},{7,6},{9,8},{10,9},{11,10},{12... | collective-permute-start | bytes 208904 | tf_op jit(solution)/shard_map/ppermute | solution.py:512
  75.6 6.3 %collective-permute-start.9 = (f32[8,8,272]{2,1,0:T(8,128)S(1)}, f32[8,8,272]{2,1,0:T(8,128)S(1)}, u32[]{:S(2)}, u32[]{:S(2)}) collective-permute-start(f32[8,8,272]{2,1,0:T(8,128)S(1)} %pad_maximum_fusion), channel_id=1, source_target_pairs={{0,1},{1,2},{2,3},{3,4},{4,5},{5,6},{6,7},{8,9},{9,10},{10,11},{11... | collective-permute-start | bytes 208904 | tf_op jit(solution)/shard_map/ppermute | solution.py:511

commit v3 on v2

v3 whole, which is shorter than its diff:
```python
import functools
import math

import jax
import jax.numpy as jnp
from jax import lax
from jax.experimental import pallas as pl
from jax.experimental.pallas import tpu as pltpu
from jax.sharding import PartitionSpec as P

RADIUS = 8
LANES = 128
SUB = 8
LOG2E = math.log2(math.e)
OPACITY = 0.008
LIGHT = (0.48, 0.6, 0.64)
SPATIAL = 1.0 / 72.0
DEPTH_W = 20.0
NORMAL_W = 2.0
CENTRE = 127.5
AHEAD = 8


def shifts(axis):
    count = lax.axis_size(axis)
    up = [(i, i + 1) for i in range(count - 1)]
    return up, [(j, i) for i, j in up]


def swapped(block, axis, stride):
    count = lax.axis_size(axis)
    route = []
    for low in range(count):
        high = low | 1 << stride
        if high != low and high < count:
            route += [(low, high), (high, low)]
    return lax.ppermute(block, axis, route)


def edges_kernel(density_ref, zlo_ref, zhi_ref, ylo_ref, yhi_ref, planes, bands, lines, sems):
    cells, rows, width = density_ref.shape
    tiles = width // LANES
    copies = []
    for side in range(2):
        copies.append(
            pltpu.make_async_copy(
                density_ref.at[side * (cells - 1)], planes.at[side], sems.at[2 * side]
            )
        )
        copies.append(
            pltpu.make_async_copy(
                density_ref.at[:, side * (rows - SUB) : side * (rows - SUB) + SUB, :],
                bands.at[side],
                sems.at[2 * side + 1],
            )
        )
    for copy in copies:
        copy.start()
    for copy in copies:
        copy.wait()
    zlo_ref[...] = planes[0].astype(jnp.float32).astype(jnp.bfloat16)
    zhi_ref[...] = planes[1].astype(jnp.float32).astype(jnp.bfloat16)
    for side, ref in ((0, ylo_ref), (1, yhi_ref)):
        row = side * (SUB - 1)
        for z in range(cells):
            lines[z : z + 1, :] = bands[side, z, row : row + 1, :].astype(jnp.float32)
        ref[...] = lines[...].astype(jnp.bfloat16)


def edges(density):
    cells, rows, width = density.shape
    vmem = pl.BlockSpec(memory_space=pltpu.VMEM)
    plane = jax.ShapeDtypeStruct((rows, width), jnp.bfloat16)
    line = jax.ShapeDtypeStruct((cells, width), jnp.bfloat16)
    return pl.pallas_call(
        edges_kernel,
        out_shape=(plane, plane, line, line),
        in_specs=[pl.BlockSpec(memory_space=pl.ANY)],
        out_specs=[vmem] * 4,
        scratch_shapes=[
            pltpu.VMEM((2, rows, width), jnp.int32),
            pltpu.VMEM((2, cells, SUB, width), jnp.int32),
            pltpu.VMEM((cells, width), jnp.float32),
            pltpu.SemaphoreType.DMA((4,)),
        ],
        compiler_params=pltpu.CompilerParams(vmem_limit_bytes=52 << 20),
        name="edges",
    )(density)


def integrate_kernel(
    place, own, flip_ref, coeff_ref, density_ref, zlo_ref, zhi_ref, ylo_ref, yhi_ref, token_ref,
    out_ref, field, zlo_f, zhi_f, sems,
):
    cells, rows, width = density_ref.shape
    tiles = width // LANES
    blocks = rows // SUB
    count = tiles // own
    position = lax.axis_index("depth")
    c, y = position % 2, position // 2 % 2
    first = (lax.rem(c + place[0], 2) + 2 * lax.rem(y + place[1], 2) + 4 * place[2]) * own
    sources = [jnp.maximum(first - 1, 0)]
    sources += [first + j for j in range(own)]
    sources += [jnp.minimum(first + own, tiles - 1)]

    def copy(b, j):
        start = pl.multiple_of(sources[j] * LANES, LANES)
        return pltpu.make_async_copy(
            density_ref.at[:, pl.ds(b * SUB, SUB), pl.ds(start, LANES)],
            field.at[:, j, pl.ds(SUB + b * SUB, SUB), :],
            sems.at[b, j],
        )

    for b in range(blocks):
        for j in range(own + 2):
            copy(b, j).start()
    flip = flip_ref[0]
    for j in range(own):
        cols = pl.ds(pl.multiple_of((first + j) * LANES, LANES), LANES)
        zlo_f[j] = zlo_ref[:, cols].astype(jnp.float32) - CENTRE
        zhi_f[j] = zhi_ref[:, cols].astype(jnp.float32) - CENTRE
        top = ylo_ref[:, cols].astype(jnp.float32).astype(jnp.int32)
        bottom = yhi_ref[:, cols].astype(jnp.float32).astype(jnp.int32)
        for z in range(cells):
            field[z, j + 1, SUB - 1 : SUB, :] = top[z : z + 1]
            field[z, j + 1, SUB + rows : SUB + rows + 1, :] = bottom[z : z + 1]

    coeffs = []
    for row in range(4):
        scale = LOG2E if row == 0 else -LOG2E
        coeffs.append([coeff_ref[row, k] * (scale / CENTRE**k) for k in range(4)])
    sign = jnp.where(flip == 1, 1.0, -1.0)
    rate = sign * OPACITY
    lx, ly, lz = (0.65 * v for v in LIGHT)
    lane = lax.broadcasted_iota(jnp.int32, (SUB, LANES), 1)
    first_lane = lane == 0
    last_lane = lane == LANES - 1
    base = (position * cells).astype(jnp.float32)
    step = 1.0 / (cells * count)
    start = (base + 0.5) * step
    finish = (base + (cells - 0.5)) * step
    h_first = jnp.where(flip == 1, 1.0 - start, start)
    h_last = jnp.where(flip == 1, 1.0 - finish, finish)
    delta = jnp.where(flip == 1, -step, step)

    def poly(c, t):
        return c[0] + t * (c[1] + t * (c[2] + t * c[3]))

    def arrive(b):
        for j in range(own + 2):
            copy(b, j).wait()
        at = pl.ds(SUB + b * SUB, SUB)

        @pl.when(first == 0)
        def _():
            for z in range(cells):
                field[z, 0, at, :] = jnp.zeros((SUB, LANES), jnp.int32)

        @pl.when(first + own == tiles)
        def _():
            for z in range(cells):
                field[z, own + 1, at, :] = jnp.zeros((SUB, LANES), jnp.int32)

    arrive(0)

    def block(b, carry):
        @pl.when(b + 1 < blocks)
        def _():
            arrive(b + 1)

        r = pl.multiple_of(b * SUB, SUB)
        for j in range(1, own + 1):
            column(r, j)
        return carry

    def column(r, j):
        at = pl.ds(r + SUB, SUB)
        zero = jnp.zeros((SUB, LANES), jnp.float32)
        tau = zero
        factor = jnp.ones((SUB, LANES), jnp.float32)
        between = zero
        sums = [zero] * 6
        below = zlo_f[j - 1, pl.ds(r, SUB), :]
        raw = field[0, j, at, :]
        here = raw.astype(jnp.float32) - CENTRE
        for z in range(cells):
            if z + 1 < cells:
                raw_above = field[z + 1, j, at, :]
                above = raw_above.astype(jnp.float32) - CENTRE
            else:
                raw_above = raw
                above = zhi_f[j - 1, pl.ds(r, SUB), :]
            left = pltpu.roll(jnp.where(last_lane, field[z, j - 1, at, :], raw), 1, 1)
            right = pltpu.roll(jnp.where(first_lane, field[z, j + 1, at, :], raw), LANES - 1, 1)
            gx = (right - left).astype(jnp.float32)
            up = field[z, j, pl.ds(r + SUB + 1, SUB), :]
            gy = (up - field[z, j, pl.ds(r + SUB - 1, SUB), :]).astype(jnp.float32)
            gz = above - below
            norm = lax.rsqrt(gx * gx + gy * gy + (gz * gz + 255.0 * 255.0))
            shade = 0.35 + jnp.abs((lx * gx + ly * gy + lz * gz) * norm)
            tau = tau + jnp.log2(1.0 + jnp.exp2(poly(coeffs[0], here)))
            following = jnp.exp2(rate * tau)
            weight = following - factor
            factor = following
            if z < cells - 1:
                between = between + following
            tilt = weight * norm
            lit = weight * shade
            terms = [lit * (1.0 / (1.0 + jnp.exp2(poly(coeffs[k], here)))) for k in (1, 2, 3)]
            terms += [tilt * gx, tilt * gy, tilt * gz]
            sums = [s + t for s, t in zip(sums, terms)]
            below, here, raw = here, above, raw_above
        inverse = 1.0 / factor
        flipped = flip == 1
        scale = jnp.where(flipped, inverse, -1.0)
        out = pl.ds(r, SUB)
        for k in range(3):
            out_ref[k, j - 1, out, :] = sums[k] * scale
            out_ref[k + 5, j - 1, out, :] = sums[k + 3] * scale
        out_ref[3, j - 1, out, :] = 1.0 - jnp.where(flipped, inverse, factor)
        out_ref[4, j - 1, out, :] = (h_last * factor - h_first - delta * between) * scale

    lax.fori_loop(0, blocks, block, 0)


def integrate(place, count, view_flip, tf_coeff, density, zlo, zhi, ylo, yhi, token):
    cells, rows, width = density.shape
    own = width // LANES // count
    smem = pl.BlockSpec(memory_space=pltpu.SMEM)
    vmem = pl.BlockSpec(memory_space=pltpu.VMEM)
    anywhere = pl.BlockSpec(memory_space=pl.ANY)
    voxels = cells * rows * own * LANES
    return pl.pallas_call(
        functools.partial(integrate_kernel, place, own),
        out_shape=jax.ShapeDtypeStruct((8, own, rows, LANES), jnp.float32),
        in_specs=[smem, smem, anywhere, vmem, vmem, vmem, vmem, anywhere],
        out_specs=vmem,
        scratch_shapes=[
            pltpu.VMEM((cells, own + 2, rows + 2 * SUB, LANES), jnp.int32),
            pltpu.VMEM((own, rows, LANES), jnp.float32),
            pltpu.VMEM((own, rows, LANES), jnp.float32),
            pltpu.SemaphoreType.DMA((rows // SUB, own + 2)),
        ],
        compiler_params=pltpu.CompilerParams(vmem_limit_bytes=52 << 20),
        cost_estimate=pl.CostEstimate(
            flops=70 * voxels, transcendentals=0, bytes_accessed=8 * voxels
        ),
        name="integrate",
    )(view_flip, tf_coeff, density, zlo, zhi, ylo, yhi, token)


def shade_kernel(inner, core_ref, halo_ref, *rest):
    if inner:
        out_ref, planes, feats, buf_a, buf_b, acc = rest
    else:
        top_ref, bottom_ref, done_ref, out_ref, planes, feats, buf_a, buf_b, acc = rest
    _, tiles, rows, _ = core_ref.shape
    blocks = rows // SUB
    chosen = list(range(1, blocks - 1)) if inner else [0, blocks - 1]
    needed = sorted({n for b in chosen for n in (b - 1, b, b + 1)})

    def at(n):
        return pl.ds(SUB + n * SUB, SUB)

    for k in range(8):
        for n in needed:
            for t in (0, tiles + 1):
                planes[k, t, at(n), :] = jnp.zeros((SUB, LANES), jnp.float32)
            if 0 <= n < blocks:
                here = slice(n * SUB, n * SUB + SUB)
                side = halo_ref[here, :]
                for j in range(tiles):
                    planes[k, j + 1, at(n), :] = core_ref[k, j, here, :]
            else:
                ref = top_ref if n < 0 else bottom_ref
                side = ref[8 * tiles]
                for j in range(tiles):
                    planes[k, j + 1, at(n), :] = ref[k * tiles + j]
            left = side[:, RADIUS * k : RADIUS * k + RADIUS]
            right = side[:, RADIUS * (8 + k) : RADIUS * (9 + k)]
            planes[k, 0, at(n), LANES - RADIUS : LANES] = left
            planes[k, tiles + 1, at(n), 0:RADIUS] = right

    def features(t, carry):
        for n in needed:
            red, green, blue, alpha, depth, nx, ny, nz = [planes[k, t, at(n), :] for k in range(8)]
            facing = jnp.maximum(LIGHT[0] * nx + LIGHT[1] * ny + LIGHT[2] * nz, 0.0)
            lit = 0.4 + 0.6 * facing
            level = (DEPTH_W * LOG2E) * depth * depth
            level = level + (NORMAL_W * LOG2E) * (nx * nx + ny * ny + nz * nz)
            feats[0, t, at(n), :] = jnp.log2(jnp.maximum(alpha, 1e-37)) - level
            feats[1, t, at(n), :] = depth
            feats[2, t, at(n), :] = nx
            feats[3, t, at(n), :] = ny
            feats[4, t, at(n), :] = nz
            feats[5, t, at(n), :] = red * lit
            feats[6, t, at(n), :] = green * lit
            feats[7, t, at(n), :] = blue * lit
        return carry

    lax.fori_loop(0, tiles + 2, features, 0)
    lane = lax.broadcasted_iota(jnp.int32, (SUB, LANES), 1)

    def shift_setup(index):
        offset = index - RADIUS
        run = offset.astype(jnp.float32)
        spread = -(SPATIAL * LOG2E) * run * run
        border = jnp.where(offset < 0, LANES + offset, offset)
        amount = jnp.where(offset > 0, LANES - offset, -offset)
        below = lane < border
        take_other = (below & (offset >= 0)) | (jnp.logical_not(below) & (offset < 0))
        return jnp.where(offset < 0, 0, 2), amount, take_other, spread

    def moved(setup, k, j, n):
        other, amount, take_other, spread = setup
        mixed = jnp.where(take_other, feats[k, j + other, at(n), :], feats[k, j + 1, at(n), :])
        result = pltpu.roll(mixed, amount, 1)
        return result + spread if k == 0 else result

    def first_shift(k, carry):
        other, amount, take_other, spread = shift_setup(jnp.int32(0))
        for j in range(tiles):
            for n in needed:
                mixed = jnp.where(take_other, feats[k, j + other, at(n), :], feats[k, j + 1, at(n), :])
                result = pltpu.roll(mixed, amount, 1)
                buf_a[k, j, at(n), :] = result + jnp.where(k == 0, spread, 0.0)
        return carry

    lax.fori_loop(0, 8, first_shift, 0)
    for k in range(4):
        for j in range(tiles):
            for b in chosen:
                acc[k, j, at(b), :] = jnp.zeros((SUB, LANES), jnp.float32)

    offsets = sorted({o for b in chosen for o in range(SUB * b - RADIUS, SUB * b + RADIUS + 1)})

    def taps(buf, next_index, next_buf):
        pending, items = [], []
        if next_buf is not None:
            setup = shift_setup(next_index)
            items = [(k, j, n) for j in range(tiles) for n in needed for k in range(8)]
        pace = -(-len(items) // (len(offsets) * tiles))

        def pump(last=False):
            for _ in range(pace):
                if items:
                    pending.append((moved(setup, *items[0]),) + items.pop(0))
            while len(pending) > (0 if last else AHEAD):
                value, k, j, n = pending.pop(0)
                next_buf[k, j, at(n), :] = value

        for j in range(tiles):
            own, sums = {}, {}
            for o in offsets:
                pump()
                q = [buf[k, j, pl.ds(SUB + o, SUB), :] for k in range(8)]
                for b in chosen:
                    dy = o - SUB * b
                    if abs(dy) > RADIUS:
                        continue
                    if dy == -RADIUS:
                        own[b] = [feats[1, j + 1, at(b), :] * (2.0 * DEPTH_W * LOG2E)]
                        own[b] += [
                            feats[k, j + 1, at(b), :] * (2.0 * NORMAL_W * LOG2E) for k in (2, 3, 4)
                        ]
                        sums[b] = [acc[k, j, at(b), :] for k in range(4)]
                    p, s = own[b], sums[b]
                    power = (q[0] + p[0] * q[1]) + (p[1] * q[2] + p[2] * q[3])
                    power = power + (p[3] * q[4] - SPATIAL * LOG2E * dy * dy)
                    weight = jnp.exp2(power)
                    sums[b] = [s[k] + weight * q[5 + k] for k in range(3)] + [s[3] + weight]
                    if dy == RADIUS:
                        for k in range(4):
                            acc[k, j, at(b), :] = sums[b][k]
        while items or pending:
            pump(not items)

    def pair(step, carry):
        taps(buf_a, 2 * step + 1, buf_b)
        taps(buf_b, 2 * step + 2, buf_a)
        return carry

    lax.fori_loop(0, RADIUS, pair, 0)
    taps(buf_a, None, None)

    if not inner:
        for k in range(3):
            out_ref[k, SUB : rows - SUB, :] = done_ref[k, SUB : rows - SUB, :]
    for j in range(tiles):
        for b in chosen:
            depth, nx, ny, nz = [feats[k, j + 1, at(b), :] for k in (1, 2, 3, 4)]
            own = (DEPTH_W * LOG2E) * depth * depth
            own = own + (NORMAL_W * LOG2E) * (nx * nx + ny * ny + nz * nz)
            level = jnp.exp2(-own)
            scale = level / (1.0 + level * acc[3, j, at(b), :])
            for k in range(3):
                out_ref[k, b * SUB : b * SUB + SUB, j * LANES : (j + 1) * LANES] = (
                    acc[k, j, at(b), :] * scale
                )


def shade(inner, core, *rest):
    _, tiles, rows, _ = core.shape
    vmem = pl.BlockSpec(memory_space=pltpu.VMEM)
    wide = (8, tiles + 2, rows + 2 * SUB, LANES)
    moved = (8, tiles, rows + 2 * SUB, LANES)
    part = rows - 2 * SUB if inner else 2 * SUB
    work = part * tiles * LANES * (2 * RADIUS + 1) ** 2
    return pl.pallas_call(
        functools.partial(shade_kernel, inner),
        out_shape=jax.ShapeDtypeStruct((3, rows, tiles * LANES), jnp.float32),
        in_specs=[vmem] * (1 + len(rest)),
        out_specs=vmem,
        scratch_shapes=[
            pltpu.VMEM(wide, jnp.float32),
            pltpu.VMEM(wide, jnp.float32),
            pltpu.VMEM(moved, jnp.float32),
            pltpu.VMEM(moved, jnp.float32),
            pltpu.VMEM((4, tiles, rows + 2 * SUB, LANES), jnp.float32),
        ],
        compiler_params=pltpu.CompilerParams(vmem_limit_bytes=24 << 20),
        cost_estimate=pl.CostEstimate(
            flops=16 * work, transcendentals=work, bytes_accessed=8 * rows * tiles * LANES * 4
        ),
        name="shade_inner" if inner else "shade_outer",
    )(core, *rest)


def compose_kernel(base, pieces, mode, leads_ref, *refs):
    images, at_ref = [], 0
    for n in pieces:
        images.append(refs[at_ref : at_ref + n])
        at_ref += n
    outs = refs[at_ref:]
    _, tiles, rows, _ = outs[0].shape
    halves = outs if mode == "halves" else outs[:1]

    def plane(parts, k):
        size = 8 // len(parts)
        return parts[k // size], k % size

    def one(t, carry):
        j = t // (rows // SUB)
        at = pl.ds(pl.multiple_of(t % (rows // SUB) * SUB, SUB), SUB)

        def read(parts):
            found = [plane(parts, k) for k in range(8)]
            return [ref[k, j, at, :] for ref, k in found]

        current = read(images[0])
        for level, parts in enumerate(images[1:]):
            other = read(parts)
            leads = leads_ref[base + level] == 1
            share = jnp.where(leads, 1.0, 1.0 - other[3])
            other_share = jnp.where(leads, 1.0 - current[3], 1.0)
            current = [c * share + o * other_share for c, o in zip(current, other)]
        for k in range(8):
            ref, kk = plane(halves, k)
            ref[kk, j, at, :] = current[k]
        return carry

    lax.fori_loop(0, tiles * (rows // SUB), one, 0)
    if mode == "borders":
        out_ref, last_ref, first_ref = outs
        last_ref[...] = jnp.zeros((rows, LANES), jnp.float32)
        first_ref[...] = jnp.zeros((rows, LANES), jnp.float32)
        for k in range(8):
            last_ref[:, RADIUS * k : RADIUS * k + RADIUS] = out_ref[
                k, tiles - 1, :, LANES - RADIUS : LANES
            ]
            first_ref[:, RADIUS * (8 + k) : RADIUS * (9 + k)] = out_ref[k, 0, :, 0:RADIUS]


def compose(base, mode, leads, *images):
    images = [i if isinstance(i, (tuple, list)) else (i,) for i in images]
    _, tiles, rows, _ = images[0][0].shape
    smem = pl.BlockSpec(memory_space=pltpu.SMEM)
    vmem = pl.BlockSpec(memory_space=pltpu.VMEM)
    whole = jax.ShapeDtypeStruct((8, tiles, rows, LANES), jnp.float32)
    half = jax.ShapeDtypeStruct((4, tiles, rows, LANES), jnp.float32)
    border = jax.ShapeDtypeStruct((rows, LANES), jnp.float32)
    outs = {"plain": (whole,), "halves": (half, half), "borders": (whole, border, border)}[mode]
    parts = [p for image in images for p in image]
    return pl.pallas_call(
        functools.partial(compose_kernel, base, [len(i) for i in images], mode),
        out_shape=outs,
        in_specs=[smem] + [vmem] * len(parts),
        out_specs=[vmem] * len(outs),
        compiler_params=pltpu.CompilerParams(vmem_limit_bytes=8 << 20),
        cost_estimate=pl.CostEstimate(
            flops=0, transcendentals=0, bytes_accessed=32 * tiles * rows * LANES
        ),
        name="compose",
    )(leads, *parts)


def reverse_bits(value, rounds):
    result = 0
    for level in range(rounds):
        result = result * 2 + (value >> level) % 2
    return result


def per_device(density, view_flip, tf_coeff):
    cells, rows, width = density.shape
    count = lax.axis_size("depth")
    position = lax.axis_index("depth")
    flipped = view_flip[0]
    rounds = count.bit_length() - 1
    high = count // 4
    first_plane, last_plane, first_line, last_line = edges(density)
    up, down = shifts("depth")
    zlo = lax.ppermute(last_plane, "depth", up)
    zhi = lax.ppermute(first_plane, "depth", down)
    up, down = shifts("tile")
    ylo = lax.ppermute(last_line, "tile", up)
    yhi = lax.ppermute(first_line, "tile", down)

    def quarter(core_bit, chip_bit, token):
        parts = [
            integrate(
                (core_bit, chip_bit, h), count, view_flip, tf_coeff, density, zlo, zhi, ylo, yhi, token
            )
            for h in range(high)
        ]
        return parts[0] if high == 1 else jnp.concatenate(parts, axis=1)

    bits = [position // 2**level % 2 for level in range(rounds)]
    leads = jnp.stack([bit == flipped for bit in bits]).astype(jnp.int32)
    far_given = quarter(1, 1, zlo)
    far_partner = swapped(far_given, "depth", 0)
    far_kept = quarter(0, 1, far_given)
    far = compose(0, "halves", leads, far_kept, far_partner)
    chip_partner = [swapped(far[0], "depth", 1)]
    near_given = quarter(1, 0, far[0])
    near_partner = swapped(near_given, "depth", 0)
    token, behind = lax.optimization_barrier((chip_partner[0], far[1]))
    chip_partner.append(swapped(behind, "depth", 1))
    near_kept = quarter(0, 0, token)
    images, base = [near_kept, near_partner, chip_partner], 0
    own = width // LANES // count
    if high > 1:
        current = compose(0, "plain", leads, *images)[0]
        order = [reverse_bits(place, rounds - 2) for place in range(high)]
        current = jnp.concatenate([current[:, p * own : (p + 1) * own] for p in order], axis=1)
        for level in range(2, rounds):
            half = current.shape[1] // 2
            kept = lax.dynamic_slice_in_dim(current, bits[level] * half, half, 1)
            given = lax.dynamic_slice_in_dim(current, (1 - bits[level]) * half, half, 1)
            partner = swapped(given, "depth", level)
            images, base = [kept, partner], level
            if level < rounds - 1:
                current = compose(level, "plain", leads, kept, partner)[0]
    core, last, first = compose(base, "borders", leads, *images)
    up, down = shifts("depth")
    halo = lax.ppermute(last, "depth", up) + lax.ppermute(first, "depth", down)
    inner = shade(True, core, halo)
    up, down = shifts("tile")

    def band(start):
        rows_at = slice(start, start + SUB)
        image = core[:, :, rows_at].reshape(8 * own, SUB, LANES)
        return jnp.concatenate([image, halo[None, rows_at]], axis=0)

    top = lax.ppermute(band(rows - SUB), "tile", up)
    bottom = lax.ppermute(band(0), "tile", down)
    return shade(False, core, halo, top, bottom, inner)


def solution(mesh):
    in_specs = (P("depth", "tile", None), P("tile"), P())
    out_specs = P(None, "tile", "depth")
    return jax.shard_map(
        per_device, mesh=mesh, in_specs=in_specs, out_specs=out_specs, check_vma=False
    )
```

time: 104 us -> 89 us (0.86)
  local copies, waits for them, and re-layouts: 10.4 us -> 0.02 us
  waiting for transfers between devices: 12.3 us -> 4.58 us
  Pallas kernels: 51.7 us -> 54.8 us
    unnamed x8 -> x2, local copies, waits for them, and re-layouts: 10.1 us -> 0.01 us
    ppermute x4, waiting for transfers between devices: 9.74 us -> 3.28 us  [the longest x2 3.28 us: per_device(): halo = lax.ppermute(last, 'depth', up) + lax.ppermute(first, 'depth', down)]
    pallas_call x4, Pallas kernels: 29.7 us -> 31.9 us  [integrate(): pl.pallas_call(functools.partial(integrate_kernel, place, own), out_shape...]
    pallas_call x1, Pallas kernels: 0.42 us -> 1.86 us  [edges(): pl.pallas_call(edges_kernel, out_shape=(plane, plane, line, line), in_spe...]
    ppermute x3 -> x4, waiting for transfers between devices: 1.24 us -> 0.01 us  [swapped(): return lax.ppermute(block, axis, route)]
    pallas_call x1 -> x4, Pallas kernels: 21.6 us -> 21 us  [the longest x2 19 us: shade(): pl.pallas_call(functools.partial(shade_kernel, inner), out_shape=jax.Shap...]
    ppermute x3 -> x4, starting transfers between devices: 3.41 us -> 3.69 us  [swapped(): return lax.ppermute(block, axis, route)]
  transfers between devices with their start and end apart: 11 -> 12, of which waited for: 6 -> 2; matrix products, arithmetic and copies ran while one was open for 0% -> 0% of each run, Pallas kernels for 22% -> 42%
where the time goes in v3:
time: 89 us; the launch traced here: 87.5 us
  Pallas kernels  54.8 us (62%)
  starting transfers between devices  27.1 us (30%)
  waiting for transfers between devices  4.58 us (5%)
  between operations  0.9 us (1%)
    pallas_call x4, Pallas kernels, integrate(): pl.pallas_call(functools.partial(integrate_kernel, place, own), out_shape...  31.9 us
    pallas_call x2, Pallas kernels, shade(): pl.pallas_call(functools.partial(shade_kernel, inner), out_shape=jax.Shap...  19 us
    ppermute x2, starting transfers between devices, per_device(): halo = lax.ppermute(last, 'depth', up) + lax.ppermute(first, 'depth', down)  5.62 us
    ppermute x1, starting transfers between devices, per_device(): bottom = lax.ppermute(band(0), 'tile', down)  3.96 us
    ppermute x1, starting transfers between devices, per_device(): zlo = lax.ppermute(last_plane, 'depth', up)  3.71 us
    ppermute x4, starting transfers between devices, swapped(): return lax.ppermute(block, axis, route)  3.69 us
    ppermute x2, waiting for transfers between devices, per_device(): halo = lax.ppermute(last, 'depth', up) + lax.ppermute(first, 'depth', down)  3.28 us
    ppermute x1, starting transfers between devices, per_device(): ylo = lax.ppermute(last_line, 'tile', up)  3.12 us
  transfers between devices with their start and end apart: 12, of which 2 were waited for; matrix products, arithmetic and copies ran while one was open for 0% of the time, Pallas kernels for 42%

profile of v3, /device:TPU:9, one launch (start us, length us, event | category | flops | bytes accessed | tf_op | source)
XLA Modules:
  0.0 87.5 jit_solution(15533822391247729353)
XLA Ops:
  0.0 1.9 %edges.1 = (bf16[64,1024]{1,0:T(8,128)(2,1)S(1)}, bf16[64,1024]{1,0:T(8,128)(2,1)S(1)}, bf16[32,1024]{1,0:T(8,128)(2,1)S(1)}, bf16[32,1024]{1,0:T(8,128)(2,1)S(1)}) custom-call(s32[32,64,1024]{2,1,0:T(8,128)} %density_ref.9), custom_call_target="tpu_custom_call" | custom-call | tf_op jit(solution)/shard_map/edges/pallas_call | solution.py:75
  1.9 3.7 %collective-permute-start = (bf16[64,1024]{1,0:T(8,128)(2,1)S(1)}, bf16[64,1024]{1,0:T(8,128)(2,1)S(1)}, u32[]{:S(2)}, u32[]{:S(2)}) collective-permute-start(bf16[64,1024]{1,0:T(8,128)(2,1)S(1)} %get-tuple-element.16), channel_id=1, source_target_pairs={{0,8},{8,16},{16,24},{1,9},{9,17},{17,25},{2,10},{10,18},{18,26},{... | collective-permute-start | bytes 393224 | tf_op jit(solution)/shard_map/ppermute | solution.py:513
  5.6 1.9 %collective-permute-start.1 = (bf16[64,1024]{1,0:T(8,128)(2,1)S(1)}, bf16[64,1024]{1,0:T(8,128)(2,1)S(1)}, u32[]{:S(2)}, u32[]{:S(2)}) collective-permute-start(bf16[64,1024]{1,0:T(8,128)(2,1)S(1)} %get-tuple-element.17), channel_id=1, source_target_pairs={{8,0},{16,8},{24,16},{9,1},{17,9},{25,17},{10,2},{18,10},{26,18},{... | collective-permute-start | bytes 393224 | tf_op jit(solution)/shard_map/ppermute | solution.py:514
  7.5 3.1 %collective-permute-start.2 = (bf16[32,1024]{1,0:T(8,128)(2,1)S(1)}, bf16[32,1024]{1,0:T(8,128)(2,1)S(1)}, u32[]{:S(2)}, u32[]{:S(2)}) collective-permute-start(bf16[32,1024]{1,0:T(8,128)(2,1)S(1)} %get-tuple-element.18), channel_id=1, source_target_pairs={{0,1},{1,2},{2,3},{3,4},{4,5},{5,6},{6,7},{8,9},{9,10},{10,11},{11... | collective-permute-start | bytes 196616 | tf_op jit(solution)/shard_map/ppermute | solution.py:516
  10.6 3.1 %collective-permute-start.3 = (bf16[32,1024]{1,0:T(8,128)(2,1)S(1)}, bf16[32,1024]{1,0:T(8,128)(2,1)S(1)}, u32[]{:S(2)}, u32[]{:S(2)}) collective-permute-start(bf16[32,1024]{1,0:T(8,128)(2,1)S(1)} %get-tuple-element.19), channel_id=1, source_target_pairs={{1,0},{2,1},{3,2},{4,3},{5,4},{6,5},{7,6},{9,8},{10,9},{11,10},{12... | collective-permute-start | bytes 196616 | tf_op jit(solution)/shard_map/ppermute | solution.py:517
  14.4 0.0 collective-permute-done.2.ylo_ref
  14.4 1.3 %collective-permute-done.3.yhi_ref = bf16[32,1024]{1,0:T(8,128)(2,1)S(1)} collective-permute-done((bf16[32,1024]{1,0:T(8,128)(2,1)S(1)}, bf16[32,1024]{1,0:T(8,128)(2,1)S(1)}, u32[]{:S(2)}, u32[]{:S(2)}) %collective-permute-start.3) | collective-permute-done | bytes 65568 | tf_op jit(solution)/shard_map/ppermute | solution.py:517
  15.7 0.0 collective-permute-done.zlo_ref.token_ref
  15.7 0.0 collective-permute-done.1.zhi_ref
  15.7 7.9 %integrate.4.token_ref = f32[8,2,64,128]{3,2,1,0:T(8,128)S(1)} custom-call(s32[1]{0:T(128)} %copy.4.flip_ref, f32[4,4]{1,0:T(4,128)S(1)} %copy-done, s32[32,64,1024]{2,1,0:T(8,128)} %density_ref.9, bf16[64,1024]{1,0:T(8,128)(2,1)S(1)} %collective-permute-done.zlo_ref.token_ref, bf16[64,1024]{1,0:T(8,128)(2,1)S(1)} %collective-permute-done.1.zhi_ref, ...), custom_call_target="tpu_custom_call" | custom-call | flops 36700160 | bytes 4194304 | tf_op jit(solution)/shard_map/integrate/pallas_call | solution.py:233
  23.6 0.1 collective-permute-start.4
  23.7 0.1 add_convert_fusion.leads_ref
  23.8 8.0 %integrate.5.refs_0_ = f32[8,2,64,128]{3,2,1,0:T(8,128)S(1)} custom-call(s32[1]{0:T(128)} %copy.4.flip_ref, f32[4,4]{1,0:T(4,128)S(1)} %copy-done, s32[32,64,1024]{2,1,0:T(8,128)} %density_ref.9, bf16[64,1024]{1,0:T(8,128)(2,1)S(1)} %collective-permute-done.zlo_ref.token_ref, bf16[64,1024]{1,0:T(8,128)(2,1)S(1)} %collective-permute-done.1.zhi_ref, ...), custom_call_target="tpu_custom_call" | custom-call | flops 36700160 | bytes 4194304 | tf_op jit(solution)/shard_map/integrate/pallas_call | solution.py:233
  31.8 0.0 collective-permute-done.4.refs_1_
  31.9 0.8 compose.2
  32.7 3.2 %collective-permute-start.5 = (f32[4,2,64,128]{3,2,1,0:T(8,128)S(1)}, f32[4,2,64,128]{3,2,1,0:T(8,128)S(1)}, u32[]{:S(2)}, u32[]{:S(2)}) collective-permute-start(f32[4,2,64,128]{3,2,1,0:T(8,128)S(1)} %get-tuple-element.20.token_ref), channel_id=1, source_target_pairs={{0,16},{16,0},{8,24},{24,8},{1,17},{17,1},{9,25},{25,9},{2,18},{18... | collective-permute-start | bytes 786440 | tf_op jit(solution)/shard_map/ppermute | solution.py:37
  35.9 8.0 %integrate.7 = f32[8,2,64,128]{3,2,1,0:T(8,128)S(1)} custom-call(s32[1]{0:T(128)} %copy.4.flip_ref, f32[4,4]{1,0:T(4,128)S(1)} %copy-done, s32[32,64,1024]{2,1,0:T(8,128)} %density_ref.9, bf16[64,1024]{1,0:T(8,128)(2,1)S(1)} %collective-permute-done.zlo_ref.token_ref, bf16[64,1024]{1,0:T(8,128)(2,1)S(1)} %collective-permute-done.1.zhi_ref, ...), custom_call_target="tpu_custom_call" | custom-call | flops 36700160 | bytes 4194304 | tf_op jit(solution)/shard_map/integrate/pallas_call | solution.py:233
  43.9 0.4 collective-permute-start.6
  44.4 0.0 collective-permute-done.5.token_ref.refs_2_
  44.4 0.0 collective-permute-start.7
  44.4 7.9 %integrate.6.refs_0_ = f32[8,2,64,128]{3,2,1,0:T(8,128)S(1)} custom-call(s32[1]{0:T(128)} %copy.4.flip_ref, f32[4,4]{1,0:T(4,128)S(1)} %copy-done, s32[32,64,1024]{2,1,0:T(8,128)} %density_ref.9, bf16[64,1024]{1,0:T(8,128)(2,1)S(1)} %collective-permute-done.zlo_ref.token_ref, bf16[64,1024]{1,0:T(8,128)(2,1)S(1)} %collective-permute-done.1.zhi_ref, ...), custom_call_target="tpu_custom_call" | custom-call | flops 36700160 | bytes 4194304 | tf_op jit(solution)/shard_map/integrate/pallas_call | solution.py:233
  52.3 0.0 collective-permute-done.7.refs_3_
  52.3 1.1 %compose.3 = (f32[8,2,64,128]{3,2,1,0:T(8,128)S(1)}, f32[64,128]{1,0:T(8,128)S(1)}, f32[64,128]{1,0:T(8,128)S(1)}) custom-call(s32[2]{0:T(128)S(1)} %add_convert_fusion.leads_ref, f32[8,2,64,128]{3,2,1,0:T(8,128)S(1)} %integrate.6.refs_0_, f32[8,2,64,128]{3,2,1,0:T(8,128)S(1)} %collective-permute-done.6.refs_1_, ...), custom_call_target="tpu_custom_call" | custom-call | bytes 524288 | tf_op jit(solution)/shard_map/compose/pallas_call | solution.py:484
  53.5 3.7 %collective-permute-start.8 = (f32[64,128]{1,0:T(8,128)S(1)}, f32[64,128]{1,0:T(8,128)S(1)}, u32[]{:S(2)}, u32[]{:S(2)}) collective-permute-start(f32[64,128]{1,0:T(8,128)S(1)} %get-tuple-element.25), channel_id=1, source_target_pairs={{0,8},{8,16},{16,24},{1,9},{9,17},{17,25},{2,10},{10,18},{18,26},{... | collective-permute-start | bytes 98312 | tf_op jit(solution)/shard_map/ppermute | solution.py:556
  57.2 1.9 %collective-permute-start.9 = (f32[64,128]{1,0:T(8,128)S(1)}, f32[64,128]{1,0:T(8,128)S(1)}, u32[]{:S(2)}, u32[]{:S(2)}) collective-permute-start(f32[64,128]{1,0:T(8,128)S(1)} %get-tuple-element.26), channel_id=1, source_target_pairs={{8,0},{16,8},{24,16},{9,1},{17,9},{25,17},{10,2},{18,10},{26,18},{... | collective-permute-start | bytes 98312 | tf_op jit(solution)/shard_map/ppermute | solution.py:556
  59.1 0.0 collective-permute-done.8
  59.1 3.3 %collective-permute-done.9 = f32[64,128]{1,0:T(8,128)S(1)} collective-permute-done((f32[64,128]{1,0:T(8,128)S(1)}, f32[64,128]{1,0:T(8,128)S(1)}, u32[]{:S(2)}, u32[]{:S(2)}) %collective-permute-start.9) | collective-permute-done | bytes 32800 | tf_op jit(solution)/shard_map/ppermute | solution.py:556
  62.4 4.0 %collective-permute-start.11 = (f32[17,8,128]{2,1,0:T(8,128)S(1)}, f32[17,8,128]{2,1,0:T(8,128)S(1)}, u32[]{:S(2)}, u32[]{:S(2)}) collective-permute-start(f32[17,8,128]{2,1,0:T(8,128)S(1)} %pad_maximum_fusion.1), channel_id=1, source_target_pairs={{1,0},{2,1},{3,2},{4,3},{5,4},{6,5},{7,6},{9,8},{10,9},{11,10},{12... | collective-permute-start | bytes 208904 | tf_op jit(solution)/shard_map/ppermute | solution.py:566
  66.4 2.0 %collective-permute-start.10 = (f32[17,8,128]{2,1,0:T(8,128)S(1)}, f32[17,8,128]{2,1,0:T(8,128)S(1)}, u32[]{:S(2)}, u32[]{:S(2)}) collective-permute-start(f32[17,8,128]{2,1,0:T(8,128)S(1)} %pad_maximum_fusion), channel_id=1, source_target_pairs={{0,1},{1,2},{2,3},{3,4},{4,5},{5,6},{6,7},{8,9},{9,10},{10,11},{11... | collective-permute-start | bytes 208904 | tf_op jit(solution)/shard_map/ppermute | solution.py:565
  68.5 12.7 %shade_inner.1.rest_2_ = f32[3,64,256]{2,1,0:T(8,128)S(1)} custom-call(f32[8,2,64,128]{3,2,1,0:T(8,128)S(1)} %get-tuple-element.24.core_ref, f32[64,128]{1,0:T(8,128)S(1)} %add.14.halo_ref), custom_call_target="tpu_custom_call" | custom-call | flops 56819712 | bytes 524288 | tf_op jit(solution)/shard_map/shade_inner/pallas_call | solution.py:409
  81.1 0.0 collective-permute-done.10.rest_0_
  81.1 6.4 %shade_outer.1 = f32[3,64,256]{2,1,0:T(8,128)} custom-call(f32[8,2,64,128]{3,2,1,0:T(8,128)S(1)} %get-tuple-element.24.core_ref, f32[64,128]{1,0:T(8,128)S(1)} %add.14.halo_ref, f32[17,8,128]{2,1,0:T(8,128)S(1)} %collective-permute-done.10.rest_0_, f32[17,8,128]{2,1,0:T(8,128)S(1)} %collective-permute-done.11.rest_1_, f32[3,64,256]{2,1,0:T(8,128)S(1)} %shade_inner.1.rest_2_), custom_call_target="tpu_custom_call" | custom-call | flops 18939904 | bytes 524288 | tf_op jit(solution)/shard_map/shade_outer/pallas_call | solution.py:409
  (9 shorter events, 0.0 us)
Async XLA Ops:
  0.0 15.7 %copy-start = (f32[4,4]{1,0:T(4,128)S(1)}, f32[4,4]{1,0:T(4,128)}, u32[]{:S(2)}) copy-start(f32[4,4]{1,0:T(4,128)} %coeff_ref.7) | copy-start | bytes 196
  1.9 13.8 %collective-permute-start = (bf16[64,1024]{1,0:T(8,128)(2,1)S(1)}, bf16[64,1024]{1,0:T(8,128)(2,1)S(1)}, u32[]{:S(2)}, u32[]{:S(2)}) collective-permute-start(bf16[64,1024]{1,0:T(8,128)(2,1)S(1)} %get-tuple-element.16), channel_id=1, source_target_pairs={{0,8},{8,16},{16,24},{1,9},{9,17},{17,25},{2,10},{10,18},{18,26},{... | collective-permute-start | bytes 393224 | tf_op jit(solution)/shard_map/ppermute | solution.py:513
  5.6 10.1 %collective-permute-start.1 = (bf16[64,1024]{1,0:T(8,128)(2,1)S(1)}, bf16[64,1024]{1,0:T(8,128)(2,1)S(1)}, u32[]{:S(2)}, u32[]{:S(2)}) collective-permute-start(bf16[64,1024]{1,0:T(8,128)(2,1)S(1)} %get-tuple-element.17), channel_id=1, source_target_pairs={{8,0},{16,8},{24,16},{9,1},{17,9},{25,17},{10,2},{18,10},{26,18},{... | collective-permute-start | bytes 393224 | tf_op jit(solution)/shard_map/ppermute | solution.py:514
  7.5 6.8 %collective-permute-start.2 = (bf16[32,1024]{1,0:T(8,128)(2,1)S(1)}, bf16[32,1024]{1,0:T(8,128)(2,1)S(1)}, u32[]{:S(2)}, u32[]{:S(2)}) collective-permute-start(bf16[32,1024]{1,0:T(8,128)(2,1)S(1)} %get-tuple-element.18), channel_id=1, source_target_pairs={{0,1},{1,2},{2,3},{3,4},{4,5},{5,6},{6,7},{8,9},{9,10},{10,11},{11... | collective-permute-start | bytes 196616 | tf_op jit(solution)/shard_map/ppermute | solution.py:516
  10.6 5.0 %collective-permute-start.3 = (bf16[32,1024]{1,0:T(8,128)(2,1)S(1)}, bf16[32,1024]{1,0:T(8,128)(2,1)S(1)}, u32[]{:S(2)}, u32[]{:S(2)}) collective-permute-start(bf16[32,1024]{1,0:T(8,128)(2,1)S(1)} %get-tuple-element.19), channel_id=1, source_target_pairs={{1,0},{2,1},{3,2},{4,3},{5,4},{6,5},{7,6},{9,8},{10,9},{11,10},{12... | collective-permute-start | bytes 196616 | tf_op jit(solution)/shard_map/ppermute | solution.py:517
  23.6 8.2 %collective-permute-start.4 = (f32[8,2,64,128]{3,2,1,0:T(8,128)S(1)}, f32[8,2,64,128]{3,2,1,0:T(8,128)S(1)}, u32[]{:S(2)}, u32[]{:S(2)}) collective-permute-start(f32[8,2,64,128]{3,2,1,0:T(8,128)S(1)} %integrate.4.token_ref), channel_id=1, source_target_pairs={{0,8},{8,0},{16,24},{24,16},{1,9},{9,1},{17,25},{25,17},{2,10},{10... | collective-permute-start | bytes 1572872 | tf_op jit(solution)/shard_map/ppermute | solution.py:37
  32.7 11.6 %collective-permute-start.5 = (f32[4,2,64,128]{3,2,1,0:T(8,128)S(1)}, f32[4,2,64,128]{3,2,1,0:T(8,128)S(1)}, u32[]{:S(2)}, u32[]{:S(2)}) collective-permute-start(f32[4,2,64,128]{3,2,1,0:T(8,128)S(1)} %get-tuple-element.20.token_ref), channel_id=1, source_target_pairs={{0,16},{16,0},{8,24},{24,8},{1,17},{17,1},{9,25},{25,9},{2,18},{18... | collective-permute-start | bytes 786440 | tf_op jit(solution)/shard_map/ppermute | solution.py:37
  43.9 8.4 %collective-permute-start.6 = (f32[8,2,64,128]{3,2,1,0:T(8,128)S(1)}, f32[8,2,64,128]{3,2,1,0:T(8,128)S(1)}, u32[]{:S(2)}, u32[]{:S(2)}) collective-permute-start(f32[8,2,64,128]{3,2,1,0:T(8,128)S(1)} %integrate.7), channel_id=1, source_target_pairs={{0,8},{8,0},{16,24},{24,16},{1,9},{9,1},{17,25},{25,17},{2,10},{10... | collective-permute-start | bytes 1572872 | tf_op jit(solution)/shard_map/ppermute | solution.py:37
  44.4 8.0 %collective-permute-start.7 = (f32[4,2,64,128]{3,2,1,0:T(8,128)S(1)}, f32[4,2,64,128]{3,2,1,0:T(8,128)S(1)}, u32[]{:S(2)}, u32[]{:S(2)}) collective-permute-start(f32[4,2,64,128]{3,2,1,0:T(8,128)S(1)} %get-tuple-element.23), channel_id=1, source_target_pairs={{0,16},{16,0},{8,24},{24,8},{1,17},{17,1},{9,25},{25,9},{2,18},{18... | collective-permute-start | bytes 786440 | tf_op jit(solution)/shard_map/ppermute | solution.py:37
  53.5 5.7 %collective-permute-start.8 = (f32[64,128]{1,0:T(8,128)S(1)}, f32[64,128]{1,0:T(8,128)S(1)}, u32[]{:S(2)}, u32[]{:S(2)}) collective-permute-start(f32[64,128]{1,0:T(8,128)S(1)} %get-tuple-element.25), channel_id=1, source_target_pairs={{0,8},{8,16},{16,24},{1,9},{9,17},{17,25},{2,10},{10,18},{18,26},{... | collective-permute-start | bytes 98312 | tf_op jit(solution)/shard_map/ppermute | solution.py:556
  57.2 5.2 %collective-permute-start.9 = (f32[64,128]{1,0:T(8,128)S(1)}, f32[64,128]{1,0:T(8,128)S(1)}, u32[]{:S(2)}, u32[]{:S(2)}) collective-permute-start(f32[64,128]{1,0:T(8,128)S(1)} %get-tuple-element.26), channel_id=1, source_target_pairs={{8,0},{16,8},{24,16},{9,1},{17,9},{25,17},{10,2},{18,10},{26,18},{... | collective-permute-start | bytes 98312 | tf_op jit(solution)/shard_map/ppermute | solution.py:556
  62.4 18.7 %collective-permute-start.11 = (f32[17,8,128]{2,1,0:T(8,128)S(1)}, f32[17,8,128]{2,1,0:T(8,128)S(1)}, u32[]{:S(2)}, u32[]{:S(2)}) collective-permute-start(f32[17,8,128]{2,1,0:T(8,128)S(1)} %pad_maximum_fusion.1), channel_id=1, source_target_pairs={{1,0},{2,1},{3,2},{4,3},{5,4},{6,5},{7,6},{9,8},{10,9},{11,10},{12... | collective-permute-start | bytes 208904 | tf_op jit(solution)/shard_map/ppermute | solution.py:566
  66.4 14.7 %collective-permute-start.10 = (f32[17,8,128]{2,1,0:T(8,128)S(1)}, f32[17,8,128]{2,1,0:T(8,128)S(1)}, u32[]{:S(2)}, u32[]{:S(2)}) collective-permute-start(f32[17,8,128]{2,1,0:T(8,128)S(1)} %pad_maximum_fusion), channel_id=1, source_target_pairs={{0,1},{1,2},{2,3},{3,4},{4,5},{5,6},{6,7},{8,9},{9,10},{10,11},{11... | collective-permute-start | bytes 208904 | tf_op jit(solution)/shard_map/ppermute | solution.py:565

commit v4 on v3

--- a/solution.py
+++ b/solution.py
@@ -88,43 +88,90 @@
     )(density)
 
 
-def integrate_kernel(
-    place, own, flip_ref, coeff_ref, density_ref, zlo_ref, zhi_ref, ylo_ref, yhi_ref, token_ref,
-    out_ref, field, zlo_f, zhi_f, sems,
-):
+def first_tile(place, own):
+    position = lax.axis_index("depth")
+    core, chip = position % 2, position // 2 % 2
+    block = lax.rem(core + place[0], 2) + 2 * lax.rem(chip + place[1], 2) + 4 * place[2]
+    return block * own
+
+
+def pack_kernel(places, own, density_ref, *refs):
+    fields, (stage, sems) = refs[:-2], refs[-2:]
     cells, rows, width = density_ref.shape
     tiles = width // LANES
+    at = pl.ds(SUB, rows)
+
+    def copy(z):
+        return pltpu.make_async_copy(density_ref.at[z], stage.at[z], sems.at[z])
+
+    for z in range(cells):
+        copy(z).start()
+    firsts = [first_tile(place, own) for place in places]
+
+    def one(z, carry):
+        copy(z).wait()
+        for first, field in zip(firsts, fields):
+            for j in range(own + 2):
+                tile = jnp.clip(first + j - 1, 0, tiles - 1)
+                cols = pl.ds(pl.multiple_of(tile * LANES, LANES), LANES)
+                field[z + 1, j, at, :] = stage[z, :, cols].astype(jnp.float32) - CENTRE
+        return carry
+
+    lax.fori_loop(0, cells, one, 0)
+    outside = jnp.full((rows, LANES), -CENTRE, jnp.float32)
+    for first, field in zip(firsts, fields):
+
+        @pl.when(first == 0)
+        def _():
+            for z in range(cells):
+                field[z + 1, 0, at, :] = outside
+
+        @pl.when(first + own == tiles)
+        def _():
+            for z in range(cells):
+                field[z + 1, own + 1, at, :] = outside
+
+
+def pack(density, places, count):
+    cells, rows, width = density.shape
+    own = width // LANES // count
+    shape = jax.ShapeDtypeStruct((cells + 2, own + 2, rows + 2 * SUB, LANES), jnp.float32)
+    return pl.pallas_call(
+        functools.partial(pack_kernel, places, own),
+        out_shape=[shape] * len(places),
+        in_specs=[pl.BlockSpec(memory_space=pl.ANY)],
+        out_specs=[pl.BlockSpec(memory_space=pltpu.VMEM)] * len(places),
+        scratch_shapes=[
+            pltpu.VMEM((cells, rows, width), jnp.int32),
+            pltpu.SemaphoreType.DMA((cells,)),
+        ],
+        compiler_params=pltpu.CompilerParams(vmem_limit_bytes=12 << 20),
+        cost_estimate=pl.CostEstimate(
+            flops=2 * density.size, transcendentals=0, bytes_accessed=4 * density.size
+        ),
+        name="pack",
+    )(density)
+
+
+def integrate_kernel(
+    place, flip_ref, coeff_ref, packed_ref, zlo_ref, zhi_ref, ylo_ref, yhi_ref, token_ref,
+    out_ref, field_ref
+):
+    planes, wide, high, _ = field_ref.shape
+    cells, own, rows = planes - 2, wide - 2, high - 2 * SUB
+    count = lax.axis_size("depth")
     blocks = rows // SUB
-    count = tiles // own
     position = lax.axis_index("depth")
-    c, y = position % 2, position // 2 % 2
-    first = (lax.rem(c + place[0], 2) + 2 * lax.rem(y + place[1], 2) + 4 * place[2]) * own
-    sources = [jnp.maximum(first - 1, 0)]
-    sources += [first + j for j in range(own)]
-    sources += [jnp.minimum(first + own, tiles - 1)]
-
-    def copy(b, j):
-        start = pl.multiple_of(sources[j] * LANES, LANES)
-        return pltpu.make_async_copy(
-            density_ref.at[:, pl.ds(b * SUB, SUB), pl.ds(start, LANES)],
-            field.at[:, j, pl.ds(SUB + b * SUB, SUB), :],
-            sems.at[b, j],
-        )
-
-    for b in range(blocks):
-        for j in range(own + 2):
-            copy(b, j).start()
-    flip = flip_ref[0]
+    first = first_tile(place, own)
     for j in range(own):
         cols = pl.ds(pl.multiple_of((first + j) * LANES, LANES), LANES)
-        zlo_f[j] = zlo_ref[:, cols].astype(jnp.float32) - CENTRE
-        zhi_f[j] = zhi_ref[:, cols].astype(jnp.float32) - CENTRE
-        top = ylo_ref[:, cols].astype(jnp.float32).astype(jnp.int32)
-        bottom = yhi_ref[:, cols].astype(jnp.float32).astype(jnp.int32)
-        for z in range(cells):
-            field[z, j + 1, SUB - 1 : SUB, :] = top[z : z + 1]
-            field[z, j + 1, SUB + rows : SUB + rows + 1, :] = bottom[z : z + 1]
-
+        for ref, z in ((zlo_ref, 0), (zhi_ref, cells + 1)):
+            field_ref[z, j + 1, SUB : SUB + rows, :] = ref[:, cols].astype(jnp.float32) - CENTRE
+        for ref, y in ((ylo_ref, SUB - 1), (yhi_ref, SUB + rows)):
+            lines = ref[:, cols].astype(jnp.float32) - CENTRE
+            for z in range(cells):
+                field_ref[z + 1, j + 1, y : y + 1, :] = lines[z : z + 1]
+    flip = flip_ref[0]
     coeffs = []
     for row in range(4):
         scale = LOG2E if row == 0 else -LOG2E
@@ -146,55 +193,25 @@
     def poly(c, t):
         return c[0] + t * (c[1] + t * (c[2] + t * c[3]))
 
-    def arrive(b):
-        for j in range(own + 2):
-            copy(b, j).wait()
-        at = pl.ds(SUB + b * SUB, SUB)
-
-        @pl.when(first == 0)
-        def _():
-            for z in range(cells):
-                field[z, 0, at, :] = jnp.zeros((SUB, LANES), jnp.int32)
-
-        @pl.when(first + own == tiles)
-        def _():
-            for z in range(cells):
-                field[z, own + 1, at, :] = jnp.zeros((SUB, LANES), jnp.int32)
-
-    arrive(0)
-
-    def block(b, carry):
-        @pl.when(b + 1 < blocks)
-        def _():
-            arrive(b + 1)
-
-        r = pl.multiple_of(b * SUB, SUB)
-        for j in range(1, own + 1):
-            column(r, j)
-        return carry
-
-    def column(r, j):
+    def block(index, carry):
+        out_j = index // blocks
+        j = out_j + 1
+        r = pl.multiple_of(index % blocks * SUB, SUB)
         at = pl.ds(r + SUB, SUB)
         zero = jnp.zeros((SUB, LANES), jnp.float32)
         tau = zero
         factor = jnp.ones((SUB, LANES), jnp.float32)
         between = zero
         sums = [zero] * 6
-        below = zlo_f[j - 1, pl.ds(r, SUB), :]
-        raw = field[0, j, at, :]
-        here = raw.astype(jnp.float32) - CENTRE
-        for z in range(cells):
-            if z + 1 < cells:
-                raw_above = field[z + 1, j, at, :]
-                above = raw_above.astype(jnp.float32) - CENTRE
-            else:
-                raw_above = raw
-                above = zhi_f[j - 1, pl.ds(r, SUB), :]
-            left = pltpu.roll(jnp.where(last_lane, field[z, j - 1, at, :], raw), 1, 1)
-            right = pltpu.roll(jnp.where(first_lane, field[z, j + 1, at, :], raw), LANES - 1, 1)
-            gx = (right - left).astype(jnp.float32)
-            up = field[z, j, pl.ds(r + SUB + 1, SUB), :]
-            gy = (up - field[z, j, pl.ds(r + SUB - 1, SUB), :]).astype(jnp.float32)
+        below = field_ref[0, j, at, :]
+        here = field_ref[1, j, at, :]
+        for z in range(1, cells + 1):
+            above = field_ref[z + 1, j, at, :]
+            left = pltpu.roll(jnp.where(last_lane, field_ref[z, j - 1, at, :], here), 1, 1)
+            right = jnp.where(first_lane, field_ref[z, j + 1, at, :], here)
+            gx = pltpu.roll(right, LANES - 1, 1) - left
+            gy = field_ref[z, j, pl.ds(r + SUB + 1, SUB), :]
+            gy = gy - field_ref[z, j, pl.ds(r + SUB - 1, SUB), :]
             gz = above - below
             norm = lax.rsqrt(gx * gx + gy * gy + (gz * gz + 255.0 * 255.0))
             shade = 0.35 + jnp.abs((lx * gx + ly * gy + lz * gz) * norm)
@@ -202,51 +219,49 @@
             following = jnp.exp2(rate * tau)
             weight = following - factor
             factor = following
-            if z < cells - 1:
+            if z < cells:
                 between = between + following
             tilt = weight * norm
             lit = weight * shade
             terms = [lit * (1.0 / (1.0 + jnp.exp2(poly(coeffs[k], here)))) for k in (1, 2, 3)]
             terms += [tilt * gx, tilt * gy, tilt * gz]
             sums = [s + t for s, t in zip(sums, terms)]
-            below, here, raw = here, above, raw_above
+            below, here = here, above
         inverse = 1.0 / factor
         flipped = flip == 1
         scale = jnp.where(flipped, inverse, -1.0)
         out = pl.ds(r, SUB)
         for k in range(3):
-            out_ref[k, j - 1, out, :] = sums[k] * scale
-            out_ref[k + 5, j - 1, out, :] = sums[k + 3] * scale
-        out_ref[3, j - 1, out, :] = 1.0 - jnp.where(flipped, inverse, factor)
-        out_ref[4, j - 1, out, :] = (h_last * factor - h_first - delta * between) * scale
-
-    lax.fori_loop(0, blocks, block, 0)
-
-
-def integrate(place, count, view_flip, tf_coeff, density, zlo, zhi, ylo, yhi, token):
-    cells, rows, width = density.shape
-    own = width // LANES // count
+            out_ref[k, out_j, out, :] = sums[k] * scale
+            out_ref[k + 5, out_j, out, :] = sums[k + 3] * scale
+        out_ref[3, out_j, out, :] = 1.0 - jnp.where(flipped, inverse, factor)
+        out_ref[4, out_j, out, :] = (h_last * factor - h_first - delta * between) * scale
+        return carry
+
+    lax.fori_loop(0, own * blocks, block, 0)
+
+
+def integrate(place, view_flip, tf_coeff, field, halos, token):
+    planes, wide, high, _ = field.shape
+    cells, own, rows = planes - 2, wide - 2, high - 2 * SUB
     smem = pl.BlockSpec(memory_space=pltpu.SMEM)
     vmem = pl.BlockSpec(memory_space=pltpu.VMEM)
-    anywhere = pl.BlockSpec(memory_space=pl.ANY)
     voxels = cells * rows * own * LANES
     return pl.pallas_call(
-        functools.partial(integrate_kernel, place, own),
-        out_shape=jax.ShapeDtypeStruct((8, own, rows, LANES), jnp.float32),
-        in_specs=[smem, smem, anywhere, vmem, vmem, vmem, vmem, anywhere],
-        out_specs=vmem,
-        scratch_shapes=[
-            pltpu.VMEM((cells, own + 2, rows + 2 * SUB, LANES), jnp.int32),
-            pltpu.VMEM((own, rows, LANES), jnp.float32),
-            pltpu.VMEM((own, rows, LANES), jnp.float32),
-            pltpu.SemaphoreType.DMA((rows // SUB, own + 2)),
-        ],
-        compiler_params=pltpu.CompilerParams(vmem_limit_bytes=52 << 20),
+        functools.partial(integrate_kernel, place),
+        out_shape=(
+            jax.ShapeDtypeStruct((8, own, rows, LANES), jnp.float32),
+            jax.ShapeDtypeStruct(field.shape, field.dtype),
+        ),
+        in_specs=[smem, smem, vmem, vmem, vmem, vmem, vmem, pl.BlockSpec(memory_space=pl.ANY)],
+        out_specs=[vmem, vmem],
+        input_output_aliases={2: 1},
+        compiler_params=pltpu.CompilerParams(vmem_limit_bytes=8 << 20),
         cost_estimate=pl.CostEstimate(
             flops=70 * voxels, transcendentals=0, bytes_accessed=8 * voxels
         ),
         name="integrate",
-    )(view_flip, tf_coeff, density, zlo, zhi, ylo, yhi, token)
+    )(view_flip, tf_coeff, field, *halos, token)[0]
 
 
 def shade_kernel(inner, core_ref, halo_ref, *rest):
@@ -516,18 +531,21 @@
     ylo = lax.ppermute(last_line, "tile", up)
     yhi = lax.ppermute(first_line, "tile", down)
 
+    halos = (zlo, zhi, ylo, yhi)
+    quarters = ((1, 1), (0, 1), (1, 0), (0, 0))
+    places = [quarter + (h,) for quarter in quarters for h in range(high)]
+    fields = dict(zip(places, pack(density, places, count)))
+
     def quarter(core_bit, chip_bit, token):
-        parts = [
-            integrate(
-                (core_bit, chip_bit, h), count, view_flip, tf_coeff, density, zlo, zhi, ylo, yhi, token
-            )
-            for h in range(high)
-        ]
+        parts = []
+        for h in range(high):
+            place = (core_bit, chip_bit, h)
+            parts.append(integrate(place, view_flip, tf_coeff, fields[place], halos, token))
         return parts[0] if high == 1 else jnp.concatenate(parts, axis=1)
 
     bits = [position // 2**level % 2 for level in range(rounds)]
     leads = jnp.stack([bit == flipped for bit in bits]).astype(jnp.int32)
-    far_given = quarter(1, 1, zlo)
+    far_given = quarter(1, 1, view_flip)
     far_partner = swapped(far_given, "depth", 0)
     far_kept = quarter(0, 1, far_given)
     far = compose(0, "halves", leads, far_kept, far_partner)

time: 89 us -> 95 us (1.067); the launches traced: 87.5 us -> 94.7 us
  local copies, waits for them, and re-layouts: 0.02 us -> 10.1 us
  Pallas kernels: 54.8 us -> 52.1 us
  waiting for transfers between devices: 4.58 us -> 3.3 us
  starting transfers between devices: 27.1 us -> 28.2 us
    unnamed x2 -> x18, local copies, waits for them, and re-layouts: 0.01 us -> 10 us
    pallas_call x4 -> x5, Pallas kernels: 31.9 us -> 29.1 us  [the longest x4 25.5 us: integrate(): pl.pallas_call(functools.partial(integrate_kernel, place), out_shape=(jax...]
    ppermute x1, waiting for transfers between devices: 1.28 us -> 0.01 us  [per_device(): yhi = lax.ppermute(first_line, 'tile', down)]
  transfers between devices with their start and end apart: 12 -> 12, of which waited for: 2 -> 1; matrix products, arithmetic and copies ran while one was open for 0% -> 0% of each run, Pallas kernels for 42% -> 37%
where the time goes in v4:
time: 95 us; the launch traced here: 94.7 us
  Pallas kernels  52.1 us (55%)
  starting transfers between devices  28.2 us (30%)
  local copies, waits for them, and re-layouts  10.1 us (11%)
  waiting for transfers between devices  3.3 us (3%)
    pallas_call x4, Pallas kernels, integrate(): pl.pallas_call(functools.partial(integrate_kernel, place), out_shape=(jax...  25.5 us
    pallas_call x2, Pallas kernels, shade(): pl.pallas_call(functools.partial(shade_kernel, inner), out_shape=jax.Shap...  19 us
    unnamed x18, local copies, waits for them, and re-layouts  10 us
    ppermute x2, starting transfers between devices, per_device(): halo = lax.ppermute(last, 'depth', up) + lax.ppermute(first, 'depth', down)  6.02 us
    ppermute x1, starting transfers between devices, per_device(): zlo = lax.ppermute(last_plane, 'depth', up)  3.97 us
    ppermute x1, starting transfers between devices, per_device(): bottom = lax.ppermute(band(0), 'tile', down)  3.96 us
    ppermute x4, starting transfers between devices, swapped(): return lax.ppermute(block, axis, route)  3.96 us
    pallas_call x1, Pallas kernels, pack(): pl.pallas_call(functools.partial(pack_kernel, places, own), out_shape=[sh...  3.53 us
  transfers between devices with their start and end apart: 12, of which 1 were waited for; matrix products, arithmetic and copies ran while one was open for 0% of the time, Pallas kernels for 37%

profile of v4, /device:TPU:9, one launch (start us, length us, event | category | flops | bytes accessed | tf_op | source)
XLA Modules:
  0.0 94.7 jit_solution(1887305523198929698)
XLA Ops:
  0.0 2.0 %edges.1 = (bf16[64,1024]{1,0:T(8,128)(2,1)S(1)}, bf16[64,1024]{1,0:T(8,128)(2,1)S(1)}, bf16[32,1024]{1,0:T(8,128)(2,1)S(1)}, bf16[32,1024]{1,0:T(8,128)(2,1)S(1)}) custom-call(s32[32,64,1024]{2,1,0:T(8,128)} %density_ref.3), custom_call_target="tpu_custom_call" | custom-call | tf_op jit(solution)/shard_map/edges/pallas_call | solution.py:75
  2.0 0.0 copy-start.6
  2.0 4.0 %collective-permute-start = (bf16[64,1024]{1,0:T(8,128)(2,1)S(1)}, bf16[64,1024]{1,0:T(8,128)(2,1)S(1)}, u32[]{:S(2)}, u32[]{:S(2)}) collective-permute-start(bf16[64,1024]{1,0:T(8,128)(2,1)S(1)} %get-tuple-element.25), channel_id=1, source_target_pairs={{0,8},{8,16},{16,24},{1,9},{9,17},{17,25},{2,10},{10,18},{18,26},{... | collective-permute-start | bytes 393224 | tf_op jit(solution)/shard_map/ppermute | solution.py:528
  6.0 1.9 %collective-permute-start.1 = (bf16[64,1024]{1,0:T(8,128)(2,1)S(1)}, bf16[64,1024]{1,0:T(8,128)(2,1)S(1)}, u32[]{:S(2)}, u32[]{:S(2)}) collective-permute-start(bf16[64,1024]{1,0:T(8,128)(2,1)S(1)} %get-tuple-element.26), channel_id=1, source_target_pairs={{8,0},{16,8},{24,16},{9,1},{17,9},{25,17},{10,2},{18,10},{26,18},{... | collective-permute-start | bytes 393224 | tf_op jit(solution)/shard_map/ppermute | solution.py:529
  7.9 3.1 %collective-permute-start.2 = (bf16[32,1024]{1,0:T(8,128)(2,1)S(1)}, bf16[32,1024]{1,0:T(8,128)(2,1)S(1)}, u32[]{:S(2)}, u32[]{:S(2)}) collective-permute-start(bf16[32,1024]{1,0:T(8,128)(2,1)S(1)} %get-tuple-element.27), channel_id=1, source_target_pairs={{0,1},{1,2},{2,3},{3,4},{4,5},{5,6},{6,7},{8,9},{9,10},{10,11},{11... | collective-permute-start | bytes 196616 | tf_op jit(solution)/shard_map/ppermute | solution.py:531
  11.1 3.1 %collective-permute-start.3 = (bf16[32,1024]{1,0:T(8,128)(2,1)S(1)}, bf16[32,1024]{1,0:T(8,128)(2,1)S(1)}, u32[]{:S(2)}, u32[]{:S(2)}) collective-permute-start(bf16[32,1024]{1,0:T(8,128)(2,1)S(1)} %get-tuple-element.28), channel_id=1, source_target_pairs={{1,0},{2,1},{3,2},{4,3},{5,4},{6,5},{7,6},{9,8},{10,9},{11,10},{12... | collective-permute-start | bytes 196616 | tf_op jit(solution)/shard_map/ppermute | solution.py:532
  14.8 3.5 %pack.1 = (f32[34,4,80,128]{3,2,1,0:T(8,128)S(1)}, f32[34,4,80,128]{3,2,1,0:T(8,128)S(1)}, f32[34,4,80,128]{3,2,1,0:T(8,128)S(1)}, f32[34,4,80,128]{3,2,1,0:T(8,128)S(1)}) custom-call(s32[32,64,1024]{2,1,0:T(8,128)S(1)} %copy-done), custom_call_target="tpu_custom_call" | custom-call | flops 4194304 | bytes 8388608 | tf_op jit(solution)/shard_map/pack/pallas_call | solution.py:139
  18.3 2.4 %copy-done.1 = f32[34,4,80,128]{3,2,1,0:T(8,128)} copy-done((f32[34,4,80,128]{3,2,1,0:T(8,128)}, f32[34,4,80,128]{3,2,1,0:T(8,128)S(1)}, u32[]{:S(2)}) %copy-start.1) | copy-done | bytes 5570584
  20.8 2.5 %copy-done.2 = f32[34,4,80,128]{3,2,1,0:T(8,128)} copy-done((f32[34,4,80,128]{3,2,1,0:T(8,128)}, f32[34,4,80,128]{3,2,1,0:T(8,128)S(1)}, u32[]{:S(2)}) %copy-start.2) | copy-done | bytes 5570584
  23.3 2.4 %copy-done.4 = f32[34,4,80,128]{3,2,1,0:T(8,128)} copy-done((f32[34,4,80,128]{3,2,1,0:T(8,128)}, f32[34,4,80,128]{3,2,1,0:T(8,128)S(1)}, u32[]{:S(2)}) %copy-start.4) | copy-done | bytes 5570584
  25.6 0.0 collective-permute-done.2.ylo_ref
  25.6 0.0 collective-permute-done.3.yhi_ref
  25.6 0.0 collective-permute-done.zlo_ref
  25.7 6.4 %integrate.4 = (f32[8,2,64,128]{3,2,1,0:T(8,128)S(1)}, f32[34,4,80,128]{3,2,1,0:T(8,128)S(1)}) custom-call(s32[1]{0:T(128)} %copy.12.flip_ref.token_ref, f32[4,4]{1,0:T(4,128)S(1)} %copy-done.6, f32[34,4,80,128]{3,2,1,0:T(8,128)S(1)} %get-tuple-element.30.packed_ref, ...), custom_call_target="tpu_custom_call", output_to_operand_aliasing={{1}: (2, {})} | custom-call | flops 36700160 | bytes 4194304 | tf_op jit(solution)/shard_map/integrate/pallas_call | solution.py:250
  32.1 0.1 collective-permute-start.4
  32.2 0.1 add_convert_fusion.leads_ref
  32.3 2.7 %copy-done.5 = f32[34,4,80,128]{3,2,1,0:T(8,128)S(1)} copy-done((f32[34,4,80,128]{3,2,1,0:T(8,128)S(1)}, f32[34,4,80,128]{3,2,1,0:T(8,128)}, u32[]{:S(2)}) %copy-start.5) | copy-done | bytes 5570584
  35.0 6.4 %integrate.5 = (f32[8,2,64,128]{3,2,1,0:T(8,128)S(1)}, f32[34,4,80,128]{3,2,1,0:T(8,128)S(1)}) custom-call(s32[1]{0:T(128)} %copy.12.flip_ref.token_ref, f32[4,4]{1,0:T(4,128)S(1)} %copy-done.6, f32[34,4,80,128]{3,2,1,0:T(8,128)S(1)} %copy-done.5, bf16[64,1024]{1,0:T(8,128)(2,1)S(1)} %collective-permute-done.zlo_ref, ...), custom_call_target="tpu_custom_call", output_to_operand_aliasing={{1}: (2, {})} | custom-call | flops 36700160 | bytes 4194304 | tf_op jit(solution)/shard_map/integrate/pallas_call | solution.py:250
  41.4 0.8 compose.2
  42.2 2.4 %collective-permute-start.5 = (f32[4,2,64,128]{3,2,1,0:T(8,128)S(1)}, f32[4,2,64,128]{3,2,1,0:T(8,128)S(1)}, u32[]{:S(2)}, u32[]{:S(2)}) collective-permute-start(f32[4,2,64,128]{3,2,1,0:T(8,128)S(1)} %get-tuple-element.33.token_ref), channel_id=1, source_target_pairs={{0,16},{16,0},{8,24},{24,8},{1,17},{17,1},{9,25},{25,9},{2,18},{18... | collective-permute-start | bytes 786440 | tf_op jit(solution)/shard_map/ppermute | solution.py:37
  44.6 6.4 %integrate.7 = (f32[8,2,64,128]{3,2,1,0:T(8,128)S(1)}, f32[34,4,80,128]{3,2,1,0:T(8,128)S(1)}) custom-call(s32[1]{0:T(128)} %copy.12.flip_ref.token_ref, f32[4,4]{1,0:T(4,128)S(1)} %copy-done.6, f32[34,4,80,128]{3,2,1,0:T(8,128)S(1)} %copy-done.3, bf16[64,1024]{1,0:T(8,128)(2,1)S(1)} %collective-permute-done.zlo_ref, ...), custom_call_target="tpu_custom_call", output_to_operand_aliasing={{1}: (2, {})} | custom-call | flops 36700160 | bytes 4194304 | tf_op jit(solution)/shard_map/integrate/pallas_call | solution.py:250
  51.0 0.4 collective-permute-start.6
  51.5 1.1 %collective-permute-start.7 = (f32[4,2,64,128]{3,2,1,0:T(8,128)S(1)}, f32[4,2,64,128]{3,2,1,0:T(8,128)S(1)}, u32[]{:S(2)}, u32[]{:S(2)}) collective-permute-start(f32[4,2,64,128]{3,2,1,0:T(8,128)S(1)} %get-tuple-element.39), channel_id=1, source_target_pairs={{0,16},{16,0},{8,24},{24,8},{1,17},{17,1},{9,25},{25,9},{2,18},{18... | collective-permute-start | bytes 786440 | tf_op jit(solution)/shard_map/ppermute | solution.py:37
  52.5 6.4 %integrate.6 = (f32[8,2,64,128]{3,2,1,0:T(8,128)S(1)}, f32[34,4,80,128]{3,2,1,0:T(8,128)S(1)}) custom-call(s32[1]{0:T(128)} %copy.12.flip_ref.token_ref, f32[4,4]{1,0:T(4,128)S(1)} %copy-done.6, f32[34,4,80,128]{3,2,1,0:T(8,128)S(1)} %bitcast.12, bf16[64,1024]{1,0:T(8,128)(2,1)S(1)} %collective-permute-done.zlo_ref, ...), custom_call_target="tpu_custom_call", output_to_operand_aliasing={{1}: (2, {})} | custom-call | flops 36700160 | bytes 4194304 | tf_op jit(solution)/shard_map/integrate/pallas_call | solution.py:250
  58.9 1.1 %compose.3 = (f32[8,2,64,128]{3,2,1,0:T(8,128)S(1)}, f32[64,128]{1,0:T(8,128)S(1)}, f32[64,128]{1,0:T(8,128)S(1)}) custom-call(s32[2]{0:T(128)S(1)} %add_convert_fusion.leads_ref, f32[8,2,64,128]{3,2,1,0:T(8,128)S(1)} %get-tuple-element.36.refs_0_, f32[8,2,64,128]{3,2,1,0:T(8,128)S(1)} %collective-permute-done.6.refs_1_, ...), custom_call_target="tpu_custom_call" | custom-call | bytes 524288 | tf_op jit(solution)/shard_map/compose/pallas_call | solution.py:499
  60.1 4.1 %collective-permute-start.8 = (f32[64,128]{1,0:T(8,128)S(1)}, f32[64,128]{1,0:T(8,128)S(1)}, u32[]{:S(2)}, u32[]{:S(2)}) collective-permute-start(f32[64,128]{1,0:T(8,128)S(1)} %get-tuple-element.41), channel_id=1, source_target_pairs={{0,8},{8,16},{16,24},{1,9},{9,17},{17,25},{2,10},{10,18},{18,26},{... | collective-permute-start | bytes 98312 | tf_op jit(solution)/shard_map/ppermute | solution.py:574
  64.2 1.9 %collective-permute-start.9 = (f32[64,128]{1,0:T(8,128)S(1)}, f32[64,128]{1,0:T(8,128)S(1)}, u32[]{:S(2)}, u32[]{:S(2)}) collective-permute-start(f32[64,128]{1,0:T(8,128)S(1)} %get-tuple-element.42), channel_id=1, source_target_pairs={{8,0},{16,8},{24,16},{9,1},{17,9},{25,17},{10,2},{18,10},{26,18},{... | collective-permute-start | bytes 98312 | tf_op jit(solution)/shard_map/ppermute | solution.py:574
  66.1 3.3 %collective-permute-done.9 = f32[64,128]{1,0:T(8,128)S(1)} collective-permute-done((f32[64,128]{1,0:T(8,128)S(1)}, f32[64,128]{1,0:T(8,128)S(1)}, u32[]{:S(2)}, u32[]{:S(2)}) %collective-permute-start.9) | collective-permute-done | bytes 32800 | tf_op jit(solution)/shard_map/ppermute | solution.py:574
  69.4 2.2 %collective-permute-start.10 = (f32[17,8,128]{2,1,0:T(8,128)S(1)}, f32[17,8,128]{2,1,0:T(8,128)S(1)}, u32[]{:S(2)}, u32[]{:S(2)}) collective-permute-start(f32[17,8,128]{2,1,0:T(8,128)S(1)} %pad_maximum_fusion), channel_id=1, source_target_pairs={{0,1},{1,2},{2,3},{3,4},{4,5},{5,6},{6,7},{8,9},{9,10},{10,11},{11... | collective-permute-start | bytes 208904 | tf_op jit(solution)/shard_map/ppermute | solution.py:583
  71.7 4.0 %collective-permute-start.11 = (f32[17,8,128]{2,1,0:T(8,128)S(1)}, f32[17,8,128]{2,1,0:T(8,128)S(1)}, u32[]{:S(2)}, u32[]{:S(2)}) collective-permute-start(f32[17,8,128]{2,1,0:T(8,128)S(1)} %pad_maximum_fusion.1), channel_id=1, source_target_pairs={{1,0},{2,1},{3,2},{4,3},{5,4},{6,5},{7,6},{9,8},{10,9},{11,10},{12... | collective-permute-start | bytes 208904 | tf_op jit(solution)/shard_map/ppermute | solution.py:584
  75.6 12.7 %shade_inner.1.rest_2_ = f32[3,64,256]{2,1,0:T(8,128)S(1)} custom-call(f32[8,2,64,128]{3,2,1,0:T(8,128)S(1)} %get-tuple-element.40.core_ref, f32[64,128]{1,0:T(8,128)S(1)} %add.14.halo_ref), custom_call_target="tpu_custom_call" | custom-call | flops 56819712 | bytes 524288 | tf_op jit(solution)/shard_map/shade_inner/pallas_call | solution.py:424
  88.3 6.4 %shade_outer.1 = f32[3,64,256]{2,1,0:T(8,128)} custom-call(f32[8,2,64,128]{3,2,1,0:T(8,128)S(1)} %get-tuple-element.40.core_ref, f32[64,128]{1,0:T(8,128)S(1)} %add.14.halo_ref, f32[17,8,128]{2,1,0:T(8,128)S(1)} %collective-permute-done.10.rest_0_, f32[17,8,128]{2,1,0:T(8,128)S(1)} %collective-permute-done.11.rest_1_, f32[3,64,256]{2,1,0:T(8,128)S(1)} %shade_inner.1.rest_2_), custom_call_target="tpu_custom_call" | custom-call | flops 18939904 | bytes 524288 | tf_op jit(solution)/shard_map/shade_outer/pallas_call | solution.py:424
  (27 shorter events, 0.1 us)
Async XLA Ops:
  0.0 14.8 %copy-start = (s32[32,64,1024]{2,1,0:T(8,128)S(1)}, s32[32,64,1024]{2,1,0:T(8,128)}, u32[]{:S(2)}) copy-start(s32[32,64,1024]{2,1,0:T(8,128)} %density_ref.3) | copy-start | bytes 25165828
  2.0 23.6 %copy-start.6 = (f32[4,4]{1,0:T(4,128)S(1)}, f32[4,4]{1,0:T(4,128)}, u32[]{:S(2)}) copy-start(f32[4,4]{1,0:T(4,128)} %coeff_ref.7) | copy-start | bytes 196
  2.0 23.6 %collective-permute-start = (bf16[64,1024]{1,0:T(8,128)(2,1)S(1)}, bf16[64,1024]{1,0:T(8,128)(2,1)S(1)}, u32[]{:S(2)}, u32[]{:S(2)}) collective-permute-start(bf16[64,1024]{1,0:T(8,128)(2,1)S(1)} %get-tuple-element.25), channel_id=1, source_target_pairs={{0,8},{8,16},{16,24},{1,9},{9,17},{17,25},{2,10},{10,18},{18,26},{... | collective-permute-start | bytes 393224 | tf_op jit(solution)/shard_map/ppermute | solution.py:528
  6.0 19.6 %collective-permute-start.1 = (bf16[64,1024]{1,0:T(8,128)(2,1)S(1)}, bf16[64,1024]{1,0:T(8,128)(2,1)S(1)}, u32[]{:S(2)}, u32[]{:S(2)}) collective-permute-start(bf16[64,1024]{1,0:T(8,128)(2,1)S(1)} %get-tuple-element.26), channel_id=1, source_target_pairs={{8,0},{16,8},{24,16},{9,1},{17,9},{25,17},{10,2},{18,10},{26,18},{... | collective-permute-start | bytes 393224 | tf_op jit(solution)/shard_map/ppermute | solution.py:529
  7.9 17.7 %collective-permute-start.2 = (bf16[32,1024]{1,0:T(8,128)(2,1)S(1)}, bf16[32,1024]{1,0:T(8,128)(2,1)S(1)}, u32[]{:S(2)}, u32[]{:S(2)}) collective-permute-start(bf16[32,1024]{1,0:T(8,128)(2,1)S(1)} %get-tuple-element.27), channel_id=1, source_target_pairs={{0,1},{1,2},{2,3},{3,4},{4,5},{5,6},{6,7},{8,9},{9,10},{10,11},{11... | collective-permute-start | bytes 196616 | tf_op jit(solution)/shard_map/ppermute | solution.py:531
  11.1 14.6 %collective-permute-start.3 = (bf16[32,1024]{1,0:T(8,128)(2,1)S(1)}, bf16[32,1024]{1,0:T(8,128)(2,1)S(1)}, u32[]{:S(2)}, u32[]{:S(2)}) collective-permute-start(bf16[32,1024]{1,0:T(8,128)(2,1)S(1)} %get-tuple-element.28), channel_id=1, source_target_pairs={{1,0},{2,1},{3,2},{4,3},{5,4},{6,5},{7,6},{9,8},{10,9},{11,10},{12... | collective-permute-start | bytes 196616 | tf_op jit(solution)/shard_map/ppermute | solution.py:532
  18.3 2.4 %copy-start.1 = (f32[34,4,80,128]{3,2,1,0:T(8,128)}, f32[34,4,80,128]{3,2,1,0:T(8,128)S(1)}, u32[]{:S(2)}) copy-start(f32[34,4,80,128]{3,2,1,0:T(8,128)S(1)} %get-tuple-element.24.packed_ref) | copy-start | bytes 16711684
  20.8 2.5 %copy-start.2 = (f32[34,4,80,128]{3,2,1,0:T(8,128)}, f32[34,4,80,128]{3,2,1,0:T(8,128)S(1)}, u32[]{:S(2)}) copy-start(f32[34,4,80,128]{3,2,1,0:T(8,128)S(1)} %get-tuple-element.37.packed_ref) | copy-start | bytes 16711684
  23.2 2.4 %copy-start.4 = (f32[34,4,80,128]{3,2,1,0:T(8,128)}, f32[34,4,80,128]{3,2,1,0:T(8,128)S(1)}, u32[]{:S(2)}) copy-start(f32[34,4,80,128]{3,2,1,0:T(8,128)S(1)} %get-tuple-element.29.packed_ref) | copy-start | bytes 16711684
  25.7 26.9 %slice-start = ((s8[5570560]{0:T(1024)(128)(4,1)}), s8[1376256]{0:T(1024)(128)(4,1)S(1)}, s32[]{:S(2)}) async-start(s8[5570560]{0:T(1024)(128)(4,1)} %bitcast.11), calls=%async_computation | async-start | bytes 2752512
  32.1 9.3 %collective-permute-start.4 = (f32[8,2,64,128]{3,2,1,0:T(8,128)S(1)}, f32[8,2,64,128]{3,2,1,0:T(8,128)S(1)}, u32[]{:S(2)}, u32[]{:S(2)}) collective-permute-start(f32[8,2,64,128]{3,2,1,0:T(8,128)S(1)} %get-tuple-element.31.token_ref), channel_id=1, source_target_pairs={{0,8},{8,0},{16,24},{24,16},{1,9},{9,1},{17,25},{25,17},{2,10},{10... | collective-permute-start | bytes 1572872 | tf_op jit(solution)/shard_map/ppermute | solution.py:37
  32.2 12.5 %copy-start.3 = (f32[34,4,80,128]{3,2,1,0:T(8,128)S(1)}, f32[34,4,80,128]{3,2,1,0:T(8,128)}, u32[]{:S(2)}) copy-start(f32[34,4,80,128]{3,2,1,0:T(8,128)} %copy-done.2) | copy-start | bytes 16711684
  32.3 2.7 %copy-start.5 = (f32[34,4,80,128]{3,2,1,0:T(8,128)S(1)}, f32[34,4,80,128]{3,2,1,0:T(8,128)}, u32[]{:S(2)}) copy-start(f32[34,4,80,128]{3,2,1,0:T(8,128)} %copy-done.4) | copy-start | bytes 16711684
  35.0 17.5 %slice-start.1 = ((s8[5570560]{0:T(1024)(128)(4,1)}), s8[4194304]{0:T(1024)(128)(4,1)S(1)}, s32[]{:S(2)}) async-start(s8[5570560]{0:T(1024)(128)(4,1)} %bitcast.11), calls=%async_computation.1 | async-start | bytes 8388608
  42.2 9.2 %collective-permute-start.5 = (f32[4,2,64,128]{3,2,1,0:T(8,128)S(1)}, f32[4,2,64,128]{3,2,1,0:T(8,128)S(1)}, u32[]{:S(2)}, u32[]{:S(2)}) collective-permute-start(f32[4,2,64,128]{3,2,1,0:T(8,128)S(1)} %get-tuple-element.33.token_ref), channel_id=1, source_target_pairs={{0,16},{16,0},{8,24},{24,8},{1,17},{17,1},{9,25},{25,9},{2,18},{18... | collective-permute-start | bytes 786440 | tf_op jit(solution)/shard_map/ppermute | solution.py:37
  51.0 7.9 %collective-permute-start.6 = (f32[8,2,64,128]{3,2,1,0:T(8,128)S(1)}, f32[8,2,64,128]{3,2,1,0:T(8,128)S(1)}, u32[]{:S(2)}, u32[]{:S(2)}) collective-permute-start(f32[8,2,64,128]{3,2,1,0:T(8,128)S(1)} %get-tuple-element.38), channel_id=1, source_target_pairs={{0,8},{8,0},{16,24},{24,16},{1,9},{9,1},{17,25},{25,17},{2,10},{10... | collective-permute-start | bytes 1572872 | tf_op jit(solution)/shard_map/ppermute | solution.py:37
  51.5 7.5 %collective-permute-start.7 = (f32[4,2,64,128]{3,2,1,0:T(8,128)S(1)}, f32[4,2,64,128]{3,2,1,0:T(8,128)S(1)}, u32[]{:S(2)}, u32[]{:S(2)}) collective-permute-start(f32[4,2,64,128]{3,2,1,0:T(8,128)S(1)} %get-tuple-element.39), channel_id=1, source_target_pairs={{0,16},{16,0},{8,24},{24,8},{1,17},{17,1},{9,25},{25,9},{2,18},{18... | collective-permute-start | bytes 786440 | tf_op jit(solution)/shard_map/ppermute | solution.py:37
  60.1 6.1 %collective-permute-start.8 = (f32[64,128]{1,0:T(8,128)S(1)}, f32[64,128]{1,0:T(8,128)S(1)}, u32[]{:S(2)}, u32[]{:S(2)}) collective-permute-start(f32[64,128]{1,0:T(8,128)S(1)} %get-tuple-element.41), channel_id=1, source_target_pairs={{0,8},{8,16},{16,24},{1,9},{9,17},{17,25},{2,10},{10,18},{18,26},{... | collective-permute-start | bytes 98312 | tf_op jit(solution)/shard_map/ppermute | solution.py:574
  64.2 5.2 %collective-permute-start.9 = (f32[64,128]{1,0:T(8,128)S(1)}, f32[64,128]{1,0:T(8,128)S(1)}, u32[]{:S(2)}, u32[]{:S(2)}) collective-permute-start(f32[64,128]{1,0:T(8,128)S(1)} %get-tuple-element.42), channel_id=1, source_target_pairs={{8,0},{16,8},{24,16},{9,1},{17,9},{25,17},{10,2},{18,10},{26,18},{... | collective-permute-start | bytes 98312 | tf_op jit(solution)/shard_map/ppermute | solution.py:574
  69.4 18.9 %collective-permute-start.10 = (f32[17,8,128]{2,1,0:T(8,128)S(1)}, f32[17,8,128]{2,1,0:T(8,128)S(1)}, u32[]{:S(2)}, u32[]{:S(2)}) collective-permute-start(f32[17,8,128]{2,1,0:T(8,128)S(1)} %pad_maximum_fusion), channel_id=1, source_target_pairs={{0,1},{1,2},{2,3},{3,4},{4,5},{5,6},{6,7},{8,9},{9,10},{10,11},{11... | collective-permute-start | bytes 208904 | tf_op jit(solution)/shard_map/ppermute | solution.py:583
  71.7 16.7 %collective-permute-start.11 = (f32[17,8,128]{2,1,0:T(8,128)S(1)}, f32[17,8,128]{2,1,0:T(8,128)S(1)}, u32[]{:S(2)}, u32[]{:S(2)}) collective-permute-start(f32[17,8,128]{2,1,0:T(8,128)S(1)} %pad_maximum_fusion.1), channel_id=1, source_target_pairs={{1,0},{2,1},{3,2},{4,3},{5,4},{6,5},{7,6},{9,8},{10,9},{11,10},{12... | collective-permute-start | bytes 208904 | tf_op jit(solution)/shard_map/ppermute | solution.py:584

commit v5 on v3

--- a/solution.py
+++ b/solution.py
@@ -18,7 +18,7 @@
 DEPTH_W = 20.0
 NORMAL_W = 2.0
 CENTRE = 127.5
-AHEAD = 8
+AHEAD = 4
 
 
 def shifts(axis):
@@ -131,7 +131,8 @@
         coeffs.append([coeff_ref[row, k] * (scale / CENTRE**k) for k in range(4)])
     sign = jnp.where(flip == 1, 1.0, -1.0)
     rate = sign * OPACITY
-    lx, ly, lz = (0.65 * v for v in LIGHT)
+    lx, ly = LIGHT[0] / LIGHT[2], LIGHT[1] / LIGHT[2]
+    ambient = 0.35 / (0.65 * LIGHT[2])
     lane = lax.broadcasted_iota(jnp.int32, (SUB, LANES), 1)
     first_lane = lane == 0
     last_lane = lane == LANES - 1
@@ -197,7 +198,7 @@
             gy = (up - field[z, j, pl.ds(r + SUB - 1, SUB), :]).astype(jnp.float32)
             gz = above - below
             norm = lax.rsqrt(gx * gx + gy * gy + (gz * gz + 255.0 * 255.0))
-            shade = 0.35 + jnp.abs((lx * gx + ly * gy + lz * gz) * norm)
+            shade = ambient + jnp.abs((lx * gx + ly * gy + gz) * norm)
             tau = tau + jnp.log2(1.0 + jnp.exp2(poly(coeffs[0], here)))
             following = jnp.exp2(rate * tau)
             weight = following - factor
@@ -215,7 +216,7 @@
         scale = jnp.where(flipped, inverse, -1.0)
         out = pl.ds(r, SUB)
         for k in range(3):
-            out_ref[k, j - 1, out, :] = sums[k] * scale
+            out_ref[k, j - 1, out, :] = sums[k] * (scale * (0.65 * LIGHT[2]))
             out_ref[k + 5, j - 1, out, :] = sums[k + 3] * scale
         out_ref[3, j - 1, out, :] = 1.0 - jnp.where(flipped, inverse, factor)
         out_ref[4, j - 1, out, :] = (h_last * factor - h_first - delta * between) * scale
@@ -302,7 +303,7 @@
     lane = lax.broadcasted_iota(jnp.int32, (SUB, LANES), 1)
 
     def shift_setup(index):
-        offset = index - RADIUS
+        offset = index - RADIUS + (index >= RADIUS).astype(jnp.int32)
         run = offset.astype(jnp.float32)
         spread = -(SPATIAL * LOG2E) * run * run
         border = jnp.where(offset < 0, LANES + offset, offset)
@@ -317,16 +318,6 @@
         result = pltpu.roll(mixed, amount, 1)
         return result + spread if k == 0 else result
 
-    def first_shift(k, carry):
-        other, amount, take_other, spread = shift_setup(jnp.int32(0))
-        for j in range(tiles):
-            for n in needed:
-                mixed = jnp.where(take_other, feats[k, j + other, at(n), :], feats[k, j + 1, at(n), :])
-                result = pltpu.roll(mixed, amount, 1)
-                buf_a[k, j, at(n), :] = result + jnp.where(k == 0, spread, 0.0)
-        return carry
-
-    lax.fori_loop(0, 8, first_shift, 0)
     for k in range(4):
         for j in range(tiles):
             for b in chosen:
@@ -334,7 +325,7 @@
 
     offsets = sorted({o for b in chosen for o in range(SUB * b - RADIUS, SUB * b + RADIUS + 1)})
 
-    def taps(buf, next_index, next_buf):
+    def taps(buf, side, next_index, next_buf):
         pending, items = [], []
         if next_buf is not None:
             setup = shift_setup(next_index)
@@ -353,7 +344,7 @@
             own, sums = {}, {}
             for o in offsets:
                 pump()
-                q = [buf[k, j, pl.ds(SUB + o, SUB), :] for k in range(8)]
+                q = [buf[k, j + side, pl.ds(SUB + o, SUB), :] for k in range(8)]
                 for b in chosen:
                     dy = o - SUB * b
                     if abs(dy) > RADIUS:
@@ -376,12 +367,12 @@
             pump(not items)
 
     def pair(step, carry):
-        taps(buf_a, 2 * step + 1, buf_b)
-        taps(buf_b, 2 * step + 2, buf_a)
+        taps(buf_a, 0, 2 * step + 1, buf_b)
+        taps(buf_b, 0, jnp.minimum(2 * step + 2, 2 * RADIUS - 1), buf_a)
         return carry
 
+    taps(feats, 1, jnp.int32(0), buf_a)
     lax.fori_loop(0, RADIUS, pair, 0)
-    taps(buf_a, None, None)
 
     if not inner:
         for k in range(3):

time: 89 us -> 87.3 us (0.981)
  Pallas kernels: 54.8 us -> 53.1 us
    pallas_call x2, Pallas kernels: 19 us -> 17.7 us  [shade(): pl.pallas_call(functools.partial(shade_kernel, inner), out_shape=jax.Shap...]
where the time goes in v5:
time: 87.3 us; the launch traced here: 85.8 us
  Pallas kernels  53.1 us (61%)
  starting transfers between devices  27.1 us (31%)
  waiting for transfers between devices  4.58 us (5%)
  between operations  0.9 us (1%)
    pallas_call x4, Pallas kernels, integrate(): pl.pallas_call(functools.partial(integrate_kernel, place, own), out_shape...  31.6 us
    pallas_call x2, Pallas kernels, shade(): pl.pallas_call(functools.partial(shade_kernel, inner), out_shape=jax.Shap...  17.7 us
    ppermute x2, starting transfers between devices, per_device(): halo = lax.ppermute(last, 'depth', up) + lax.ppermute(first, 'depth', down)  5.62 us
    ppermute x1, starting transfers between devices, per_device(): bottom = lax.ppermute(band(0), 'tile', down)  3.96 us
    ppermute x1, starting transfers between devices, per_device(): zlo = lax.ppermute(last_plane, 'depth', up)  3.71 us
    ppermute x4, starting transfers between devices, swapped(): return lax.ppermute(block, axis, route)  3.68 us
    ppermute x2, waiting for transfers between devices, per_device(): halo = lax.ppermute(last, 'depth', up) + lax.ppermute(first, 'depth', down)  3.28 us
    ppermute x1, starting transfers between devices, per_device(): ylo = lax.ppermute(last_line, 'tile', up)  3.12 us
  transfers between devices with their start and end apart: 12, of which 2 were waited for; matrix products, arithmetic and copies ran while one was open for 0% of the time, Pallas kernels for 42%

profile of v5, /device:TPU:9, one launch (start us, length us, event | category | flops | bytes accessed | tf_op | source)
XLA Modules:
  0.0 85.8 jit_solution(803657088133156300)
XLA Ops:
  0.0 1.9 %edges.1 = (bf16[64,1024]{1,0:T(8,128)(2,1)S(1)}, bf16[64,1024]{1,0:T(8,128)(2,1)S(1)}, bf16[32,1024]{1,0:T(8,128)(2,1)S(1)}, bf16[32,1024]{1,0:T(8,128)(2,1)S(1)}) custom-call(s32[32,64,1024]{2,1,0:T(8,128)} %density_ref.9), custom_call_target="tpu_custom_call" | custom-call | tf_op jit(solution)/shard_map/edges/pallas_call | solution.py:75
  1.9 3.7 %collective-permute-start = (bf16[64,1024]{1,0:T(8,128)(2,1)S(1)}, bf16[64,1024]{1,0:T(8,128)(2,1)S(1)}, u32[]{:S(2)}, u32[]{:S(2)}) collective-permute-start(bf16[64,1024]{1,0:T(8,128)(2,1)S(1)} %get-tuple-element.16), channel_id=1, source_target_pairs={{0,8},{8,16},{16,24},{1,9},{9,17},{17,25},{2,10},{10,18},{18,26},{... | collective-permute-start | bytes 393224 | tf_op jit(solution)/shard_map/ppermute | solution.py:504
  5.6 1.9 %collective-permute-start.1 = (bf16[64,1024]{1,0:T(8,128)(2,1)S(1)}, bf16[64,1024]{1,0:T(8,128)(2,1)S(1)}, u32[]{:S(2)}, u32[]{:S(2)}) collective-permute-start(bf16[64,1024]{1,0:T(8,128)(2,1)S(1)} %get-tuple-element.17), channel_id=1, source_target_pairs={{8,0},{16,8},{24,16},{9,1},{17,9},{25,17},{10,2},{18,10},{26,18},{... | collective-permute-start | bytes 393224 | tf_op jit(solution)/shard_map/ppermute | solution.py:505
  7.5 3.1 %collective-permute-start.2 = (bf16[32,1024]{1,0:T(8,128)(2,1)S(1)}, bf16[32,1024]{1,0:T(8,128)(2,1)S(1)}, u32[]{:S(2)}, u32[]{:S(2)}) collective-permute-start(bf16[32,1024]{1,0:T(8,128)(2,1)S(1)} %get-tuple-element.18), channel_id=1, source_target_pairs={{0,1},{1,2},{2,3},{3,4},{4,5},{5,6},{6,7},{8,9},{9,10},{10,11},{11... | collective-permute-start | bytes 196616 | tf_op jit(solution)/shard_map/ppermute | solution.py:507
  10.6 3.1 %collective-permute-start.3 = (bf16[32,1024]{1,0:T(8,128)(2,1)S(1)}, bf16[32,1024]{1,0:T(8,128)(2,1)S(1)}, u32[]{:S(2)}, u32[]{:S(2)}) collective-permute-start(bf16[32,1024]{1,0:T(8,128)(2,1)S(1)} %get-tuple-element.19), channel_id=1, source_target_pairs={{1,0},{2,1},{3,2},{4,3},{5,4},{6,5},{7,6},{9,8},{10,9},{11,10},{12... | collective-permute-start | bytes 196616 | tf_op jit(solution)/shard_map/ppermute | solution.py:508
  14.4 0.0 collective-permute-done.2.ylo_ref
  14.4 1.3 %collective-permute-done.3.yhi_ref = bf16[32,1024]{1,0:T(8,128)(2,1)S(1)} collective-permute-done((bf16[32,1024]{1,0:T(8,128)(2,1)S(1)}, bf16[32,1024]{1,0:T(8,128)(2,1)S(1)}, u32[]{:S(2)}, u32[]{:S(2)}) %collective-permute-start.3) | collective-permute-done | bytes 65568 | tf_op jit(solution)/shard_map/ppermute | solution.py:508
  15.7 0.0 collective-permute-done.zlo_ref.token_ref
  15.7 0.0 collective-permute-done.1.zhi_ref
  15.7 7.9 %integrate.4.token_ref = f32[8,2,64,128]{3,2,1,0:T(8,128)S(1)} custom-call(s32[1]{0:T(128)} %copy.4.flip_ref, f32[4,4]{1,0:T(4,128)S(1)} %copy-done, s32[32,64,1024]{2,1,0:T(8,128)} %density_ref.9, bf16[64,1024]{1,0:T(8,128)(2,1)S(1)} %collective-permute-done.zlo_ref.token_ref, bf16[64,1024]{1,0:T(8,128)(2,1)S(1)} %collective-permute-done.1.zhi_ref, ...), custom_call_target="tpu_custom_call" | custom-call | flops 36700160 | bytes 4194304 | tf_op jit(solution)/shard_map/integrate/pallas_call | solution.py:234
  23.5 0.1 collective-permute-start.4
  23.7 0.1 add_convert_fusion.leads_ref
  23.7 7.9 %integrate.5.refs_0_ = f32[8,2,64,128]{3,2,1,0:T(8,128)S(1)} custom-call(s32[1]{0:T(128)} %copy.4.flip_ref, f32[4,4]{1,0:T(4,128)S(1)} %copy-done, s32[32,64,1024]{2,1,0:T(8,128)} %density_ref.9, bf16[64,1024]{1,0:T(8,128)(2,1)S(1)} %collective-permute-done.zlo_ref.token_ref, bf16[64,1024]{1,0:T(8,128)(2,1)S(1)} %collective-permute-done.1.zhi_ref, ...), custom_call_target="tpu_custom_call" | custom-call | flops 36700160 | bytes 4194304 | tf_op jit(solution)/shard_map/integrate/pallas_call | solution.py:234
  31.7 0.0 collective-permute-done.4.refs_1_
  31.7 0.8 compose.2
  32.6 3.2 %collective-permute-start.5 = (f32[4,2,64,128]{3,2,1,0:T(8,128)S(1)}, f32[4,2,64,128]{3,2,1,0:T(8,128)S(1)}, u32[]{:S(2)}, u32[]{:S(2)}) collective-permute-start(f32[4,2,64,128]{3,2,1,0:T(8,128)S(1)} %get-tuple-element.20.token_ref), channel_id=1, source_target_pairs={{0,16},{16,0},{8,24},{24,8},{1,17},{17,1},{9,25},{25,9},{2,18},{18... | collective-permute-start | bytes 786440 | tf_op jit(solution)/shard_map/ppermute | solution.py:37
  35.7 7.9 %integrate.7 = f32[8,2,64,128]{3,2,1,0:T(8,128)S(1)} custom-call(s32[1]{0:T(128)} %copy.4.flip_ref, f32[4,4]{1,0:T(4,128)S(1)} %copy-done, s32[32,64,1024]{2,1,0:T(8,128)} %density_ref.9, bf16[64,1024]{1,0:T(8,128)(2,1)S(1)} %collective-permute-done.zlo_ref.token_ref, bf16[64,1024]{1,0:T(8,128)(2,1)S(1)} %collective-permute-done.1.zhi_ref, ...), custom_call_target="tpu_custom_call" | custom-call | flops 36700160 | bytes 4194304 | tf_op jit(solution)/shard_map/integrate/pallas_call | solution.py:234
  43.7 0.4 collective-permute-start.6
  44.1 0.0 collective-permute-done.5.token_ref.refs_2_
  44.1 0.0 collective-permute-start.7
  44.1 7.9 %integrate.6.refs_0_ = f32[8,2,64,128]{3,2,1,0:T(8,128)S(1)} custom-call(s32[1]{0:T(128)} %copy.4.flip_ref, f32[4,4]{1,0:T(4,128)S(1)} %copy-done, s32[32,64,1024]{2,1,0:T(8,128)} %density_ref.9, bf16[64,1024]{1,0:T(8,128)(2,1)S(1)} %collective-permute-done.zlo_ref.token_ref, bf16[64,1024]{1,0:T(8,128)(2,1)S(1)} %collective-permute-done.1.zhi_ref, ...), custom_call_target="tpu_custom_call" | custom-call | flops 36700160 | bytes 4194304 | tf_op jit(solution)/shard_map/integrate/pallas_call | solution.py:234
  52.0 0.0 collective-permute-done.6.refs_1_
  52.0 1.1 %compose.3 = (f32[8,2,64,128]{3,2,1,0:T(8,128)S(1)}, f32[64,128]{1,0:T(8,128)S(1)}, f32[64,128]{1,0:T(8,128)S(1)}) custom-call(s32[2]{0:T(128)S(1)} %add_convert_fusion.leads_ref, f32[8,2,64,128]{3,2,1,0:T(8,128)S(1)} %integrate.6.refs_0_, f32[8,2,64,128]{3,2,1,0:T(8,128)S(1)} %collective-permute-done.6.refs_1_, ...), custom_call_target="tpu_custom_call" | custom-call | bytes 524288 | tf_op jit(solution)/shard_map/compose/pallas_call | solution.py:475
  53.1 3.7 %collective-permute-start.8 = (f32[64,128]{1,0:T(8,128)S(1)}, f32[64,128]{1,0:T(8,128)S(1)}, u32[]{:S(2)}, u32[]{:S(2)}) collective-permute-start(f32[64,128]{1,0:T(8,128)S(1)} %get-tuple-element.25), channel_id=1, source_target_pairs={{0,8},{8,16},{16,24},{1,9},{9,17},{17,25},{2,10},{10,18},{18,26},{... | collective-permute-start | bytes 98312 | tf_op jit(solution)/shard_map/ppermute | solution.py:547
  56.8 1.9 %collective-permute-start.9 = (f32[64,128]{1,0:T(8,128)S(1)}, f32[64,128]{1,0:T(8,128)S(1)}, u32[]{:S(2)}, u32[]{:S(2)}) collective-permute-start(f32[64,128]{1,0:T(8,128)S(1)} %get-tuple-element.26), channel_id=1, source_target_pairs={{8,0},{16,8},{24,16},{9,1},{17,9},{25,17},{10,2},{18,10},{26,18},{... | collective-permute-start | bytes 98312 | tf_op jit(solution)/shard_map/ppermute | solution.py:547
  58.8 0.0 collective-permute-done.8
  58.8 3.3 %collective-permute-done.9 = f32[64,128]{1,0:T(8,128)S(1)} collective-permute-done((f32[64,128]{1,0:T(8,128)S(1)}, f32[64,128]{1,0:T(8,128)S(1)}, u32[]{:S(2)}, u32[]{:S(2)}) %collective-permute-start.9) | collective-permute-done | bytes 32800 | tf_op jit(solution)/shard_map/ppermute | solution.py:547
  62.1 4.0 %collective-permute-start.11 = (f32[17,8,128]{2,1,0:T(8,128)S(1)}, f32[17,8,128]{2,1,0:T(8,128)S(1)}, u32[]{:S(2)}, u32[]{:S(2)}) collective-permute-start(f32[17,8,128]{2,1,0:T(8,128)S(1)} %pad_maximum_fusion.1), channel_id=1, source_target_pairs={{1,0},{2,1},{3,2},{4,3},{5,4},{6,5},{7,6},{9,8},{10,9},{11,10},{12... | collective-permute-start | bytes 208904 | tf_op jit(solution)/shard_map/ppermute | solution.py:557
  66.1 2.0 %collective-permute-start.10 = (f32[17,8,128]{2,1,0:T(8,128)S(1)}, f32[17,8,128]{2,1,0:T(8,128)S(1)}, u32[]{:S(2)}, u32[]{:S(2)}) collective-permute-start(f32[17,8,128]{2,1,0:T(8,128)S(1)} %pad_maximum_fusion), channel_id=1, source_target_pairs={{0,1},{1,2},{2,3},{3,4},{4,5},{5,6},{6,7},{8,9},{9,10},{10,11},{11... | collective-permute-start | bytes 208904 | tf_op jit(solution)/shard_map/ppermute | solution.py:556
  68.1 11.9 %shade_inner.1.rest_2_ = f32[3,64,256]{2,1,0:T(8,128)S(1)} custom-call(f32[8,2,64,128]{3,2,1,0:T(8,128)S(1)} %get-tuple-element.24.core_ref, f32[64,128]{1,0:T(8,128)S(1)} %add.14.halo_ref), custom_call_target="tpu_custom_call" | custom-call | flops 56819712 | bytes 524288 | tf_op jit(solution)/shard_map/shade_inner/pallas_call | solution.py:400
  80.1 0.0 collective-permute-done.10.rest_0_
  80.1 5.7 %shade_outer.1 = f32[3,64,256]{2,1,0:T(8,128)} custom-call(f32[8,2,64,128]{3,2,1,0:T(8,128)S(1)} %get-tuple-element.24.core_ref, f32[64,128]{1,0:T(8,128)S(1)} %add.14.halo_ref, f32[17,8,128]{2,1,0:T(8,128)S(1)} %collective-permute-done.10.rest_0_, f32[17,8,128]{2,1,0:T(8,128)S(1)} %collective-permute-done.11.rest_1_, f32[3,64,256]{2,1,0:T(8,128)S(1)} %shade_inner.1.rest_2_), custom_call_target="tpu_custom_call" | custom-call | flops 18939904 | bytes 524288 | tf_op jit(solution)/shard_map/shade_outer/pallas_call | solution.py:400
  (9 shorter events, 0.0 us)
Async XLA Ops:
  0.0 15.7 %copy-start = (f32[4,4]{1,0:T(4,128)S(1)}, f32[4,4]{1,0:T(4,128)}, u32[]{:S(2)}) copy-start(f32[4,4]{1,0:T(4,128)} %coeff_ref.7) | copy-start | bytes 196
  1.9 13.8 %collective-permute-start = (bf16[64,1024]{1,0:T(8,128)(2,1)S(1)}, bf16[64,1024]{1,0:T(8,128)(2,1)S(1)}, u32[]{:S(2)}, u32[]{:S(2)}) collective-permute-start(bf16[64,1024]{1,0:T(8,128)(2,1)S(1)} %get-tuple-element.16), channel_id=1, source_target_pairs={{0,8},{8,16},{16,24},{1,9},{9,17},{17,25},{2,10},{10,18},{18,26},{... | collective-permute-start | bytes 393224 | tf_op jit(solution)/shard_map/ppermute | solution.py:504
  5.6 10.1 %collective-permute-start.1 = (bf16[64,1024]{1,0:T(8,128)(2,1)S(1)}, bf16[64,1024]{1,0:T(8,128)(2,1)S(1)}, u32[]{:S(2)}, u32[]{:S(2)}) collective-permute-start(bf16[64,1024]{1,0:T(8,128)(2,1)S(1)} %get-tuple-element.17), channel_id=1, source_target_pairs={{8,0},{16,8},{24,16},{9,1},{17,9},{25,17},{10,2},{18,10},{26,18},{... | collective-permute-start | bytes 393224 | tf_op jit(solution)/shard_map/ppermute | solution.py:505
  7.5 6.8 %collective-permute-start.2 = (bf16[32,1024]{1,0:T(8,128)(2,1)S(1)}, bf16[32,1024]{1,0:T(8,128)(2,1)S(1)}, u32[]{:S(2)}, u32[]{:S(2)}) collective-permute-start(bf16[32,1024]{1,0:T(8,128)(2,1)S(1)} %get-tuple-element.18), channel_id=1, source_target_pairs={{0,1},{1,2},{2,3},{3,4},{4,5},{5,6},{6,7},{8,9},{9,10},{10,11},{11... | collective-permute-start | bytes 196616 | tf_op jit(solution)/shard_map/ppermute | solution.py:507
  10.6 5.0 %collective-permute-start.3 = (bf16[32,1024]{1,0:T(8,128)(2,1)S(1)}, bf16[32,1024]{1,0:T(8,128)(2,1)S(1)}, u32[]{:S(2)}, u32[]{:S(2)}) collective-permute-start(bf16[32,1024]{1,0:T(8,128)(2,1)S(1)} %get-tuple-element.19), channel_id=1, source_target_pairs={{1,0},{2,1},{3,2},{4,3},{5,4},{6,5},{7,6},{9,8},{10,9},{11,10},{12... | collective-permute-start | bytes 196616 | tf_op jit(solution)/shard_map/ppermute | solution.py:508
  23.5 8.2 %collective-permute-start.4 = (f32[8,2,64,128]{3,2,1,0:T(8,128)S(1)}, f32[8,2,64,128]{3,2,1,0:T(8,128)S(1)}, u32[]{:S(2)}, u32[]{:S(2)}) collective-permute-start(f32[8,2,64,128]{3,2,1,0:T(8,128)S(1)} %integrate.4.token_ref), channel_id=1, source_target_pairs={{0,8},{8,0},{16,24},{24,16},{1,9},{9,1},{17,25},{25,17},{2,10},{10... | collective-permute-start | bytes 1572872 | tf_op jit(solution)/shard_map/ppermute | solution.py:37
  32.6 11.6 %collective-permute-start.5 = (f32[4,2,64,128]{3,2,1,0:T(8,128)S(1)}, f32[4,2,64,128]{3,2,1,0:T(8,128)S(1)}, u32[]{:S(2)}, u32[]{:S(2)}) collective-permute-start(f32[4,2,64,128]{3,2,1,0:T(8,128)S(1)} %get-tuple-element.20.token_ref), channel_id=1, source_target_pairs={{0,16},{16,0},{8,24},{24,8},{1,17},{17,1},{9,25},{25,9},{2,18},{18... | collective-permute-start | bytes 786440 | tf_op jit(solution)/shard_map/ppermute | solution.py:37
  43.7 8.3 %collective-permute-start.6 = (f32[8,2,64,128]{3,2,1,0:T(8,128)S(1)}, f32[8,2,64,128]{3,2,1,0:T(8,128)S(1)}, u32[]{:S(2)}, u32[]{:S(2)}) collective-permute-start(f32[8,2,64,128]{3,2,1,0:T(8,128)S(1)} %integrate.7), channel_id=1, source_target_pairs={{0,8},{8,0},{16,24},{24,16},{1,9},{9,1},{17,25},{25,17},{2,10},{10... | collective-permute-start | bytes 1572872 | tf_op jit(solution)/shard_map/ppermute | solution.py:37
  44.1 7.9 %collective-permute-start.7 = (f32[4,2,64,128]{3,2,1,0:T(8,128)S(1)}, f32[4,2,64,128]{3,2,1,0:T(8,128)S(1)}, u32[]{:S(2)}, u32[]{:S(2)}) collective-permute-start(f32[4,2,64,128]{3,2,1,0:T(8,128)S(1)} %get-tuple-element.23), channel_id=1, source_target_pairs={{0,16},{16,0},{8,24},{24,8},{1,17},{17,1},{9,25},{25,9},{2,18},{18... | collective-permute-start | bytes 786440 | tf_op jit(solution)/shard_map/ppermute | solution.py:37
  53.1 5.7 %collective-permute-start.8 = (f32[64,128]{1,0:T(8,128)S(1)}, f32[64,128]{1,0:T(8,128)S(1)}, u32[]{:S(2)}, u32[]{:S(2)}) collective-permute-start(f32[64,128]{1,0:T(8,128)S(1)} %get-tuple-element.25), channel_id=1, source_target_pairs={{0,8},{8,16},{16,24},{1,9},{9,17},{17,25},{2,10},{10,18},{18,26},{... | collective-permute-start | bytes 98312 | tf_op jit(solution)/shard_map/ppermute | solution.py:547
  56.8 5.2 %collective-permute-start.9 = (f32[64,128]{1,0:T(8,128)S(1)}, f32[64,128]{1,0:T(8,128)S(1)}, u32[]{:S(2)}, u32[]{:S(2)}) collective-permute-start(f32[64,128]{1,0:T(8,128)S(1)} %get-tuple-element.26), channel_id=1, source_target_pairs={{8,0},{16,8},{24,16},{9,1},{17,9},{25,17},{10,2},{18,10},{26,18},{... | collective-permute-start | bytes 98312 | tf_op jit(solution)/shard_map/ppermute | solution.py:547
  62.1 18.0 %collective-permute-start.11 = (f32[17,8,128]{2,1,0:T(8,128)S(1)}, f32[17,8,128]{2,1,0:T(8,128)S(1)}, u32[]{:S(2)}, u32[]{:S(2)}) collective-permute-start(f32[17,8,128]{2,1,0:T(8,128)S(1)} %pad_maximum_fusion.1), channel_id=1, source_target_pairs={{1,0},{2,1},{3,2},{4,3},{5,4},{6,5},{7,6},{9,8},{10,9},{11,10},{12... | collective-permute-start | bytes 208904 | tf_op jit(solution)/shard_map/ppermute | solution.py:557
  66.1 14.0 %collective-permute-start.10 = (f32[17,8,128]{2,1,0:T(8,128)S(1)}, f32[17,8,128]{2,1,0:T(8,128)S(1)}, u32[]{:S(2)}, u32[]{:S(2)}) collective-permute-start(f32[17,8,128]{2,1,0:T(8,128)S(1)} %pad_maximum_fusion), channel_id=1, source_target_pairs={{0,1},{1,2},{2,3},{3,4},{4,5},{5,6},{6,7},{8,9},{9,10},{10,11},{11... | collective-permute-start | bytes 208904 | tf_op jit(solution)/shard_map/ppermute | solution.py:556

commit v6 on v5

--- a/solution.py
+++ b/solution.py
@@ -88,17 +88,16 @@
     )(density)
 
 
-def integrate_kernel(
-    place, own, flip_ref, coeff_ref, density_ref, zlo_ref, zhi_ref, ylo_ref, yhi_ref, token_ref,
-    out_ref, field, zlo_f, zhi_f, sems,
-):
+def first_tile(place, own):
+    position = lax.axis_index("depth")
+    c, y = position % 2, position // 2 % 2
+    return (lax.rem(c + place[0], 2) + 2 * lax.rem(y + place[1], 2) + 4 * place[2]) * own
+
+
+def tile_copies(place, own, density_ref, field, sems):
     cells, rows, width = density_ref.shape
     tiles = width // LANES
-    blocks = rows // SUB
-    count = tiles // own
-    position = lax.axis_index("depth")
-    c, y = position % 2, position // 2 % 2
-    first = (lax.rem(c + place[0], 2) + 2 * lax.rem(y + place[1], 2) + 4 * place[2]) * own
+    first = first_tile(place, own)
     sources = [jnp.maximum(first - 1, 0)]
     sources += [first + j for j in range(own)]
     sources += [jnp.minimum(first + own, tiles - 1)]
@@ -111,9 +110,73 @@
             sems.at[b, j],
         )
 
-    for b in range(blocks):
+    def begin(b):
         for j in range(own + 2):
             copy(b, j).start()
+
+    def arrive(b):
+        for j in range(own + 2):
+            copy(b, j).wait()
+        at = pl.ds(SUB + b * SUB, SUB)
+
+        @pl.when(first == 0)
+        def _():
+            for z in range(cells):
+                field[z, 0, at, :] = jnp.zeros((SUB, LANES), jnp.int32)
+
+        @pl.when(first + own == tiles)
+        def _():
+            for z in range(cells):
+                field[z, own + 1, at, :] = jnp.zeros((SUB, LANES), jnp.int32)
+
+    return begin, arrive
+
+
+def stage_kernel(place, own, density_ref, field_ref, sems):
+    blocks = density_ref.shape[1] // SUB
+    begin, arrive = tile_copies(place, own, density_ref, field_ref, sems)
+    for b in range(blocks):
+        begin(b)
+    lax.fori_loop(0, blocks, lambda b, carry: arrive(b) or carry, 0)
+
+
+def stage(place, count, density):
+    cells, rows, width = density.shape
+    own = width // LANES // count
+    shape = (cells, own + 2, rows + 2 * SUB, LANES)
+    return pl.pallas_call(
+        functools.partial(stage_kernel, place, own),
+        out_shape=jax.ShapeDtypeStruct(shape, jnp.int32),
+        in_specs=[pl.BlockSpec(memory_space=pl.ANY)],
+        out_specs=pl.BlockSpec(memory_space=pltpu.VMEM),
+        scratch_shapes=[pltpu.SemaphoreType.DMA((rows // SUB, own + 2))],
+        compiler_params=pltpu.CompilerParams(vmem_limit_bytes=48 << 20),
+        cost_estimate=pl.CostEstimate(
+            flops=0, transcendentals=0, bytes_accessed=8 * cells * rows * (own + 2) * LANES
+        ),
+        name="stage",
+    )(density)
+
+
+def integrate_kernel(
+    place, own, staged, flip_ref, coeff_ref, density_ref, zlo_ref, zhi_ref, ylo_ref, yhi_ref,
+    token_ref, out_ref, *scratch,
+):
+    if staged:
+        field, (zlo_f, zhi_f, top_f, bottom_f) = token_ref, scratch
+    else:
+        field, zlo_f, zhi_f, sems = scratch
+    _, width = zlo_ref.shape
+    cells, rows = ylo_ref.shape[0], zlo_ref.shape[0]
+    tiles = width // LANES
+    blocks = rows // SUB
+    count = tiles // own
+    position = lax.axis_index("depth")
+    first = first_tile(place, own)
+    if not staged:
+        begin, arrive = tile_copies(place, own, density_ref, field, sems)
+        for b in range(blocks):
+            begin(b)
     flip = flip_ref[0]
     for j in range(own):
         cols = pl.ds(pl.multiple_of((first + j) * LANES, LANES), LANES)
@@ -121,7 +184,10 @@
         zhi_f[j] = zhi_ref[:, cols].astype(jnp.float32) - CENTRE
         top = ylo_ref[:, cols].astype(jnp.float32).astype(jnp.int32)
         bottom = yhi_ref[:, cols].astype(jnp.float32).astype(jnp.int32)
-        for z in range(cells):
+        if staged:
+            top_f[j] = top
+            bottom_f[j] = bottom
+        for z in range(0 if staged else cells):
             field[z, j + 1, SUB - 1 : SUB, :] = top[z : z + 1]
             field[z, j + 1, SUB + rows : SUB + rows + 1, :] = bottom[z : z + 1]
 
@@ -147,27 +213,16 @@
     def poly(c, t):
         return c[0] + t * (c[1] + t * (c[2] + t * c[3]))
 
-    def arrive(b):
-        for j in range(own + 2):
-            copy(b, j).wait()
-        at = pl.ds(SUB + b * SUB, SUB)
-
-        @pl.when(first == 0)
-        def _():
-            for z in range(cells):
-                field[z, 0, at, :] = jnp.zeros((SUB, LANES), jnp.int32)
-
-        @pl.when(first + own == tiles)
-        def _():
-            for z in range(cells):
-                field[z, own + 1, at, :] = jnp.zeros((SUB, LANES), jnp.int32)
-
-    arrive(0)
+    row = lax.broadcasted_iota(jnp.int32, (SUB, LANES), 0)
+    if not staged:
+        arrive(0)
 
     def block(b, carry):
-        @pl.when(b + 1 < blocks)
-        def _():
-            arrive(b + 1)
+        if not staged:
+
+            @pl.when(b + 1 < blocks)
+            def _():
+                arrive(b + 1)
 
         r = pl.multiple_of(b * SUB, SUB)
         for j in range(1, own + 1):
@@ -195,7 +250,11 @@
             right = pltpu.roll(jnp.where(first_lane, field[z, j + 1, at, :], raw), LANES - 1, 1)
             gx = (right - left).astype(jnp.float32)
             up = field[z, j, pl.ds(r + SUB + 1, SUB), :]
-            gy = (up - field[z, j, pl.ds(r + SUB - 1, SUB), :]).astype(jnp.float32)
+            down = field[z, j, pl.ds(r + SUB - 1, SUB), :]
+            if staged:
+                up = jnp.where(row + r == rows - 1, bottom_f[j - 1, z : z + 1, :], up)
+                down = jnp.where(row + r == 0, top_f[j - 1, z : z + 1, :], down)
+            gy = (up - down).astype(jnp.float32)
             gz = above - below
             norm = lax.rsqrt(gx * gx + gy * gy + (gz * gz + 255.0 * 255.0))
             shade = ambient + jnp.abs((lx * gx + ly * gy + gz) * norm)
@@ -224,30 +283,29 @@
     lax.fori_loop(0, blocks, block, 0)
 
 
-def integrate(place, count, view_flip, tf_coeff, density, zlo, zhi, ylo, yhi, token):
+def integrate(place, count, view_flip, tf_coeff, density, zlo, zhi, ylo, yhi, token, staged):
     cells, rows, width = density.shape
     own = width // LANES // count
     smem = pl.BlockSpec(memory_space=pltpu.SMEM)
     vmem = pl.BlockSpec(memory_space=pltpu.VMEM)
     anywhere = pl.BlockSpec(memory_space=pl.ANY)
     voxels = cells * rows * own * LANES
+    copied = pltpu.VMEM((cells, own + 2, rows + 2 * SUB, LANES), jnp.int32)
+    borders = [pltpu.VMEM((own, rows, LANES), jnp.float32)] * 2
+    line = pltpu.VMEM((own, cells, LANES), jnp.int32)
+    sems = pltpu.SemaphoreType.DMA((rows // SUB, own + 2))
     return pl.pallas_call(
-        functools.partial(integrate_kernel, place, own),
+        functools.partial(integrate_kernel, place, own, staged),
         out_shape=jax.ShapeDtypeStruct((8, own, rows, LANES), jnp.float32),
-        in_specs=[smem, smem, anywhere, vmem, vmem, vmem, vmem, anywhere],
+        in_specs=[smem, smem, anywhere] + [vmem] * 4 + [vmem if staged else anywhere],
         out_specs=vmem,
-        scratch_shapes=[
-            pltpu.VMEM((cells, own + 2, rows + 2 * SUB, LANES), jnp.int32),
-            pltpu.VMEM((own, rows, LANES), jnp.float32),
-            pltpu.VMEM((own, rows, LANES), jnp.float32),
-            pltpu.SemaphoreType.DMA((rows // SUB, own + 2)),
-        ],
-        compiler_params=pltpu.CompilerParams(vmem_limit_bytes=52 << 20),
+        scratch_shapes=(borders + [line, line]) if staged else ([copied] + borders + [sems]),
+        compiler_params=pltpu.CompilerParams(vmem_limit_bytes=(40 if staged else 52) << 20),
         cost_estimate=pl.CostEstimate(
             flops=70 * voxels, transcendentals=0, bytes_accessed=8 * voxels
         ),
         name="integrate",
-    )(view_flip, tf_coeff, density, zlo, zhi, ylo, yhi, token)
+    )(view_flip, tf_coeff, view_flip if staged else density, zlo, zhi, ylo, yhi, token)
 
 
 def shade_kernel(inner, core_ref, halo_ref, *rest):
@@ -508,17 +566,21 @@
     yhi = lax.ppermute(first_line, "tile", down)
 
     def quarter(core_bit, chip_bit, token):
-        parts = [
-            integrate(
-                (core_bit, chip_bit, h), count, view_flip, tf_coeff, density, zlo, zhi, ylo, yhi, token
+        parts = []
+        for h in range(high):
+            place = (core_bit, chip_bit, h)
+            given = stage(place, count, density) if token is None else token
+            parts.append(
+                integrate(
+                    place, count, view_flip, tf_coeff, density, zlo, zhi, ylo, yhi, given,
+                    token is None,
+                )
             )
-            for h in range(high)
-        ]
         return parts[0] if high == 1 else jnp.concatenate(parts, axis=1)
 
     bits = [position // 2**level % 2 for level in range(rounds)]
     leads = jnp.stack([bit == flipped for bit in bits]).astype(jnp.int32)
-    far_given = quarter(1, 1, zlo)
+    far_given = quarter(1, 1, None)
     far_partner = swapped(far_given, "depth", 0)
     far_kept = quarter(0, 1, far_given)
     far = compose(0, "halves", leads, far_kept, far_partner)

time: 87.3 us -> 85.4 us (0.978); the launches traced: 85.8 us -> 85.1 us
  waiting for transfers between devices: 4.58 us -> 3.3 us
  Pallas kernels: 53.1 us -> 54.3 us
    ppermute x1, starting transfers between devices: 2.03 us -> 3.59 us  [per_device(): top = lax.ppermute(band(rows - SUB), 'tile', up)]
    ppermute x1, starting transfers between devices: 3.96 us -> 2.59 us  [per_device(): bottom = lax.ppermute(band(0), 'tile', down)]
    ppermute x1, waiting for transfers between devices: 1.28 us -> 0.01 us  [per_device(): yhi = lax.ppermute(first_line, 'tile', down)]
    pallas_call x4 -> x5, Pallas kernels: 31.6 us -> 32.8 us  [the longest x4 30.2 us: integrate(): pl.pallas_call(functools.partial(integrate_kernel, place, own, staged), o...]
  transfers between devices with their start and end apart: 12 -> 12, of which waited for: 2 -> 1; matrix products, arithmetic and copies ran while one was open for 0% -> 0% of each run, Pallas kernels for 42% -> 45%
where the time goes in v6:
time: 85.4 us; the launch traced here: 85.1 us
  Pallas kernels  54.3 us (64%)
  starting transfers between devices  26.4 us (31%)
  waiting for transfers between devices  3.3 us (4%)
  between operations  0.94 us (1%)
    pallas_call x4, Pallas kernels, integrate(): pl.pallas_call(functools.partial(integrate_kernel, place, own, staged), o...  30.2 us
    pallas_call x2, Pallas kernels, shade(): pl.pallas_call(functools.partial(shade_kernel, inner), out_shape=jax.Shap...  17.7 us
    ppermute x2, starting transfers between devices, per_device(): halo = lax.ppermute(last, 'depth', up) + lax.ppermute(first, 'depth', down)  5.61 us
    ppermute x1, starting transfers between devices, per_device(): zlo = lax.ppermute(last_plane, 'depth', up)  3.71 us
    ppermute x1, starting transfers between devices, per_device(): top = lax.ppermute(band(rows - SUB), 'tile', up)  3.59 us
    ppermute x2, waiting for transfers between devices, per_device(): halo = lax.ppermute(last, 'depth', up) + lax.ppermute(first, 'depth', down)  3.28 us
    ppermute x1, starting transfers between devices, per_device(): ylo = lax.ppermute(last_line, 'tile', up)  3.12 us
    ppermute x1, starting transfers between devices, per_device(): yhi = lax.ppermute(first_line, 'tile', down)  3.06 us
  transfers between devices with their start and end apart: 12, of which 1 were waited for; matrix products, arithmetic and copies ran while one was open for 0% of the time, Pallas kernels for 45%

profile of v6, /device:TPU:9, one launch (start us, length us, event | category | flops | bytes accessed | tf_op | source)
XLA Modules:
  0.0 85.1 jit_solution(9816459828489699923)
XLA Ops:
  0.0 1.9 %edges.1 = (bf16[64,1024]{1,0:T(8,128)(2,1)S(1)}, bf16[64,1024]{1,0:T(8,128)(2,1)S(1)}, bf16[32,1024]{1,0:T(8,128)(2,1)S(1)}, bf16[32,1024]{1,0:T(8,128)(2,1)S(1)}) custom-call(s32[32,64,1024]{2,1,0:T(8,128)} %density_ref.10), custom_call_target="tpu_custom_call" | custom-call | tf_op jit(solution)/shard_map/edges/pallas_call | solution.py:75
  1.9 0.0 copy-start
  1.9 3.7 %collective-permute-start = (bf16[64,1024]{1,0:T(8,128)(2,1)S(1)}, bf16[64,1024]{1,0:T(8,128)(2,1)S(1)}, u32[]{:S(2)}, u32[]{:S(2)}) collective-permute-start(bf16[64,1024]{1,0:T(8,128)(2,1)S(1)} %get-tuple-element.16), channel_id=1, source_target_pairs={{0,8},{8,16},{16,24},{1,9},{9,17},{17,25},{2,10},{10,18},{18,26},{... | collective-permute-start | bytes 393224 | tf_op jit(solution)/shard_map/ppermute | solution.py:562
  5.6 1.9 %collective-permute-start.1 = (bf16[64,1024]{1,0:T(8,128)(2,1)S(1)}, bf16[64,1024]{1,0:T(8,128)(2,1)S(1)}, u32[]{:S(2)}, u32[]{:S(2)}) collective-permute-start(bf16[64,1024]{1,0:T(8,128)(2,1)S(1)} %get-tuple-element.17), channel_id=1, source_target_pairs={{8,0},{16,8},{24,16},{9,1},{17,9},{25,17},{10,2},{18,10},{26,18},{... | collective-permute-start | bytes 393224 | tf_op jit(solution)/shard_map/ppermute | solution.py:563
  7.5 3.1 %collective-permute-start.2 = (bf16[32,1024]{1,0:T(8,128)(2,1)S(1)}, bf16[32,1024]{1,0:T(8,128)(2,1)S(1)}, u32[]{:S(2)}, u32[]{:S(2)}) collective-permute-start(bf16[32,1024]{1,0:T(8,128)(2,1)S(1)} %get-tuple-element.18), channel_id=1, source_target_pairs={{0,1},{1,2},{2,3},{3,4},{4,5},{5,6},{6,7},{8,9},{9,10},{10,11},{11... | collective-permute-start | bytes 196616 | tf_op jit(solution)/shard_map/ppermute | solution.py:565
  10.6 3.1 %collective-permute-start.3 = (bf16[32,1024]{1,0:T(8,128)(2,1)S(1)}, bf16[32,1024]{1,0:T(8,128)(2,1)S(1)}, u32[]{:S(2)}, u32[]{:S(2)}) collective-permute-start(bf16[32,1024]{1,0:T(8,128)(2,1)S(1)} %get-tuple-element.19), channel_id=1, source_target_pairs={{1,0},{2,1},{3,2},{4,3},{5,4},{6,5},{7,6},{9,8},{10,9},{11,10},{12... | collective-permute-start | bytes 196616 | tf_op jit(solution)/shard_map/ppermute | solution.py:566
  13.7 2.6 %stage.1.token_ref = s32[32,4,80,128]{3,2,1,0:T(8,128)S(1)} custom-call(s32[32,64,1024]{2,1,0:T(8,128)} %density_ref.10), custom_call_target="tpu_custom_call" | custom-call | bytes 8388608 | tf_op jit(solution)/shard_map/stage/pallas_call | solution.py:147
  17.0 0.0 collective-permute-done.2.ylo_ref
  17.0 0.0 collective-permute-done.zlo_ref
  17.0 0.0 collective-permute-done.1.zhi_ref
  17.0 6.4 %integrate.4.token_ref = f32[8,2,64,128]{3,2,1,0:T(8,128)S(1)} custom-call(s32[1]{0:T(128)} %copy.4.flip_ref.density_ref, f32[4,4]{1,0:T(4,128)S(1)} %copy-done, s32[1]{0:T(128)} %copy.4.flip_ref.density_ref, bf16[64,1024]{1,0:T(8,128)(2,1)S(1)} %collective-permute-done.zlo_ref, bf16[64,1024]{1,0:T(8,128)(2,1)S(1)} %collective-permute-done.1.zhi_ref, ...), custom_call_target="tpu_custom_call" | custom-call | flops 36700160 | bytes 4194304 | tf_op jit(solution)/shard_map/integrate/pallas_call | solution.py:297
  23.5 0.1 collective-permute-start.4
  23.6 0.1 add_convert_fusion.leads_ref
  23.7 7.9 %integrate.5.refs_0_ = f32[8,2,64,128]{3,2,1,0:T(8,128)S(1)} custom-call(s32[1]{0:T(128)} %copy.4.flip_ref.density_ref, f32[4,4]{1,0:T(4,128)S(1)} %copy-done, s32[32,64,1024]{2,1,0:T(8,128)} %density_ref.10, bf16[64,1024]{1,0:T(8,128)(2,1)S(1)} %collective-permute-done.zlo_ref, bf16[64,1024]{1,0:T(8,128)(2,1)S(1)} %collective-permute-done.1.zhi_ref, ...), custom_call_target="tpu_custom_call" | custom-call | flops 36700160 | bytes 4194304 | tf_op jit(solution)/shard_map/integrate/pallas_call | solution.py:297
  31.6 0.0 collective-permute-done.4.refs_1_
  31.6 0.8 compose.2
  32.5 2.3 %collective-permute-start.5 = (f32[4,2,64,128]{3,2,1,0:T(8,128)S(1)}, f32[4,2,64,128]{3,2,1,0:T(8,128)S(1)}, u32[]{:S(2)}, u32[]{:S(2)}) collective-permute-start(f32[4,2,64,128]{3,2,1,0:T(8,128)S(1)} %get-tuple-element.20.token_ref), channel_id=1, source_target_pairs={{0,16},{16,0},{8,24},{24,8},{1,17},{17,1},{9,25},{25,9},{2,18},{18... | collective-permute-start | bytes 786440 | tf_op jit(solution)/shard_map/ppermute | solution.py:37
  34.8 7.9 %integrate.7 = f32[8,2,64,128]{3,2,1,0:T(8,128)S(1)} custom-call(s32[1]{0:T(128)} %copy.4.flip_ref.density_ref, f32[4,4]{1,0:T(4,128)S(1)} %copy-done, s32[32,64,1024]{2,1,0:T(8,128)} %density_ref.10, bf16[64,1024]{1,0:T(8,128)(2,1)S(1)} %collective-permute-done.zlo_ref, bf16[64,1024]{1,0:T(8,128)(2,1)S(1)} %collective-permute-done.1.zhi_ref, ...), custom_call_target="tpu_custom_call" | custom-call | flops 36700160 | bytes 4194304 | tf_op jit(solution)/shard_map/integrate/pallas_call | solution.py:297
  42.8 0.4 collective-permute-start.6
  43.2 0.0 collective-permute-done.5.token_ref.refs_2_
  43.2 0.0 collective-permute-start.7
  43.2 7.9 %integrate.6.refs_0_ = f32[8,2,64,128]{3,2,1,0:T(8,128)S(1)} custom-call(s32[1]{0:T(128)} %copy.4.flip_ref.density_ref, f32[4,4]{1,0:T(4,128)S(1)} %copy-done, s32[32,64,1024]{2,1,0:T(8,128)} %density_ref.10, bf16[64,1024]{1,0:T(8,128)(2,1)S(1)} %collective-permute-done.zlo_ref, bf16[64,1024]{1,0:T(8,128)(2,1)S(1)} %collective-permute-done.1.zhi_ref, ...), custom_call_target="tpu_custom_call" | custom-call | flops 36700160 | bytes 4194304 | tf_op jit(solution)/shard_map/integrate/pallas_call | solution.py:297
  51.1 0.0 collective-permute-done.6.refs_1_
  51.1 0.0 collective-permute-done.7.refs_3_
  51.1 1.1 %compose.3 = (f32[8,2,64,128]{3,2,1,0:T(8,128)S(1)}, f32[64,128]{1,0:T(8,128)S(1)}, f32[64,128]{1,0:T(8,128)S(1)}) custom-call(s32[2]{0:T(128)S(1)} %add_convert_fusion.leads_ref, f32[8,2,64,128]{3,2,1,0:T(8,128)S(1)} %integrate.6.refs_0_, f32[8,2,64,128]{3,2,1,0:T(8,128)S(1)} %collective-permute-done.6.refs_1_, ...), custom_call_target="tpu_custom_call" | custom-call | bytes 524288 | tf_op jit(solution)/shard_map/compose/pallas_call | solution.py:533
  52.2 3.7 %collective-permute-start.8 = (f32[64,128]{1,0:T(8,128)S(1)}, f32[64,128]{1,0:T(8,128)S(1)}, u32[]{:S(2)}, u32[]{:S(2)}) collective-permute-start(f32[64,128]{1,0:T(8,128)S(1)} %get-tuple-element.25), channel_id=1, source_target_pairs={{0,8},{8,16},{16,24},{1,9},{9,17},{17,25},{2,10},{10,18},{18,26},{... | collective-permute-start | bytes 98312 | tf_op jit(solution)/shard_map/ppermute | solution.py:609
  55.9 1.9 %collective-permute-start.9 = (f32[64,128]{1,0:T(8,128)S(1)}, f32[64,128]{1,0:T(8,128)S(1)}, u32[]{:S(2)}, u32[]{:S(2)}) collective-permute-start(f32[64,128]{1,0:T(8,128)S(1)} %get-tuple-element.26), channel_id=1, source_target_pairs={{8,0},{16,8},{24,16},{9,1},{17,9},{25,17},{10,2},{18,10},{26,18},{... | collective-permute-start | bytes 98312 | tf_op jit(solution)/shard_map/ppermute | solution.py:609
  57.9 3.3 %collective-permute-done.9 = f32[64,128]{1,0:T(8,128)S(1)} collective-permute-done((f32[64,128]{1,0:T(8,128)S(1)}, f32[64,128]{1,0:T(8,128)S(1)}, u32[]{:S(2)}, u32[]{:S(2)}) %collective-permute-start.9) | collective-permute-done | bytes 32800 | tf_op jit(solution)/shard_map/ppermute | solution.py:609
  61.2 3.6 %collective-permute-start.10 = (f32[17,8,128]{2,1,0:T(8,128)S(1)}, f32[17,8,128]{2,1,0:T(8,128)S(1)}, u32[]{:S(2)}, u32[]{:S(2)}) collective-permute-start(f32[17,8,128]{2,1,0:T(8,128)S(1)} %pad_maximum_fusion), channel_id=1, source_target_pairs={{0,1},{1,2},{2,3},{3,4},{4,5},{5,6},{6,7},{8,9},{9,10},{10,11},{11... | collective-permute-start | bytes 208904 | tf_op jit(solution)/shard_map/ppermute | solution.py:618
  64.8 2.6 %collective-permute-start.11 = (f32[17,8,128]{2,1,0:T(8,128)S(1)}, f32[17,8,128]{2,1,0:T(8,128)S(1)}, u32[]{:S(2)}, u32[]{:S(2)}) collective-permute-start(f32[17,8,128]{2,1,0:T(8,128)S(1)} %pad_maximum_fusion.1), channel_id=1, source_target_pairs={{1,0},{2,1},{3,2},{4,3},{5,4},{6,5},{7,6},{9,8},{10,9},{11,10},{12... | collective-permute-start | bytes 208904 | tf_op jit(solution)/shard_map/ppermute | solution.py:619
  67.4 11.9 %shade_inner.1.rest_2_ = f32[3,64,256]{2,1,0:T(8,128)S(1)} custom-call(f32[8,2,64,128]{3,2,1,0:T(8,128)S(1)} %get-tuple-element.24.core_ref, f32[64,128]{1,0:T(8,128)S(1)} %add.14.halo_ref), custom_call_target="tpu_custom_call" | custom-call | flops 56819712 | bytes 524288 | tf_op jit(solution)/shard_map/shade_inner/pallas_call | solution.py:458
  79.3 5.7 %shade_outer.1 = f32[3,64,256]{2,1,0:T(8,128)} custom-call(f32[8,2,64,128]{3,2,1,0:T(8,128)S(1)} %get-tuple-element.24.core_ref, f32[64,128]{1,0:T(8,128)S(1)} %add.14.halo_ref, f32[17,8,128]{2,1,0:T(8,128)S(1)} %collective-permute-done.10.rest_0_, f32[17,8,128]{2,1,0:T(8,128)S(1)} %collective-permute-done.11.rest_1_, f32[3,64,256]{2,1,0:T(8,128)S(1)} %shade_inner.1.rest_2_), custom_call_target="tpu_custom_call" | custom-call | flops 18939904 | bytes 524288 | tf_op jit(solution)/shard_map/shade_outer/pallas_call | solution.py:458
  (10 shorter events, 0.1 us)
Async XLA Ops:
  1.9 15.2 %copy-start = (f32[4,4]{1,0:T(4,128)S(1)}, f32[4,4]{1,0:T(4,128)}, u32[]{:S(2)}) copy-start(f32[4,4]{1,0:T(4,128)} %coeff_ref.7) | copy-start | bytes 196
  1.9 15.1 %collective-permute-start = (bf16[64,1024]{1,0:T(8,128)(2,1)S(1)}, bf16[64,1024]{1,0:T(8,128)(2,1)S(1)}, u32[]{:S(2)}, u32[]{:S(2)}) collective-permute-start(bf16[64,1024]{1,0:T(8,128)(2,1)S(1)} %get-tuple-element.16), channel_id=1, source_target_pairs={{0,8},{8,16},{16,24},{1,9},{9,17},{17,25},{2,10},{10,18},{18,26},{... | collective-permute-start | bytes 393224 | tf_op jit(solution)/shard_map/ppermute | solution.py:562
  5.6 11.4 %collective-permute-start.1 = (bf16[64,1024]{1,0:T(8,128)(2,1)S(1)}, bf16[64,1024]{1,0:T(8,128)(2,1)S(1)}, u32[]{:S(2)}, u32[]{:S(2)}) collective-permute-start(bf16[64,1024]{1,0:T(8,128)(2,1)S(1)} %get-tuple-element.17), channel_id=1, source_target_pairs={{8,0},{16,8},{24,16},{9,1},{17,9},{25,17},{10,2},{18,10},{26,18},{... | collective-permute-start | bytes 393224 | tf_op jit(solution)/shard_map/ppermute | solution.py:563
  7.5 9.5 %collective-permute-start.2 = (bf16[32,1024]{1,0:T(8,128)(2,1)S(1)}, bf16[32,1024]{1,0:T(8,128)(2,1)S(1)}, u32[]{:S(2)}, u32[]{:S(2)}) collective-permute-start(bf16[32,1024]{1,0:T(8,128)(2,1)S(1)} %get-tuple-element.18), channel_id=1, source_target_pairs={{0,1},{1,2},{2,3},{3,4},{4,5},{5,6},{6,7},{8,9},{9,10},{10,11},{11... | collective-permute-start | bytes 196616 | tf_op jit(solution)/shard_map/ppermute | solution.py:565
  10.6 6.3 %collective-permute-start.3 = (bf16[32,1024]{1,0:T(8,128)(2,1)S(1)}, bf16[32,1024]{1,0:T(8,128)(2,1)S(1)}, u32[]{:S(2)}, u32[]{:S(2)}) collective-permute-start(bf16[32,1024]{1,0:T(8,128)(2,1)S(1)} %get-tuple-element.19), channel_id=1, source_target_pairs={{1,0},{2,1},{3,2},{4,3},{5,4},{6,5},{7,6},{9,8},{10,9},{11,10},{12... | collective-permute-start | bytes 196616 | tf_op jit(solution)/shard_map/ppermute | solution.py:566
  23.5 8.2 %collective-permute-start.4 = (f32[8,2,64,128]{3,2,1,0:T(8,128)S(1)}, f32[8,2,64,128]{3,2,1,0:T(8,128)S(1)}, u32[]{:S(2)}, u32[]{:S(2)}) collective-permute-start(f32[8,2,64,128]{3,2,1,0:T(8,128)S(1)} %integrate.4.token_ref), channel_id=1, source_target_pairs={{0,8},{8,0},{16,24},{24,16},{1,9},{9,1},{17,25},{25,17},{2,10},{10... | collective-permute-start | bytes 1572872 | tf_op jit(solution)/shard_map/ppermute | solution.py:37
  32.5 10.7 %collective-permute-start.5 = (f32[4,2,64,128]{3,2,1,0:T(8,128)S(1)}, f32[4,2,64,128]{3,2,1,0:T(8,128)S(1)}, u32[]{:S(2)}, u32[]{:S(2)}) collective-permute-start(f32[4,2,64,128]{3,2,1,0:T(8,128)S(1)} %get-tuple-element.20.token_ref), channel_id=1, source_target_pairs={{0,16},{16,0},{8,24},{24,8},{1,17},{17,1},{9,25},{25,9},{2,18},{18... | collective-permute-start | bytes 786440 | tf_op jit(solution)/shard_map/ppermute | solution.py:37
  42.8 8.3 %collective-permute-start.6 = (f32[8,2,64,128]{3,2,1,0:T(8,128)S(1)}, f32[8,2,64,128]{3,2,1,0:T(8,128)S(1)}, u32[]{:S(2)}, u32[]{:S(2)}) collective-permute-start(f32[8,2,64,128]{3,2,1,0:T(8,128)S(1)} %integrate.7), channel_id=1, source_target_pairs={{0,8},{8,0},{16,24},{24,16},{1,9},{9,1},{17,25},{25,17},{2,10},{10... | collective-permute-start | bytes 1572872 | tf_op jit(solution)/shard_map/ppermute | solution.py:37
  43.2 7.9 %collective-permute-start.7 = (f32[4,2,64,128]{3,2,1,0:T(8,128)S(1)}, f32[4,2,64,128]{3,2,1,0:T(8,128)S(1)}, u32[]{:S(2)}, u32[]{:S(2)}) collective-permute-start(f32[4,2,64,128]{3,2,1,0:T(8,128)S(1)} %get-tuple-element.23), channel_id=1, source_target_pairs={{0,16},{16,0},{8,24},{24,8},{1,17},{17,1},{9,25},{25,9},{2,18},{18... | collective-permute-start | bytes 786440 | tf_op jit(solution)/shard_map/ppermute | solution.py:37
  52.2 5.7 %collective-permute-start.8 = (f32[64,128]{1,0:T(8,128)S(1)}, f32[64,128]{1,0:T(8,128)S(1)}, u32[]{:S(2)}, u32[]{:S(2)}) collective-permute-start(f32[64,128]{1,0:T(8,128)S(1)} %get-tuple-element.25), channel_id=1, source_target_pairs={{0,8},{8,16},{16,24},{1,9},{9,17},{17,25},{2,10},{10,18},{18,26},{... | collective-permute-start | bytes 98312 | tf_op jit(solution)/shard_map/ppermute | solution.py:609
  55.9 5.2 %collective-permute-start.9 = (f32[64,128]{1,0:T(8,128)S(1)}, f32[64,128]{1,0:T(8,128)S(1)}, u32[]{:S(2)}, u32[]{:S(2)}) collective-permute-start(f32[64,128]{1,0:T(8,128)S(1)} %get-tuple-element.26), channel_id=1, source_target_pairs={{8,0},{16,8},{24,16},{9,1},{17,9},{25,17},{10,2},{18,10},{26,18},{... | collective-permute-start | bytes 98312 | tf_op jit(solution)/shard_map/ppermute | solution.py:609
  61.2 18.1 %collective-permute-start.10 = (f32[17,8,128]{2,1,0:T(8,128)S(1)}, f32[17,8,128]{2,1,0:T(8,128)S(1)}, u32[]{:S(2)}, u32[]{:S(2)}) collective-permute-start(f32[17,8,128]{2,1,0:T(8,128)S(1)} %pad_maximum_fusion), channel_id=1, source_target_pairs={{0,1},{1,2},{2,3},{3,4},{4,5},{5,6},{6,7},{8,9},{9,10},{10,11},{11... | collective-permute-start | bytes 208904 | tf_op jit(solution)/shard_map/ppermute | solution.py:618
  64.8 14.5 %collective-permute-start.11 = (f32[17,8,128]{2,1,0:T(8,128)S(1)}, f32[17,8,128]{2,1,0:T(8,128)S(1)}, u32[]{:S(2)}, u32[]{:S(2)}) collective-permute-start(f32[17,8,128]{2,1,0:T(8,128)S(1)} %pad_maximum_fusion.1), channel_id=1, source_target_pairs={{1,0},{2,1},{3,2},{4,3},{5,4},{6,5},{7,6},{9,8},{10,9},{11,10},{12... | collective-permute-start | bytes 208904 | tf_op jit(solution)/shard_map/ppermute | solution.py:619

commit v7 on v6

--- a/solution.py
+++ b/solution.py
@@ -49,7 +49,7 @@
         )
         copies.append(
             pltpu.make_async_copy(
-                density_ref.at[:, side * (rows - SUB) : side * (rows - SUB) + SUB, :],
+                density_ref.at[:, side * (rows - 1) : side * (rows - 1) + 1, :],
                 bands.at[side],
                 sems.at[2 * side + 1],
             )
@@ -61,9 +61,8 @@
     zlo_ref[...] = planes[0].astype(jnp.float32).astype(jnp.bfloat16)
     zhi_ref[...] = planes[1].astype(jnp.float32).astype(jnp.bfloat16)
     for side, ref in ((0, ylo_ref), (1, yhi_ref)):
-        row = side * (SUB - 1)
         for z in range(cells):
-            lines[z : z + 1, :] = bands[side, z, row : row + 1, :].astype(jnp.float32)
+            lines[z : z + 1, :] = bands[side, z].astype(jnp.float32)
         ref[...] = lines[...].astype(jnp.bfloat16)
 
 
@@ -79,7 +78,7 @@
         out_specs=[vmem] * 4,
         scratch_shapes=[
             pltpu.VMEM((2, rows, width), jnp.int32),
-            pltpu.VMEM((2, cells, SUB, width), jnp.int32),
+            pltpu.VMEM((2, cells, 1, width), jnp.int32),
             pltpu.VMEM((cells, width), jnp.float32),
             pltpu.SemaphoreType.DMA((4,)),
         ],

time: 85.4 us -> 84.8 us (level)
  no operation moved by 1% of the time
where the time goes in v7:
time: 84.8 us; the launch traced here: 84.5 us
  Pallas kernels  53.7 us (63%)
  starting transfers between devices  26.4 us (31%)
  waiting for transfers between devices  3.3 us (4%)
  between operations  0.94 us (1%)
    pallas_call x4, Pallas kernels, integrate(): pl.pallas_call(functools.partial(integrate_kernel, place, own, staged), o...  30.2 us
    pallas_call x2, Pallas kernels, shade(): pl.pallas_call(functools.partial(shade_kernel, inner), out_shape=jax.Shap...  17.7 us
    ppermute x2, starting transfers between devices, per_device(): halo = lax.ppermute(last, 'depth', up) + lax.ppermute(first, 'depth', down)  5.61 us
    ppermute x1, starting transfers between devices, per_device(): zlo = lax.ppermute(last_plane, 'depth', up)  3.71 us
    ppermute x1, starting transfers between devices, per_device(): top = lax.ppermute(band(rows - SUB), 'tile', up)  3.59 us
    ppermute x2, waiting for transfers between devices, per_device(): halo = lax.ppermute(last, 'depth', up) + lax.ppermute(first, 'depth', down)  3.28 us
    ppermute x1, starting transfers between devices, per_device(): ylo = lax.ppermute(last_line, 'tile', up)  3.12 us
    ppermute x1, starting transfers between devices, per_device(): yhi = lax.ppermute(first_line, 'tile', down)  3.06 us
  transfers between devices with their start and end apart: 12, of which 1 were waited for; matrix products, arithmetic and copies ran while one was open for 0% of the time, Pallas kernels for 45%

profile of v7, /device:TPU:9, one launch (start us, length us, event | category | flops | bytes accessed | tf_op | source)
XLA Modules:
  0.0 84.5 jit_solution(13111737392994351261)
XLA Ops:
  0.0 1.2 %edges.1 = (bf16[64,1024]{1,0:T(8,128)(2,1)S(1)}, bf16[64,1024]{1,0:T(8,128)(2,1)S(1)}, bf16[32,1024]{1,0:T(8,128)(2,1)S(1)}, bf16[32,1024]{1,0:T(8,128)(2,1)S(1)}) custom-call(s32[32,64,1024]{2,1,0:T(8,128)} %density_ref.10), custom_call_target="tpu_custom_call" | custom-call | tf_op jit(solution)/shard_map/edges/pallas_call | solution.py:74
  1.3 0.0 copy-start
  1.3 3.7 %collective-permute-start = (bf16[64,1024]{1,0:T(8,128)(2,1)S(1)}, bf16[64,1024]{1,0:T(8,128)(2,1)S(1)}, u32[]{:S(2)}, u32[]{:S(2)}) collective-permute-start(bf16[64,1024]{1,0:T(8,128)(2,1)S(1)} %get-tuple-element.16), channel_id=1, source_target_pairs={{0,8},{8,16},{16,24},{1,9},{9,17},{17,25},{2,10},{10,18},{18,26},{... | collective-permute-start | bytes 393224 | tf_op jit(solution)/shard_map/ppermute | solution.py:561
  5.0 1.9 %collective-permute-start.1 = (bf16[64,1024]{1,0:T(8,128)(2,1)S(1)}, bf16[64,1024]{1,0:T(8,128)(2,1)S(1)}, u32[]{:S(2)}, u32[]{:S(2)}) collective-permute-start(bf16[64,1024]{1,0:T(8,128)(2,1)S(1)} %get-tuple-element.17), channel_id=1, source_target_pairs={{8,0},{16,8},{24,16},{9,1},{17,9},{25,17},{10,2},{18,10},{26,18},{... | collective-permute-start | bytes 393224 | tf_op jit(solution)/shard_map/ppermute | solution.py:562
  6.9 3.1 %collective-permute-start.2 = (bf16[32,1024]{1,0:T(8,128)(2,1)S(1)}, bf16[32,1024]{1,0:T(8,128)(2,1)S(1)}, u32[]{:S(2)}, u32[]{:S(2)}) collective-permute-start(bf16[32,1024]{1,0:T(8,128)(2,1)S(1)} %get-tuple-element.18), channel_id=1, source_target_pairs={{0,1},{1,2},{2,3},{3,4},{4,5},{5,6},{6,7},{8,9},{9,10},{10,11},{11... | collective-permute-start | bytes 196616 | tf_op jit(solution)/shard_map/ppermute | solution.py:564
  10.0 3.1 %collective-permute-start.3 = (bf16[32,1024]{1,0:T(8,128)(2,1)S(1)}, bf16[32,1024]{1,0:T(8,128)(2,1)S(1)}, u32[]{:S(2)}, u32[]{:S(2)}) collective-permute-start(bf16[32,1024]{1,0:T(8,128)(2,1)S(1)} %get-tuple-element.19), channel_id=1, source_target_pairs={{1,0},{2,1},{3,2},{4,3},{5,4},{6,5},{7,6},{9,8},{10,9},{11,10},{12... | collective-permute-start | bytes 196616 | tf_op jit(solution)/shard_map/ppermute | solution.py:565
  13.1 2.6 %stage.1.token_ref = s32[32,4,80,128]{3,2,1,0:T(8,128)S(1)} custom-call(s32[32,64,1024]{2,1,0:T(8,128)} %density_ref.10), custom_call_target="tpu_custom_call" | custom-call | bytes 8388608 | tf_op jit(solution)/shard_map/stage/pallas_call | solution.py:146
  16.4 0.0 collective-permute-done.2.ylo_ref
  16.4 0.0 collective-permute-done.3.yhi_ref
  16.4 0.0 collective-permute-done.zlo_ref
  16.4 6.4 %integrate.4.token_ref = f32[8,2,64,128]{3,2,1,0:T(8,128)S(1)} custom-call(s32[1]{0:T(128)} %copy.4.flip_ref.density_ref, f32[4,4]{1,0:T(4,128)S(1)} %copy-done, s32[1]{0:T(128)} %copy.4.flip_ref.density_ref, bf16[64,1024]{1,0:T(8,128)(2,1)S(1)} %collective-permute-done.zlo_ref, bf16[64,1024]{1,0:T(8,128)(2,1)S(1)} %collective-permute-done.1.zhi_ref, ...), custom_call_target="tpu_custom_call" | custom-call | flops 36700160 | bytes 4194304 | tf_op jit(solution)/shard_map/integrate/pallas_call | solution.py:296
  22.9 0.1 collective-permute-start.4
  23.0 0.1 add_convert_fusion.leads_ref
  23.1 7.9 %integrate.5.refs_0_ = f32[8,2,64,128]{3,2,1,0:T(8,128)S(1)} custom-call(s32[1]{0:T(128)} %copy.4.flip_ref.density_ref, f32[4,4]{1,0:T(4,128)S(1)} %copy-done, s32[32,64,1024]{2,1,0:T(8,128)} %density_ref.10, bf16[64,1024]{1,0:T(8,128)(2,1)S(1)} %collective-permute-done.zlo_ref, bf16[64,1024]{1,0:T(8,128)(2,1)S(1)} %collective-permute-done.1.zhi_ref, ...), custom_call_target="tpu_custom_call" | custom-call | flops 36700160 | bytes 4194304 | tf_op jit(solution)/shard_map/integrate/pallas_call | solution.py:296
  31.0 0.8 %compose.2 = (f32[4,2,64,128]{3,2,1,0:T(8,128)S(1)}, f32[4,2,64,128]{3,2,1,0:T(8,128)S(1)}) custom-call(s32[2]{0:T(128)S(1)} %add_convert_fusion.leads_ref, f32[8,2,64,128]{3,2,1,0:T(8,128)S(1)} %integrate.5.refs_0_, f32[8,2,64,128]{3,2,1,0:T(8,128)S(1)} %collective-permute-done.4.refs_1_), custom_call_target="tpu_custom_call" | custom-call | bytes 524288 | tf_op jit(solution)/shard_map/compose/pallas_call | solution.py:532
  31.9 2.3 %collective-permute-start.5 = (f32[4,2,64,128]{3,2,1,0:T(8,128)S(1)}, f32[4,2,64,128]{3,2,1,0:T(8,128)S(1)}, u32[]{:S(2)}, u32[]{:S(2)}) collective-permute-start(f32[4,2,64,128]{3,2,1,0:T(8,128)S(1)} %get-tuple-element.20.token_ref), channel_id=1, source_target_pairs={{0,16},{16,0},{8,24},{24,8},{1,17},{17,1},{9,25},{25,9},{2,18},{18... | collective-permute-start | bytes 786440 | tf_op jit(solution)/shard_map/ppermute | solution.py:37
  34.2 7.9 %integrate.7 = f32[8,2,64,128]{3,2,1,0:T(8,128)S(1)} custom-call(s32[1]{0:T(128)} %copy.4.flip_ref.density_ref, f32[4,4]{1,0:T(4,128)S(1)} %copy-done, s32[32,64,1024]{2,1,0:T(8,128)} %density_ref.10, bf16[64,1024]{1,0:T(8,128)(2,1)S(1)} %collective-permute-done.zlo_ref, bf16[64,1024]{1,0:T(8,128)(2,1)S(1)} %collective-permute-done.1.zhi_ref, ...), custom_call_target="tpu_custom_call" | custom-call | flops 36700160 | bytes 4194304 | tf_op jit(solution)/shard_map/integrate/pallas_call | solution.py:296
  42.2 0.4 collective-permute-start.6
  42.6 0.0 collective-permute-done.5.token_ref.refs_2_
  42.6 0.0 collective-permute-start.7
  42.6 7.9 %integrate.6.refs_0_ = f32[8,2,64,128]{3,2,1,0:T(8,128)S(1)} custom-call(s32[1]{0:T(128)} %copy.4.flip_ref.density_ref, f32[4,4]{1,0:T(4,128)S(1)} %copy-done, s32[32,64,1024]{2,1,0:T(8,128)} %density_ref.10, bf16[64,1024]{1,0:T(8,128)(2,1)S(1)} %collective-permute-done.zlo_ref, bf16[64,1024]{1,0:T(8,128)(2,1)S(1)} %collective-permute-done.1.zhi_ref, ...), custom_call_target="tpu_custom_call" | custom-call | flops 36700160 | bytes 4194304 | tf_op jit(solution)/shard_map/integrate/pallas_call | solution.py:296
  50.5 0.0 collective-permute-done.6.refs_1_
  50.5 1.1 %compose.3 = (f32[8,2,64,128]{3,2,1,0:T(8,128)S(1)}, f32[64,128]{1,0:T(8,128)S(1)}, f32[64,128]{1,0:T(8,128)S(1)}) custom-call(s32[2]{0:T(128)S(1)} %add_convert_fusion.leads_ref, f32[8,2,64,128]{3,2,1,0:T(8,128)S(1)} %integrate.6.refs_0_, f32[8,2,64,128]{3,2,1,0:T(8,128)S(1)} %collective-permute-done.6.refs_1_, ...), custom_call_target="tpu_custom_call" | custom-call | bytes 524288 | tf_op jit(solution)/shard_map/compose/pallas_call | solution.py:532
  51.6 3.7 %collective-permute-start.8 = (f32[64,128]{1,0:T(8,128)S(1)}, f32[64,128]{1,0:T(8,128)S(1)}, u32[]{:S(2)}, u32[]{:S(2)}) collective-permute-start(f32[64,128]{1,0:T(8,128)S(1)} %get-tuple-element.25), channel_id=1, source_target_pairs={{0,8},{8,16},{16,24},{1,9},{9,17},{17,25},{2,10},{10,18},{18,26},{... | collective-permute-start | bytes 98312 | tf_op jit(solution)/shard_map/ppermute | solution.py:608
  55.3 1.9 %collective-permute-start.9 = (f32[64,128]{1,0:T(8,128)S(1)}, f32[64,128]{1,0:T(8,128)S(1)}, u32[]{:S(2)}, u32[]{:S(2)}) collective-permute-start(f32[64,128]{1,0:T(8,128)S(1)} %get-tuple-element.26), channel_id=1, source_target_pairs={{8,0},{16,8},{24,16},{9,1},{17,9},{25,17},{10,2},{18,10},{26,18},{... | collective-permute-start | bytes 98312 | tf_op jit(solution)/shard_map/ppermute | solution.py:608
  57.3 0.0 collective-permute-done.8
  57.3 3.3 %collective-permute-done.9 = f32[64,128]{1,0:T(8,128)S(1)} collective-permute-done((f32[64,128]{1,0:T(8,128)S(1)}, f32[64,128]{1,0:T(8,128)S(1)}, u32[]{:S(2)}, u32[]{:S(2)}) %collective-permute-start.9) | collective-permute-done | bytes 32800 | tf_op jit(solution)/shard_map/ppermute | solution.py:608
  60.6 3.6 %collective-permute-start.10 = (f32[17,8,128]{2,1,0:T(8,128)S(1)}, f32[17,8,128]{2,1,0:T(8,128)S(1)}, u32[]{:S(2)}, u32[]{:S(2)}) collective-permute-start(f32[17,8,128]{2,1,0:T(8,128)S(1)} %pad_maximum_fusion), channel_id=1, source_target_pairs={{0,1},{1,2},{2,3},{3,4},{4,5},{5,6},{6,7},{8,9},{9,10},{10,11},{11... | collective-permute-start | bytes 208904 | tf_op jit(solution)/shard_map/ppermute | solution.py:617
  64.2 2.6 %collective-permute-start.11 = (f32[17,8,128]{2,1,0:T(8,128)S(1)}, f32[17,8,128]{2,1,0:T(8,128)S(1)}, u32[]{:S(2)}, u32[]{:S(2)}) collective-permute-start(f32[17,8,128]{2,1,0:T(8,128)S(1)} %pad_maximum_fusion.1), channel_id=1, source_target_pairs={{1,0},{2,1},{3,2},{4,3},{5,4},{6,5},{7,6},{9,8},{10,9},{11,10},{12... | collective-permute-start | bytes 208904 | tf_op jit(solution)/shard_map/ppermute | solution.py:618
  66.8 11.9 %shade_inner.1.rest_2_ = f32[3,64,256]{2,1,0:T(8,128)S(1)} custom-call(f32[8,2,64,128]{3,2,1,0:T(8,128)S(1)} %get-tuple-element.24.core_ref, f32[64,128]{1,0:T(8,128)S(1)} %add.14.halo_ref), custom_call_target="tpu_custom_call" | custom-call | flops 56819712 | bytes 524288 | tf_op jit(solution)/shard_map/shade_inner/pallas_call | solution.py:457
  78.7 0.0 collective-permute-done.10.rest_0_
  78.7 5.7 %shade_outer.1 = f32[3,64,256]{2,1,0:T(8,128)} custom-call(f32[8,2,64,128]{3,2,1,0:T(8,128)S(1)} %get-tuple-element.24.core_ref, f32[64,128]{1,0:T(8,128)S(1)} %add.14.halo_ref, f32[17,8,128]{2,1,0:T(8,128)S(1)} %collective-permute-done.10.rest_0_, f32[17,8,128]{2,1,0:T(8,128)S(1)} %collective-permute-done.11.rest_1_, f32[3,64,256]{2,1,0:T(8,128)S(1)} %shade_inner.1.rest_2_), custom_call_target="tpu_custom_call" | custom-call | flops 18939904 | bytes 524288 | tf_op jit(solution)/shard_map/shade_outer/pallas_call | solution.py:457
  (10 shorter events, 0.1 us)
Async XLA Ops:
  1.3 15.2 %copy-start = (f32[4,4]{1,0:T(4,128)S(1)}, f32[4,4]{1,0:T(4,128)}, u32[]{:S(2)}) copy-start(f32[4,4]{1,0:T(4,128)} %coeff_ref.7) | copy-start | bytes 196
  1.3 15.1 %collective-permute-start = (bf16[64,1024]{1,0:T(8,128)(2,1)S(1)}, bf16[64,1024]{1,0:T(8,128)(2,1)S(1)}, u32[]{:S(2)}, u32[]{:S(2)}) collective-permute-start(bf16[64,1024]{1,0:T(8,128)(2,1)S(1)} %get-tuple-element.16), channel_id=1, source_target_pairs={{0,8},{8,16},{16,24},{1,9},{9,17},{17,25},{2,10},{10,18},{18,26},{... | collective-permute-start | bytes 393224 | tf_op jit(solution)/shard_map/ppermute | solution.py:561
  5.0 11.4 %collective-permute-start.1 = (bf16[64,1024]{1,0:T(8,128)(2,1)S(1)}, bf16[64,1024]{1,0:T(8,128)(2,1)S(1)}, u32[]{:S(2)}, u32[]{:S(2)}) collective-permute-start(bf16[64,1024]{1,0:T(8,128)(2,1)S(1)} %get-tuple-element.17), channel_id=1, source_target_pairs={{8,0},{16,8},{24,16},{9,1},{17,9},{25,17},{10,2},{18,10},{26,18},{... | collective-permute-start | bytes 393224 | tf_op jit(solution)/shard_map/ppermute | solution.py:562
  6.9 9.5 %collective-permute-start.2 = (bf16[32,1024]{1,0:T(8,128)(2,1)S(1)}, bf16[32,1024]{1,0:T(8,128)(2,1)S(1)}, u32[]{:S(2)}, u32[]{:S(2)}) collective-permute-start(bf16[32,1024]{1,0:T(8,128)(2,1)S(1)} %get-tuple-element.18), channel_id=1, source_target_pairs={{0,1},{1,2},{2,3},{3,4},{4,5},{5,6},{6,7},{8,9},{9,10},{10,11},{11... | collective-permute-start | bytes 196616 | tf_op jit(solution)/shard_map/ppermute | solution.py:564
  10.0 6.3 %collective-permute-start.3 = (bf16[32,1024]{1,0:T(8,128)(2,1)S(1)}, bf16[32,1024]{1,0:T(8,128)(2,1)S(1)}, u32[]{:S(2)}, u32[]{:S(2)}) collective-permute-start(bf16[32,1024]{1,0:T(8,128)(2,1)S(1)} %get-tuple-element.19), channel_id=1, source_target_pairs={{1,0},{2,1},{3,2},{4,3},{5,4},{6,5},{7,6},{9,8},{10,9},{11,10},{12... | collective-permute-start | bytes 196616 | tf_op jit(solution)/shard_map/ppermute | solution.py:565
  22.9 8.2 %collective-permute-start.4 = (f32[8,2,64,128]{3,2,1,0:T(8,128)S(1)}, f32[8,2,64,128]{3,2,1,0:T(8,128)S(1)}, u32[]{:S(2)}, u32[]{:S(2)}) collective-permute-start(f32[8,2,64,128]{3,2,1,0:T(8,128)S(1)} %integrate.4.token_ref), channel_id=1, source_target_pairs={{0,8},{8,0},{16,24},{24,16},{1,9},{9,1},{17,25},{25,17},{2,10},{10... | collective-permute-start | bytes 1572872 | tf_op jit(solution)/shard_map/ppermute | solution.py:37
  31.9 10.7 %collective-permute-start.5 = (f32[4,2,64,128]{3,2,1,0:T(8,128)S(1)}, f32[4,2,64,128]{3,2,1,0:T(8,128)S(1)}, u32[]{:S(2)}, u32[]{:S(2)}) collective-permute-start(f32[4,2,64,128]{3,2,1,0:T(8,128)S(1)} %get-tuple-element.20.token_ref), channel_id=1, source_target_pairs={{0,16},{16,0},{8,24},{24,8},{1,17},{17,1},{9,25},{25,9},{2,18},{18... | collective-permute-start | bytes 786440 | tf_op jit(solution)/shard_map/ppermute | solution.py:37
  42.2 8.3 %collective-permute-start.6 = (f32[8,2,64,128]{3,2,1,0:T(8,128)S(1)}, f32[8,2,64,128]{3,2,1,0:T(8,128)S(1)}, u32[]{:S(2)}, u32[]{:S(2)}) collective-permute-start(f32[8,2,64,128]{3,2,1,0:T(8,128)S(1)} %integrate.7), channel_id=1, source_target_pairs={{0,8},{8,0},{16,24},{24,16},{1,9},{9,1},{17,25},{25,17},{2,10},{10... | collective-permute-start | bytes 1572872 | tf_op jit(solution)/shard_map/ppermute | solution.py:37
  42.6 7.9 %collective-permute-start.7 = (f32[4,2,64,128]{3,2,1,0:T(8,128)S(1)}, f32[4,2,64,128]{3,2,1,0:T(8,128)S(1)}, u32[]{:S(2)}, u32[]{:S(2)}) collective-permute-start(f32[4,2,64,128]{3,2,1,0:T(8,128)S(1)} %get-tuple-element.23), channel_id=1, source_target_pairs={{0,16},{16,0},{8,24},{24,8},{1,17},{17,1},{9,25},{25,9},{2,18},{18... | collective-permute-start | bytes 786440 | tf_op jit(solution)/shard_map/ppermute | solution.py:37
  51.6 5.7 %collective-permute-start.8 = (f32[64,128]{1,0:T(8,128)S(1)}, f32[64,128]{1,0:T(8,128)S(1)}, u32[]{:S(2)}, u32[]{:S(2)}) collective-permute-start(f32[64,128]{1,0:T(8,128)S(1)} %get-tuple-element.25), channel_id=1, source_target_pairs={{0,8},{8,16},{16,24},{1,9},{9,17},{17,25},{2,10},{10,18},{18,26},{... | collective-permute-start | bytes 98312 | tf_op jit(solution)/shard_map/ppermute | solution.py:608
  55.3 5.2 %collective-permute-start.9 = (f32[64,128]{1,0:T(8,128)S(1)}, f32[64,128]{1,0:T(8,128)S(1)}, u32[]{:S(2)}, u32[]{:S(2)}) collective-permute-start(f32[64,128]{1,0:T(8,128)S(1)} %get-tuple-element.26), channel_id=1, source_target_pairs={{8,0},{16,8},{24,16},{9,1},{17,9},{25,17},{10,2},{18,10},{26,18},{... | collective-permute-start | bytes 98312 | tf_op jit(solution)/shard_map/ppermute | solution.py:608
  60.6 18.1 %collective-permute-start.10 = (f32[17,8,128]{2,1,0:T(8,128)S(1)}, f32[17,8,128]{2,1,0:T(8,128)S(1)}, u32[]{:S(2)}, u32[]{:S(2)}) collective-permute-start(f32[17,8,128]{2,1,0:T(8,128)S(1)} %pad_maximum_fusion), channel_id=1, source_target_pairs={{0,1},{1,2},{2,3},{3,4},{4,5},{5,6},{6,7},{8,9},{9,10},{10,11},{11... | collective-permute-start | bytes 208904 | tf_op jit(solution)/shard_map/ppermute | solution.py:617
  64.2 14.5 %collective-permute-start.11 = (f32[17,8,128]{2,1,0:T(8,128)S(1)}, f32[17,8,128]{2,1,0:T(8,128)S(1)}, u32[]{:S(2)}, u32[]{:S(2)}) collective-permute-start(f32[17,8,128]{2,1,0:T(8,128)S(1)} %pad_maximum_fusion.1), channel_id=1, source_target_pairs={{1,0},{2,1},{3,2},{4,3},{5,4},{6,5},{7,6},{9,8},{10,9},{11,10},{12... | collective-permute-start | bytes 208904 | tf_op jit(solution)/shard_map/ppermute | solution.py:618
